TPU v7x, 32 devices: a whole 2x2x4 slice. The times are simulated.
32 devices in a mesh: seq: 4 (over y, x), dp: 8 (over z, core).
Axes of the slice: x: 2, y: 2, z: 4, core: 2. Of those that a mesh axis runs over, the one named last changes fastest.
Arguments:
- hidden_in: bfloat16 [24, 512, 768], P('dp', 'seq'), may hold values from -6 to 6
- lengths: int32 [24], P('dp'), may hold values from 20 to 512, as said below
- qkv_weight: bfloat16 [768, 2304], replicated, may hold values from -0.21875 to 0.21875
- query_bias: float32 [768], replicated, may hold values from -3 to 3
- value_bias: float32 [768], replicated, may hold values from -0.6 to 0.6
- out_weight: bfloat16 [768, 768], replicated, may hold values from -1.75 to 1.75
- out_bias: float32 [768], replicated, may hold values from -1.2 to 1.2
- attn_gain: float32 [768], replicated, may hold values from 0.5 to 1.5
- attn_shift: float32 [768], replicated, may hold values from -1.2 to 1.2
- up_weight: bfloat16 [768, 3072], replicated, may hold values from -0.21875 to 0.21875
- up_bias: float32 [3072], replicated, may hold values from -3 to 3
- down_weight: bfloat16 [3072, 768], replicated, may hold values from -0.109375 to 0.109375
- down_bias: float32 [768], replicated, may hold values from -1.2 to 1.2
- ffn_gain: float32 [768], replicated, may hold values from 0.5 to 1.5
- ffn_shift: float32 [768], replicated, may hold values from -1.2 to 1.2
- cotangent: bfloat16 [24, 512, 768], P('dp', 'seq'), may hold values from -6 to 6
Outputs:
- layer_out: bfloat16 [24, 512, 768], P('dp', 'seq')
- input_grad: bfloat16 [24, 512, 768], P('dp', 'seq')
- qkv_weight_grad: float32 [768, 2304], replicated
- query_bias_grad: float32 [768], replicated
- value_bias_grad: float32 [768], replicated
- out_weight_grad: float32 [768, 768], replicated
- out_bias_grad: float32 [768], replicated
- attn_gain_grad: float32 [768], replicated
- attn_shift_grad: float32 [768], replicated
- up_weight_grad: float32 [768, 3072], replicated
- up_bias_grad: float32 [3072], replicated
- down_weight_grad: float32 [3072, 768], replicated
- down_bias_grad: float32 [768], replicated
- ffn_gain_grad: float32 [768], replicated
- ffn_shift_grad: float32 [768], replicated
Inputs may be any that keep to these rules, and one draw needn't show every extreme that they name: `lengths`: keys at positions at or past a passage's length are padding; in every draw some passage has length 512 and some 20.
All inputs are finite; a program needn't handle non-finite values.
Results may differ from a plain program's by a relative error of at most 0.015.
Values may be sent and summed in bfloat16 or wider, within the bound.
No kernel may reach another device: no remote copies, remote signals or barrier semaphores. Data moves between devices by JAX's collectives and lax.ppermute only.
A program may use at most 192 MiB of HBM per device.

v0:
```python
import jax
import jax.numpy as jnp
from jax import lax
from jax.sharding import PartitionSpec as P

HEADS = 12


def layer_norm(values, gain, shift):
    center = values - jnp.mean(values, -1, keepdims=True)
    spread = jnp.mean(center * center, -1, keepdims=True)
    return center * lax.rsqrt(spread + 1e-12) * gain + shift


def exact_gelu(values):
    return jax.nn.gelu(values, approximate=False)


def masked_scores(query, keys, length):
    scale = query.shape[-1] ** (-0.5)
    scores = jnp.einsum("qhd,khd->hqk", query, keys, preferred_element_type=jnp.float32) * scale
    valid = jnp.arange(keys.shape[0]) < length
    return jnp.where(valid[None, None, :], scores, -1e30)


def attend(query, keys, values, length):
    scores = masked_scores(query, keys, length)
    peak = jnp.max(scores, -1, keepdims=True)
    expo = jnp.exp(scores - peak)
    total = jnp.sum(expo, -1, keepdims=True)
    probs = (expo / total).astype(jnp.bfloat16)
    context = jnp.einsum("hqk,khd->qhd", probs, values, preferred_element_type=jnp.float32)
    return (context.astype(jnp.bfloat16), (peak + jnp.log(total))[..., 0])


def attend_back(query, keys, values, length, logsum, dcontext):
    scale = query.shape[-1] ** (-0.5)
    probs = jnp.exp(masked_scores(query, keys, length) - logsum[..., None])
    dvalues = jnp.einsum(
        "hqk,qhd->khd", probs.astype(jnp.bfloat16), dcontext, preferred_element_type=jnp.float32
    )
    dprobs = jnp.einsum("qhd,khd->hqk", dcontext, values, preferred_element_type=jnp.float32)
    dscores = (probs * (dprobs - jnp.sum(dprobs * probs, -1, keepdims=True))).astype(jnp.bfloat16)
    dquery = jnp.einsum("hqk,khd->qhd", dscores, keys, preferred_element_type=jnp.float32) * scale
    dkeys = jnp.einsum("hqk,qhd->khd", dscores, query, preferred_element_type=jnp.float32) * scale
    return (dquery, dkeys, dvalues)


def body(
    hidden_in,
    lengths,
    qkv_weight,
    query_bias,
    value_bias,
    out_weight,
    out_bias,
    attn_gain,
    attn_shift,
    up_weight,
    up_bias,
    down_weight,
    down_bias,
    ffn_gain,
    ffn_shift,
    cotangent,
):
    count, local_len, width = hidden_in.shape
    rows = count * local_len
    head_size = width // HEADS
    tokens = hidden_in.reshape(rows, width)
    joined = jnp.concatenate([query_bias, jnp.zeros_like(query_bias), value_bias])
    qkv = (jnp.dot(tokens, qkv_weight, preferred_element_type=jnp.float32) + joined).astype(
        jnp.bfloat16
    )
    qkv_split = qkv.reshape(count, local_len, 3, HEADS, head_size)
    grouped = lax.all_to_all(qkv_split, "seq", split_axis=3, concat_axis=1, tiled=True)

    def forward_heads(item):
        block, length = item
        return attend(block[:, 0], block[:, 1], block[:, 2], length)

    context_heads, logsum = lax.map(forward_heads, (grouped, lengths))
    context = lax.all_to_all(context_heads, "seq", split_axis=1, concat_axis=2, tiled=True)
    context_rows = context.reshape(rows, width)
    attn = jnp.dot(context_rows, out_weight, preferred_element_type=jnp.float32) + out_bias
    first, first_back = jax.vjp(
        layer_norm, tokens.astype(jnp.float32) + attn, attn_gain, attn_shift
    )
    first_low = first.astype(jnp.bfloat16)
    upper = jnp.dot(first_low, up_weight, preferred_element_type=jnp.float32) + up_bias
    active, gelu_back = jax.vjp(exact_gelu, upper)
    active_low = active.astype(jnp.bfloat16)
    ffn = jnp.dot(active_low, down_weight, preferred_element_type=jnp.float32) + down_bias
    result, second_back = jax.vjp(layer_norm, first + ffn, ffn_gain, ffn_shift)
    layer_out = result.astype(jnp.bfloat16).reshape(count, local_len, width)
    dsecond, ffn_gain_grad, ffn_shift_grad = second_back(
        cotangent.reshape(rows, width).astype(jnp.float32)
    )
    dffn = dsecond.astype(jnp.bfloat16)
    down_weight_grad = jnp.dot(active_low.T, dffn, preferred_element_type=jnp.float32)
    down_bias_grad = jnp.sum(dffn, 0, dtype=jnp.float32)
    dactive = jnp.dot(dffn, down_weight.T, preferred_element_type=jnp.float32)
    dupper = gelu_back(dactive)[0].astype(jnp.bfloat16)
    up_weight_grad = jnp.dot(first_low.T, dupper, preferred_element_type=jnp.float32)
    up_bias_grad = jnp.sum(dupper, 0, dtype=jnp.float32)
    dfirst = dsecond + jnp.dot(dupper, up_weight.T, preferred_element_type=jnp.float32)
    dresid, attn_gain_grad, attn_shift_grad = first_back(dfirst)
    dattn = dresid.astype(jnp.bfloat16)
    out_weight_grad = jnp.dot(context_rows.T, dattn, preferred_element_type=jnp.float32)
    out_bias_grad = jnp.sum(dattn, 0, dtype=jnp.float32)
    dcontext = jnp.dot(dattn, out_weight.T, preferred_element_type=jnp.float32).astype(jnp.bfloat16)
    dcontext = dcontext.reshape(count, local_len, HEADS, head_size)
    dcontext_heads = lax.all_to_all(dcontext, "seq", split_axis=2, concat_axis=1, tiled=True)

    def backward_heads(item):
        block, length, logs, dblock = item
        return attend_back(block[:, 0], block[:, 1], block[:, 2], length, logs, dblock)

    dquery, dkeys, dvalues = lax.map(backward_heads, (grouped, lengths, logsum, dcontext_heads))
    dgrouped = jnp.stack([dquery, dkeys, dvalues], 2).astype(jnp.bfloat16)
    dqkv_split = lax.all_to_all(dgrouped, "seq", split_axis=1, concat_axis=3, tiled=True)
    dqkv = dqkv_split.reshape(rows, 3 * width)
    qkv_weight_grad = jnp.dot(tokens.T, dqkv, preferred_element_type=jnp.float32)
    query_bias_grad = jnp.sum(dqkv[:, :width], 0, dtype=jnp.float32)
    value_bias_grad = jnp.sum(dqkv[:, 2 * width :], 0, dtype=jnp.float32)
    input_grad = dresid + jnp.dot(dqkv, qkv_weight.T, preferred_element_type=jnp.float32)
    input_grad = input_grad.astype(jnp.bfloat16).reshape(count, local_len, width)
    pieces = [
        qkv_weight_grad,
        query_bias_grad,
        value_bias_grad,
        out_weight_grad,
        out_bias_grad,
        attn_gain_grad,
        attn_shift_grad,
        up_weight_grad,
        up_bias_grad,
        down_weight_grad,
        down_bias_grad,
        ffn_gain_grad,
        ffn_shift_grad,
    ]
    shapes = [piece.shape for piece in pieces]
    sizes_list = [piece.size for piece in pieces]
    flat = jnp.concatenate([piece.reshape(-1) for piece in pieces])
    members = lax.axis_size(("seq", "dp"))
    total = flat.shape[0]
    padded = -(-total // members) * members
    flat = jnp.concatenate([flat, jnp.zeros((padded - total,), jnp.float32)])
    shares = lax.psum_scatter(flat, ("seq", "dp"), scatter_dimension=0, tiled=True)
    summed = lax.all_gather(shares, ("seq", "dp"), axis=0, tiled=True)
    outputs = []
    offset = 0
    for shape_now, size_now in zip(shapes, sizes_list):
        outputs.append(summed[offset : offset + size_now].reshape(shape_now))
        offset = offset + size_now
    return (
        layer_out,
        input_grad,
        outputs[0],
        outputs[1],
        outputs[2],
        outputs[3],
        outputs[4],
        outputs[5],
        outputs[6],
        outputs[7],
        outputs[8],
        outputs[9],
        outputs[10],
        outputs[11],
        outputs[12],
    )


def solution(mesh):
    return jax.shard_map(
        body,
        mesh=mesh,
        in_specs=(
            P("dp", "seq", None),
            P("dp"),
            P(),
            P(),
            P(),
            P(),
            P(),
            P(),
            P(),
            P(),
            P(),
            P(),
            P(),
            P(),
            P(),
            P("dp", "seq", None),
        ),
        out_specs=(
            P("dp", "seq", None),
            P("dp", "seq", None),
            P(),
            P(),
            P(),
            P(),
            P(),
            P(),
            P(),
            P(),
            P(),
            P(),
            P(),
            P(),
            P(),
        ),
        check_vma=False,
    )
```

profile of v0, /device:TPU:0, one launch (start us, length us, event | category | flops | bytes accessed | tf_op | source)
XLA Modules:
  0.0 1436.6 jit_solution(16022272245876856078)
XLA Ops:
  9.2 3.8 fusion.34
  13.0 6.4 reshape.215
  19.4 6.2 copy.85
  25.7 5.2 all-to-all-start
  30.9 22.1 %all-to-all-done = bf16[3,128,3,12,64]{1,4,2,0,3:T(8,128)(2,1)} async-done(((bf16[3,128,3,12,64]{1,4,2,0,3:T(8,128)(2,1)}), bf16[3,128,3,12,64]{1,4,2,0,3:T(8,128)(2,1)}, u32[]{:S(2)}, u32[]{:S(2)}) %all-to-all-start) | async-done | bytes 1769504 | tf_op jit(solution)/shard_map/all_to_all | solution.py:76
  53.0 4.3 copy.87
  57.3 4.0 all_to_all.51
  61.4 18.3 %while.26 = (s32[]{:T(128)}, bf16[3,512,3,64]{1,3,2,0:T(8,128)(2,1)}, f32[3,3,512]{2,1,0:T(4,128)}, bf16[3,512,3,3,64]{1,4,3,2,0:T(8,128)(2,1)}, s32[3]{0:T(128)S(1)}, /*index=5*/s32[]{:T(128)}) while((s32[]{:T(128)}, bf16[3,512,3,64]{1,3,2,0:T(8,128)(2,1)}, f32[3,3,512]{2,1,0:T(4,128)}, bf16[3,512,3,3,64]{1,4,3,2,0:T(8,128)(2,1)}, ...), condition=%wide.region_3.4_spmd, body=%wide.region_0.3_spmd.sunk | while | flops 210861056 | bytes 11460713 | solution.py:82
  65.2 1.6 fusion.94
  71.3 1.6 fusion.94
  77.4 1.6 fusion.94
  79.6 3.4 copy.88
  83.0 3.9 reshape.217
  86.9 13.7 all_to_all.66
  100.6 3.9 reshape.218
  104.4 4.0 copy.89
  108.5 2.6 fusion.57
  111.4 14.9 %multiply_convert_fusion.1 = (bf16[384,3072]{1,0:T(8,128)(2,1)S(1)}, f32[384,3072]{1,0:T(8,128)S(1)}, f32[384,3072]{1,0:T(8,128)}) fusion(f32[3072]{0:T(1024)S(1)} %copy-done.32, bf16[768,3072]{1,0:T(8,128)(2,1)} %param.29, f32[384,768]{1,0:T(8,128)S(1)} %get-tuple-element.153, f32[768]{0:T(1024)S(1)} %copy-done.20, f32[768]{0:T(1024)S(1)} %copy-done.19, ...), kind=kOutput, calls=%fused_computation.49 | convolution fusion | flops 1891270656 | bytes 17716224 | tf_op jit(solution)/shard_map/dot_general | solution.py:90
  126.4 2.1 fusion.58
  130.0 1.4 fusion.53
  132.1 6.2 convert_reduce_fusion
  138.4 2.9 multiply_reduce_fusion.1
  144.4 1.5 convolution_convert_fusion
  145.9 2.8 reshape.216
  148.7 2.6 copy.91
  151.3 4.2 all-to-all-start.2
  155.5 7.2 all-to-all-done.2
  162.7 2.3 copy.93
  165.0 2.2 all_to_all.58
  167.3 28.4 %while.27 = (s32[]{:T(128)}, bf16[3,512,3,64]{1,3,2,0:T(8,128)(2,1)}, bf16[3,512,3,64]{1,3,2,0:T(8,128)(2,1)}, bf16[3,512,3,64]{1,3,2,0:T(8,128)(2,1)}, bf16[3,5...) while((s32[]{:T(128)}, ...), condition=%wide.region_14.15_spmd, body=%wide.region_12.14_spmd.sunk | while | flops 510589952 | bytes 43878732 | solution.py:119
  195.7 2.8 pad_maximum_fusion
  198.5 7.6 copy.94
  206.2 5.9 reshape.219
  212.1 4.4 all-to-all-start.3
  216.7 1.8 convert_reduce_fusion.1
  218.5 3.5 fusion.43
  222.0 3.2 reshape.208
  225.2 4.9 convolution_bitcast_fusion.1
  230.1 6.0 copy.109
  236.0 5.2 fusion.59
  241.2 10.8 reshape.210
  252.0 5.8 reshape.220
  257.8 9.8 copy.95
  267.5 2.0 copy.121
  270.8 5.0 convolution_bitcast_fusion
  275.8 8.0 copy.96
  283.7 7.9 reshape.207
  291.6 5.1 constant_dynamic-update-slice_fusion.9
  299.3 21.2 %dynamic-update-slice.4 = f32[7087104]{0:T(1024)} dynamic-update-slice(f32[7087104]{0:T(1024)} %constant_dynamic-update-slice_fusion.7, f32[589824]{0:T(1024)} %reshape.208, s32[]{} %constant.137) | dynamic-update-slice | bytes 4718596
  324.5 80.6 %dynamic-update-slice.8 = f32[7087104]{0:T(1024)} dynamic-update-slice(f32[7087104]{0:T(1024)} %constant_dynamic-update-slice_fusion.4, f32[2359296]{0:T(1024)} %bitcast.200, s32[]{} %constant.141) | dynamic-update-slice | bytes 18874372
  406.4 80.4 %dynamic-update-slice.10 = f32[7087104]{0:T(1024)} dynamic-update-slice(f32[7087104]{0:T(1024)} %constant_dynamic-update-slice_fusion.3, f32[2359296]{0:T(1024)} %reshape.210, s32[]{} %constant.143) | dynamic-update-slice | bytes 18874372
  491.0 434.7 %all-reduce.7.cloned.1.call-done = f32[7087104]{0:T(1024)} async-done(((f32[7087104]{0:T(1024)}), f32[7087104]{0:T(1024)}) %all-reduce.7.cloned.1.call-update) | async-done | bytes 28348432
  925.7 9.5 broadcast.123
  935.2 3.1 dynamic-slice_dynamic-update-slice_fusion
  938.9 4.2 fusion.37
  943.1 427.3 %all-reduce.5.cloned.1.call-done = f32[7087104]{0:T(1024)} async-done(((f32[7087104]{0:T(1024)}), f32[7087104]{0:T(1024)}) %all-reduce.5.cloned.1.call-update) | async-done | bytes 28348432
  1370.5 3.2 slice.122
  1373.7 3.4 slice.100
  1377.0 14.2 fusion.56
  1391.3 11.3 slice.107
  1402.6 5.2 slice.119
  1407.7 8.2 slice.96
  1416.0 10.9 reshape.211
  1428.2 1.4 fusion.55
  (195 shorter events, 64.5 us)
Async XLA Ops:
  7.2 2.0 copy-start
  25.7 27.3 %all-to-all-start = ((bf16[3,128,3,12,64]{1,4,2,0,3:T(8,128)(2,1)}), bf16[3,128,3,12,64]{1,4,2,0,3:T(8,128)(2,1)}, u32[]{:S(2)}, u32[]{:S(2)}) async-start(bf16[3,128,3,12,64]{1,4,2,0,3:T(8,128)(2,1)} %copy.85), calls=%async_computation | async-start | bytes 3538944 | tf_op jit(solution)/shard_map/all_to_all | solution.py:76
  53.0 8.4 copy-start.35
  86.9 21.6 %copy-start.33 = (f32[768]{0:T(1024)S(1)}, f32[768]{0:T(1024)}, u32[]{:S(2)}) copy-start(f32[768]{0:T(1024)} %param.26) | copy-start | bytes 9220
  108.5 2.9 copy-start.19
  108.5 2.9 copy-start.20
  108.5 2.9 copy-start.32
  108.5 17.9 %slice-start = ((s8[4718592]{0:T(1024)(128)(4,1)}), s8[4194304]{0:T(1024)(128)(4,1)S(1)}, s32[]{:S(2)}) async-start(s8[4718592]{0:T(1024)(128)(4,1)} %bitcast.218), calls=%async_computation.6 | async-start | bytes 8388608
  111.1 30.2 %copy-start.3 = (f32[384,768]{1,0:T(8,128)}, f32[384,768]{1,0:T(8,128)S(1)}, u32[]{:S(2)}) copy-start(f32[384,768]{1,0:T(8,128)S(1)} %get-tuple-element.153) | copy-start | bytes 3538948
  111.4 15.0 %slice-start.1 = ((s8[4718592]{0:T(1024)(128)(4,1)}), s8[524288]{0:T(1024)(128)(4,1)S(1)}, s32[]{:S(2)}) async-start(s8[4718592]{0:T(1024)(128)(4,1)} %bitcast.218), calls=%async_computation.7 | async-start | bytes 1048576
  111.4 14.9 %copy-start.34 = (f32[768]{0:T(1024)S(1)}, f32[768]{0:T(1024)}, u32[]{:S(2)}) copy-start(f32[768]{0:T(1024)} %param.32) | copy-start | bytes 9220
  126.3 2.2 copy-start.6
  126.4 2.5 copy-start.4
  126.4 2.5 copy-start.21
  126.4 3.6 copy-start.29
  130.0 8.4 slice-start.2
  132.1 6.2 copy-start.8
  132.1 6.3 slice-start.3
  138.4 2.9 copy-start.11
  141.3 3.1 copy-start.31
  141.8 1.0 copy-start.5
  141.8 1.8 copy-start.27
  143.6 0.8 copy-start.10
  151.3 11.4 all-to-all-start.2
  167.3 4.7 copy-start.2
  167.3 4.7 copy-start.13
  172.6 0.8 copy-start.14
  173.5 1.1 copy-start.15
  173.5 1.7 copy-start.17
  175.1 0.8 copy-start.16
  175.9 0.8 copy-start.18
  176.8 4.7 copy-start.2
  176.8 4.7 copy-start.13
  182.1 0.8 copy-start.14
  182.9 1.1 copy-start.15
  182.9 1.7 copy-start.17
  184.6 0.8 copy-start.16
  185.4 0.8 copy-start.18
  186.2 4.7 copy-start.2
  186.2 4.7 copy-start.13
  191.6 0.8 copy-start.14
  192.4 1.1 copy-start.15
  192.4 1.7 copy-start.17
  194.1 0.8 copy-start.16
  194.9 0.8 copy-start.18
  212.1 39.9 %all-to-all-start.3 = ((bf16[4,2,110592]{2,1,0:T(2,128)(2,1)}), bf16[4,2,110592]{2,1,0:T(2,128)(2,1)}, u32[]{:S(2)}, u32[]{:S(2)}) async-start(bf16[4,2,110592]{2,1,0:T(2,128)(2,1)} %reshape.219), calls=%async_computation.3 | async-start | bytes 3538944 | tf_op jit(solution)/shard_map/all_to_all | solution.py:121
  216.5 709.2 %all-reduce.7.cloned.1.call-start = ((), (), s32[]{:S(2)}) async-start(), calls=%async_computation.5 | async-start | bytes 56696832
  230.1 6.0 copy-start.7
  230.1 6.0 copy-start.9
  267.5 3.2 copy-start.12
  269.6 1.2 copy-start.1
  296.7 23.9 %copy-start.24 = (f32[768]{0:T(1024)S(1)}, f32[768]{0:T(1024)}, u32[]{:S(2)}) copy-start(f32[768]{0:T(1024)} %get-tuple-element.129) | copy-start | bytes 9220
  296.7 26.5 %copy-start.30 = (f32[768]{0:T(1024)S(1)}, f32[768]{0:T(1024)}, u32[]{:S(2)}) copy-start(f32[768]{0:T(1024)} %get-tuple-element.98) | copy-start | bytes 9220
  324.5 80.6 %copy-start.26 = (f32[3072]{0:T(1024)S(1)}, f32[3072]{0:T(1024)}, u32[]{:S(2)}) copy-start(f32[3072]{0:T(1024)} %get-tuple-element.127) | copy-start | bytes 36868
  406.4 80.4 %copy-start.23 = (f32[768]{0:T(1024)S(1)}, f32[768]{0:T(1024)}, u32[]{:S(2)}) copy-start(f32[768]{0:T(1024)} %get-tuple-element.125) | copy-start | bytes 9220
  406.4 81.7 %copy-start.22 = (f32[768]{0:T(1024)S(1)}, f32[768]{0:T(1024)}, u32[]{:S(2)}) copy-start(f32[768]{0:T(1024)} %get-tuple-element.94) | copy-start | bytes 9220
  406.4 83.0 %copy-start.25 = (f32[768]{0:T(1024)S(1)}, f32[768]{0:T(1024)}, u32[]{:S(2)}) copy-start(f32[768]{0:T(1024)} %convert_reduce_fusion.1) | copy-start | bytes 9220
  490.8 879.7 %all-reduce.5.cloned.1.call-start = ((), (), s32[]{:S(2)}) async-start(), calls=%async_computation.4 | async-start | bytes 56696832
  938.3 0.7 copy-start.28
Sparse Core Ops, SparseCore 0:
  490.9 434.7 all-reduce.6
  938.4 432.0 all-reduce.4
where the time goes:
time: 1460 us; the launch traced here: 1440 us
  waiting for transfers between devices  891 us (61%)
  local copies, waits for them, and re-layouts  408 us (28%)
  matrix products  73.4 us (5%)
  other arithmetic  21.1 us (1%)
  between operations  14.6 us (1%)
    unnamed x4, waiting for transfers between devices  862 us
    unnamed x86, local copies, waits for them, and re-layouts  242 us
    slice x8, local copies, waits for them, and re-layouts, body(): outputs.append(summed[offset:offset + size_now].reshape(shape_now))  48.2 us
  transfers between devices with their start and end apart: 5, of which 4 were waited for; matrix products, arithmetic and copies ran while one was open for 3% of the time, Pallas kernels for 0%

commit v1 on v0

v1 whole, which is shorter than its diff:
```python
import functools
import math

import jax
import jax.numpy as jnp
from jax import lax
from jax.experimental import pallas as pl
from jax.experimental.pallas import tpu as pltpu
from jax.sharding import PartitionSpec as P

HEADS = 12
EPS = 1e-12
BF = jnp.bfloat16
F32 = jnp.float32
VMEM_LIMIT = 60 * 1024 * 1024
LOG2E = math.log2(math.e)
S_SEQ, S_LEN, S_CORE, S_X, S_Y = range(5)


def dot_nn(left, right):
    return lax.dot_general(left, right, (((1,), (0,)), ((), ())), preferred_element_type=F32)


def dot_nt(left, right):
    return lax.dot_general(left, right, (((1,), (1,)), ((), ())), preferred_element_type=F32)


def dot_tn(left, right):
    return lax.dot_general(left, right, (((0,), (0,)), ((), ())), preferred_element_type=F32)


def params(flag=None):
    return pltpu.CompilerParams(vmem_limit_bytes=VMEM_LIMIT)


def cost(flops, nbytes, trans=0):
    return pl.CostEstimate(flops=int(flops), bytes_accessed=int(nbytes), transcendentals=int(trans))


def full(shape):
    zeros = (0,) * len(shape)
    return pl.BlockSpec(shape, lambda *_: zeros)


def shape_of(shape, dtype):
    return jax.ShapeDtypeStruct(shape, dtype)


def attn_fwd_body(sc, h0, h1, h2, h3, wq, wk, wv, qb, vb, wo, ob, gain, shift,
                  hid, q_o, k_o, v_o, ctx_o, lse_o, n1_o, r1_o, low_o, acc, lse_s):
    step = pl.program_id(0)
    steps = pl.num_programs(0)
    local = h0.shape[0]
    rows = hid.shape[0]
    head = wq.shape[1] // 2

    @pl.when(step == 0)
    def _():
        for at, ref in enumerate((h0, h1, h2, h3)):
            hid[at * local:(at + 1) * local, :] = ref[...]
        acc[...] = jnp.zeros_like(acc)
        lse_s[...] = jnp.zeros_like(lse_s)

    x = hid[...]
    w = jnp.concatenate([wq[...], wk[...], wv[...]], axis=1)
    both = dot_nn(x, w)
    wide = 2 * head
    q_o[...] = (both[:, :wide] + qb[...]).astype(BF)
    k_o[...] = both[:, wide:2 * wide].astype(BF)
    v_o[...] = (both[:, 2 * wide:] + vb[...]).astype(BF)
    k = k_o[...]
    v = v_o[...]
    key = lax.broadcasted_iota(jnp.int32, (1, rows), 1)
    place = ((key // local) ^ sc[S_SEQ]) * local + key % local
    mask = jnp.where(place < sc[S_LEN], 0.0, -1e30).astype(F32)
    scale = head ** (-0.5) * LOG2E
    chunk = 256
    lane = lax.broadcasted_iota(jnp.int32, (chunk, wide), 1)
    lane_l = lax.broadcasted_iota(jnp.int32, (chunk, lse_s.shape[1]), 1)
    for part in range(rows // chunk):
        span = pl.ds(part * chunk, chunk)
        q = q_o[span, :]
        outs = []
        tops = []
        for h in range(2):
            mine = (lane >= h * head) & (lane < (h + 1) * head)
            qh = jnp.where(mine, q, jnp.zeros_like(q))
            s = dot_nt(qh, k) * scale + mask
            top = jnp.max(s, -1, keepdims=True)
            e = jnp.exp2(s - top)
            total = jnp.sum(e, -1, keepdims=True)
            pv = dot_nn(e.astype(BF), v)
            outs.append(pv / total)
            tops.append(top + jnp.log2(total))
        ctx_o[span, :] = jnp.where(lane < head, outs[0], outs[1]).astype(BF)
        old = lse_s[span, :]
        old = jnp.where(lane_l == 2 * step, tops[0], old)
        lse_s[span, :] = jnp.where(lane_l == 2 * step + 1, tops[1], old)
    acc[...] += dot_nn(ctx_o[...], wo[...])

    @pl.when(step == steps - 1)
    def _():
        lse_o[...] = jnp.transpose(lse_s[...])[:lse_o.shape[0], :]
        for part in range(rows // local):
            span = pl.ds(part * local, local)
            val = hid[span, :].astype(F32) + (acc[span, :] + ob[...])
            cen = val - jnp.mean(val, -1, keepdims=True)
            r = lax.rsqrt(jnp.mean(cen * cen, -1, keepdims=True) + EPS)
            n = cen * r
            n1_o[span, :] = n
            r1_o[span, :] = jnp.broadcast_to(r, (local, r1_o.shape[1]))
            low_o[span, :] = (n * gain[...] + shift[...]).astype(BF)


def attn_fwd(sc, blocks, qkv_w, qb, vb, out_w, ob, gain, shift):
    local, width = blocks[0].shape
    rows = local * len(blocks)
    pairs = HEADS // 2
    wide = width // pairs
    row = lambda i, s: (0, i)
    grid = pltpu.PrefetchScalarGridSpec(
        num_scalar_prefetch=1,
        grid=(pairs,),
        in_specs=[full((local, width))] * 4 + [
            pl.BlockSpec((width, wide), lambda i, s: (0, i)),
            pl.BlockSpec((width, wide), lambda i, s: (0, pairs + i)),
            pl.BlockSpec((width, wide), lambda i, s: (0, 2 * pairs + i)),
            pl.BlockSpec((1, wide), row),
            pl.BlockSpec((1, wide), row),
            pl.BlockSpec((wide, width), lambda i, s: (i, 0)),
            full((1, width)), full((1, width)), full((1, width)),
        ],
        out_specs=[
            full((rows, width)),
            pl.BlockSpec((rows, wide), row),
            pl.BlockSpec((rows, wide), row),
            pl.BlockSpec((rows, wide), row),
            pl.BlockSpec((rows, wide), row),
            full((16, rows)),
            full((rows, width)),
            full((rows, 128)),
            full((rows, width)),
        ],
        scratch_shapes=[pltpu.VMEM((rows, width), F32), pltpu.VMEM((rows, 128), F32)],
    )
    wide_bf = shape_of((rows, width), BF)
    return pl.pallas_call(
        attn_fwd_body,
        grid_spec=grid,
        out_shape=[wide_bf, wide_bf, wide_bf, wide_bf, wide_bf, shape_of((16, rows), F32),
                   shape_of((rows, width), F32), shape_of((rows, 128), F32), wide_bf],
        compiler_params=params(),
        cost_estimate=cost(2 * rows * width * width * 4 + 4 * rows * rows * width, 12 * rows * width + 8 * width * width,
                           HEADS * rows * rows),
        name="attn_fwd",
    )(sc, *blocks, qkv_w, qkv_w, qkv_w, qb, vb, out_w, ob, gain, shift)


def ffn_fwd_body(low, n1, gain1, shift1, wu, ub, wd, db, gain2, shift2, c0, c1, c2, c3,
                 act_o, slope_o, l0, l1, l2, l3, dsec_o, dffn_o, stat_o, acc):
    step = pl.program_id(0)
    steps = pl.num_programs(0)
    local = c0.shape[0]
    up = dot_nn(low[...], wu[...]) + ub[...]
    cdf = 0.5 * (1.0 + lax.erf(up * (2.0 ** -0.5)))
    bell = jnp.exp2(up * up * (-0.5 * LOG2E)) * ((2.0 * math.pi) ** -0.5)
    act = (up * cdf).astype(BF)
    act_o[...] = act
    slope_o[...] = (cdf + up * bell).astype(BF)
    term = dot_nn(act, wd[...])

    @pl.when(step == 0)
    def _():
        acc[...] = term

    @pl.when(step > 0)
    def _():
        acc[...] += term

    @pl.when(step == steps - 1)
    def _():
        gains = jnp.zeros((1, n1.shape[1]), F32)
        shifts = jnp.zeros((1, n1.shape[1]), F32)
        downs = jnp.zeros((1, n1.shape[1]), F32)
        for at, (cot, lo) in enumerate(((c0, l0), (c1, l1), (c2, l2), (c3, l3))):
            span = pl.ds(at * local, local)
            first = n1[span, :] * gain1[...] + shift1[...]
            val = first + (acc[span, :] + db[...])
            cen = val - jnp.mean(val, -1, keepdims=True)
            r = lax.rsqrt(jnp.mean(cen * cen, -1, keepdims=True) + EPS)
            n = cen * r
            lo[...] = (n * gain2[...] + shift2[...]).astype(BF)
            dy = cot[...].astype(F32)
            dn = dy * gain2[...]
            ds = r * (dn - jnp.mean(dn, -1, keepdims=True) - n * jnp.mean(dn * n, -1, keepdims=True))
            dsec_o[span, :] = ds
            dlow = ds.astype(BF)
            dffn_o[span, :] = dlow
            gains += jnp.sum(dy * n, 0, keepdims=True)
            shifts += jnp.sum(dy, 0, keepdims=True)
            downs += jnp.sum(dlow.astype(F32), 0, keepdims=True)
        stat_o[0:1, :] = gains
        stat_o[1:2, :] = shifts
        stat_o[2:3, :] = downs
        stat_o[3:8, :] = jnp.zeros((5, stat_o.shape[1]), F32)


def ffn_fwd(low, n1, gain1, shift1, wu, ub, wd, db, gain2, shift2, cots):
    rows, width = low.shape
    inner = wu.shape[1]
    tile = 512
    steps = inner // tile
    local = cots[0].shape[0]
    one = full((1, width))
    wide = full((rows, width))
    quarter = full((local, width))
    col = pl.BlockSpec((rows, tile), lambda i: (0, i))
    grid = pl.GridSpec(
        grid=(steps,),
        in_specs=[wide, wide, one, one, pl.BlockSpec((width, tile), lambda i: (0, i)),
                  pl.BlockSpec((1, tile), lambda i: (0, i)),
                  pl.BlockSpec((tile, width), lambda i: (i, 0)), one, one, one] + [quarter] * 4,
        out_specs=[col, col] + [quarter] * 4 + [wide, wide, full((8, width))],
        scratch_shapes=[pltpu.VMEM((rows, width), F32)],
    )
    return pl.pallas_call(
        ffn_fwd_body,
        grid_spec=grid,
        out_shape=[shape_of((rows, inner), BF)] * 2 + [shape_of((local, width), BF)] * 4
        + [shape_of((rows, width), F32), shape_of((rows, width), BF), shape_of((8, width), F32)],
        compiler_params=params(),
        cost_estimate=cost(4 * rows * width * inner, 4 * width * inner + 4 * rows * inner, 2 * rows * inner),
        name="ffn_fwd",
    )(low, n1, gain1, shift1, wu, ub, wd, db, gain2, shift2, *cots)


def ffn_bwd_body(dffn, wd, slope, wu, dsec, n1, r1, gain1, wo,
                 dup_o, ubg_o, dres_o, dattn_o, dctx_o, stat_o, acc):
    step = pl.program_id(0)
    steps = pl.num_programs(0)
    dact = dot_nt(dffn[...], wd[...])
    dup = (dact * slope[...].astype(F32)).astype(BF)
    dup_o[...] = dup
    ubg_o[...] = jnp.sum(dup.astype(F32), 0, keepdims=True)
    term = dot_nt(dup, wu[...])

    @pl.when(step == 0)
    def _():
        acc[...] = term

    @pl.when(step > 0)
    def _():
        acc[...] += term

    @pl.when(step == steps - 1)
    def _():
        rows, width = n1.shape
        local = 128
        gains = jnp.zeros((1, width), F32)
        shifts = jnp.zeros((1, width), F32)
        outs = jnp.zeros((1, width), F32)
        for at in range(rows // local):
            span = pl.ds(at * local, local)
            dfirst = dsec[span, :] + acc[span, :]
            n = n1[span, :]
            dn = dfirst * gain1[...]
            r = r1[span, 0:1]
            dres = r * (dn - jnp.mean(dn, -1, keepdims=True) - n * jnp.mean(dn * n, -1, keepdims=True))
            dres_o[span, :] = dres
            dlow = dres.astype(BF)
            dattn_o[span, :] = dlow
            gains += jnp.sum(dfirst * n, 0, keepdims=True)
            shifts += jnp.sum(dfirst, 0, keepdims=True)
            outs += jnp.sum(dlow.astype(F32), 0, keepdims=True)
        stat_o[0:1, :] = gains
        stat_o[1:2, :] = shifts
        stat_o[2:3, :] = outs
        stat_o[3:8, :] = jnp.zeros((5, width), F32)
        dctx_o[...] = dot_nt(dattn_o[...], wo[...]).astype(BF)


def ffn_bwd(dffn, wd, slope, wu, dsec, n1, r1, gain1, wo):
    rows, width = dffn.shape
    inner = wu.shape[1]
    tile = 512
    steps = inner // tile
    wide = full((rows, width))
    col = pl.BlockSpec((rows, tile), lambda i: (0, i))
    grid = pl.GridSpec(
        grid=(steps,),
        in_specs=[wide, pl.BlockSpec((tile, width), lambda i: (i, 0)), col,
                  pl.BlockSpec((width, tile), lambda i: (0, i)), wide, wide, full((rows, 128)),
                  full((1, width)), full((width, width))],
        out_specs=[col, pl.BlockSpec((1, tile), lambda i: (0, i)), wide, wide, wide, full((8, width))],
        scratch_shapes=[pltpu.VMEM((rows, width), F32)],
    )
    return pl.pallas_call(
        ffn_bwd_body,
        grid_spec=grid,
        out_shape=[shape_of((rows, inner), BF), shape_of((1, inner), F32), shape_of((rows, width), F32),
                   shape_of((rows, width), BF), shape_of((rows, width), BF), shape_of((8, width), F32)],
        compiler_params=params(),
        cost_estimate=cost(4 * rows * width * inner, 4 * width * inner + 4 * rows * inner),
        name="ffn_bwd",
    )(dffn, wd, slope, wu, dsec, n1, r1, gain1, wo)


def attn_bwd_body(sc, q_r, k_r, v_r, g_r, lse, wq, wk, wv, dres,
                  dq_o, dk_o, dv_o, qbg_o, vbg_o, i0, i1, i2, i3, acc):
    step = pl.program_id(0)
    steps = pl.num_programs(0)
    rows, wide = q_r.shape
    head = wide // 2
    local = i0.shape[0]
    scale = head ** (-0.5)
    q = q_r[...]
    g = g_r[...]
    k = k_r[...]
    v = v_r[...]
    lane = lax.broadcasted_iota(jnp.int32, (rows, wide), 1)
    chunk = 256
    nchunk = rows // chunk
    dks = [[None, None] for _ in range(nchunk)]
    dvs = [[None, None] for _ in range(nchunk)]
    dqs = []
    for h in range(2):
        mine = (lane >= h * head) & (lane < (h + 1) * head)
        qh = jnp.where(mine, q, jnp.zeros_like(q))
        gh = jnp.where(mine, g, jnp.zeros_like(g))
        row = lse[pl.ds(2 * step + h, 1), :]
        ps = []
        dps = []
        delta = jnp.zeros((1, rows), F32)
        for c in range(nchunk):
            kc = k[c * chunk:(c + 1) * chunk, :]
            vc = v[c * chunk:(c + 1) * chunk, :]
            key = lax.broadcasted_iota(jnp.int32, (chunk, 1), 0) + c * chunk
            place = ((key // local) ^ sc[S_SEQ]) * local + key % local
            mask = jnp.where(place < sc[S_LEN], 0.0, -1e30).astype(F32)
            s = dot_nt(kc, qh) * (scale * LOG2E) + mask
            p = jnp.exp2(s - row)
            dp = dot_nt(vc, gh)
            delta += jnp.sum(p * dp, 0, keepdims=True)
            dvs[c][h] = dot_nn(p.astype(BF), g)
            ps.append(p)
            dps.append(dp)
        dq = None
        for c in range(nchunk):
            ds = (ps[c] * (dps[c] - delta)).astype(BF)
            dks[c][h] = dot_nn(ds, q)
            term = dot_tn(ds, k[c * chunk:(c + 1) * chunk, :])
            dq = term if dq is None else dq + term
        dqs.append(dq)
    low = lane < head
    low_c = low[:chunk, :]
    dq_o[...] = (jnp.where(low, dqs[0], dqs[1]) * scale).astype(BF)
    for c in range(nchunk):
        span = pl.ds(c * chunk, chunk)
        dk_o[span, :] = (jnp.where(low_c, dks[c][0], dks[c][1]) * scale).astype(BF)
        dv_o[span, :] = jnp.where(low_c, dvs[c][0], dvs[c][1]).astype(BF)
    dqv = dq_o[...]
    dkv = dk_o[...]
    dvv = dv_o[...]
    qbg_o[...] = jnp.sum(dqv.astype(F32), 0, keepdims=True)
    vbg_o[...] = jnp.sum(dvv.astype(F32), 0, keepdims=True)
    three = jnp.concatenate([dqv, dkv, dvv], axis=1)
    w = jnp.concatenate([wq[...], wk[...], wv[...]], axis=1)
    term = dot_nt(three, w)

    @pl.when(step == 0)
    def _():
        acc[...] = dres[...] + term

    @pl.when(step > 0)
    def _():
        acc[...] += term

    @pl.when(step == steps - 1)
    def _():
        for at, ref in enumerate((i0, i1, i2, i3)):
            ref[...] = acc[pl.ds(at * local, local), :].astype(BF)


def attn_bwd(sc, q, k, v, g, lse, qkv_w, dres, local):
    rows, width = q.shape
    pairs = HEADS // 2
    wide = width // pairs
    col = pl.BlockSpec((rows, wide), lambda i, s: (0, i))
    one = pl.BlockSpec((1, wide), lambda i, s: (0, i))
    quarter = full((local, width))
    grid = pltpu.PrefetchScalarGridSpec(
        num_scalar_prefetch=1,
        grid=(pairs,),
        in_specs=[col, col, col, col, full(lse.shape),
                  pl.BlockSpec((width, wide), lambda i, s: (0, i)),
                  pl.BlockSpec((width, wide), lambda i, s: (0, pairs + i)),
                  pl.BlockSpec((width, wide), lambda i, s: (0, 2 * pairs + i)),
                  full((rows, width))],
        out_specs=[col, col, col, one, one] + [quarter] * 4,
        scratch_shapes=[pltpu.VMEM((rows, width), F32)],
    )
    wide_bf = shape_of((rows, width), BF)
    vec = shape_of((1, width), F32)
    return pl.pallas_call(
        attn_bwd_body,
        grid_spec=grid,
        out_shape=[wide_bf, wide_bf, wide_bf, vec, vec] + [shape_of((local, width), BF)] * 4,
        compiler_params=params(),
        cost_estimate=cost(6 * rows * width * width + 10 * rows * rows * width, 12 * rows * width + 6 * width * width,
                           HEADS * rows * rows),
        name="attn_bwd",
    )(sc, q, k, v, g, lse, qkv_w, qkv_w, qkv_w, dres)


def wgrad_body(sc, la, lp, ra, rp, sa, sb, ka, kb):
    step = pl.program_id(0)
    val = (dot_tn(la[...], ra[...]) + dot_tn(lp[...], rp[...])).astype(BF)
    for at, ref in enumerate((sa, sb, ka, kb)):
        @pl.when(step == at)
        def _():
            ref[...] = val


def half_of(j, sc):
    bit = jnp.where(j % 2 == 0, sc[S_X], sc[S_Y])
    return jnp.where(j < 2, 1 - bit, bit)


def wgrad(sc, la, lp, ra, rp, maps, name):
    rows = la.shape[0]
    unit = 768
    half = unit // 2
    m_la, m_lp, m_ra, m_rp = maps
    grid = pltpu.PrefetchScalarGridSpec(
        num_scalar_prefetch=1,
        grid=(4,),
        in_specs=[pl.BlockSpec((rows, half), m_la), pl.BlockSpec((rows, half), m_lp),
                  pl.BlockSpec((rows, unit), m_ra), pl.BlockSpec((rows, unit), m_rp)],
        out_specs=[full((half, unit))] * 4,
    )
    return pl.pallas_call(
        wgrad_body,
        grid_spec=grid,
        out_shape=[shape_of((half, unit), BF)] * 4,
        compiler_params=params(),
        cost_estimate=cost(2 * 4 * half * unit * rows * 2, 8 * half * unit + 8 * rows * unit),
        name=name,
    )(sc, la, lp, ra, rp)


def wgrad_mix_body(sc, hid, hidp, ctx, ctxp, dq, dk, dv, da, r1p, r2p, sa, sb, ka, kb):
    step = pl.program_id(0)
    core = sc[S_CORE]
    first = step % 2 == 0
    for at, ref in enumerate((sa, sb, ka, kb)):
        if at % 2 == 0:
            @pl.when((step == at) & (core == 0))
            def _():
                ref[...] = (dot_tn(hid[...], dq[...]) + dot_tn(hidp[...], r1p[...])).astype(BF)

            @pl.when((step == at) & (core == 1))
            def _():
                ref[...] = (dot_tn(hid[...], dv[...]) + dot_tn(hidp[...], r1p[...])).astype(BF)
        else:
            @pl.when((step == at) & (core == 0))
            def _():
                ref[...] = (dot_tn(hid[...], dk[...]) + dot_tn(hidp[...], r2p[...])).astype(BF)

            @pl.when((step == at) & (core == 1))
            def _():
                ref[...] = (dot_tn(ctx[...], da[...]) + dot_tn(ctxp[...], r2p[...])).astype(BF)


def wgrad_mix(sc, hid, hidp, ctx, ctxp, dq, dk, dv, da, r1p, r2p):
    rows, unit = hid.shape
    half = unit // 2
    cut = pl.BlockSpec((rows, half), lambda j, s: (0, half_of(j, s)))
    wide = full((rows, unit))
    grid = pltpu.PrefetchScalarGridSpec(
        num_scalar_prefetch=1,
        grid=(4,),
        in_specs=[cut] * 4 + [wide] * 6,
        out_specs=[full((half, unit))] * 4,
    )
    return pl.pallas_call(
        wgrad_mix_body,
        grid_spec=grid,
        out_shape=[shape_of((half, unit), BF)] * 4,
        compiler_params=params(),
        cost_estimate=cost(2 * 4 * half * unit * rows * 2, 8 * half * unit + 20 * rows * unit),
        name="wgrad_mix",
    )(sc, hid, hidp, ctx, ctxp, dq, dk, dv, da, r1p, r2p)


def swap(value, axis, mask, size):
    return lax.ppermute(value, axis, [(i, i ^ mask) for i in range(size)])


def add_low(one, two):
    return (one.astype(F32) + two.astype(F32)).astype(BF)


def cut_half(value, bit, dim, keep):
    size = value.shape[dim] // 2
    at = bit if keep else 1 - bit
    return lax.dynamic_slice_in_dim(value, at * size, size, dim)


def join(own, other, bit, dim):
    return jnp.where(
        bit == 0, jnp.concatenate([own, other], dim), jnp.concatenate([other, own], dim)
    )


class Ring:
    def __init__(self, nseq, ndp, seq, dp):
        self.nseq, self.ndp, self.seq, self.dp = nseq, ndp, seq, dp
        self.x = seq & 1
        self.y = (seq >> 1) & 1
        self.dp_masks = []
        mask = 2
        while mask < ndp:
            self.dp_masks.append(mask)
            mask *= 2

    def over_x(self, value):
        return swap(value, "seq", 1, self.nseq)

    def over_y(self, value):
        return swap(value, "seq", 2, self.nseq)

    def over_dp(self, value, mask):
        return swap(value, "dp", mask, self.ndp)

    def reduce(self, sa, sb, ka, kb):
        ra = self.over_x(sa)
        rb = self.over_y(sb)
        ta = add_low(cut_half(ka, self.y, 0, False), cut_half(ra, self.y, 0, False))
        tb = add_low(cut_half(kb, self.x, 0, False), cut_half(rb, self.x, 0, False))
        ua = add_low(cut_half(ka, self.y, 0, True), cut_half(ra, self.y, 0, True))
        ub = add_low(cut_half(kb, self.x, 0, True), cut_half(rb, self.x, 0, True))
        va = self.over_y(ta)
        vb = self.over_x(tb)
        cur = jnp.stack([add_low(ua, va), add_low(ub, vb)])
        self.halved = []
        for mask in self.dp_masks:
            bit = jnp.where((self.dp & mask) != 0, 1, 0)
            if cur.shape[1] % 32 == 0:
                got = self.over_dp(cut_half(cur, bit, 1, False), mask)
                cur = add_low(cut_half(cur, bit, 1, True), got)
                self.halved.append((mask, bit))
            else:
                cur = add_low(cur, self.over_dp(cur, mask))
        return cur

    def gather(self, cur):
        for mask, bit in reversed(self.halved):
            cur = join(cur, self.over_dp(cur, mask), bit, 1)
        a, b = cur[0], cur[1]
        a = join(a, self.over_y(a), self.y, 0)
        b = join(b, self.over_x(b), self.x, 0)
        a = join(a, self.over_x(a), self.x, 0)
        b = join(b, self.over_y(b), self.y, 0)
        return a, b


def body(
    hidden_in,
    lengths,
    qkv_weight,
    query_bias,
    value_bias,
    out_weight,
    out_bias,
    attn_gain,
    attn_shift,
    up_weight,
    up_bias,
    down_weight,
    down_bias,
    ffn_gain,
    ffn_shift,
    cotangent,
):
    count, local, width = hidden_in.shape
    inner = up_weight.shape[1]
    nseq = lax.axis_size("seq")
    ndp = lax.axis_size("dp")
    seq = lax.axis_index("seq")
    dp = lax.axis_index("dp")
    core = dp & 1
    ring = Ring(nseq, ndp, seq, dp)
    line = lambda vec: vec.reshape(1, -1)

    holder = jnp.minimum(seq, count - 1)
    own_len = lax.dynamic_index_in_dim(lengths, holder, 0, False)
    own_len = jnp.where(seq < count, own_len, nseq * local)
    sc = jnp.stack([seq, own_len, core, ring.x, ring.y, core, core, core]).astype(jnp.int32)

    def to_holder(value):
        blocks = [lax.dynamic_index_in_dim(value, holder, 0, False)]
        for k in range(1, nseq):
            at = jnp.minimum(seq ^ k, count - 1)
            part = lax.dynamic_index_in_dim(value, at, 0, False)
            pairs = [(i, i ^ k) for i in range(nseq) if (i ^ k) < count]
            blocks.append(lax.ppermute(part, "seq", pairs))
        return blocks

    def from_holder(blocks):
        got = [blocks[0]]
        for k in range(1, nseq):
            pairs = [(i, i ^ k) for i in range(nseq) if i < count]
            got.append(lax.ppermute(blocks[k], "seq", pairs))
        outs = []
        for p in range(count):
            value = got[0]
            for k in range(1, nseq):
                value = jnp.where((seq ^ p) == k, got[k], value)
            outs.append(value)
        return jnp.stack(outs)

    hids = to_holder(hidden_in)
    hids, cot_in = lax.optimization_barrier((hids, cotangent))
    cots = to_holder(cot_in)
    cots[0] = jnp.where(seq < count, cots[0], jnp.zeros_like(cots[0]))

    hid, q, k, v, ctx, lse, n1, r1, low = attn_fwd(
        sc, hids, qkv_weight, line(query_bias), line(value_bias), out_weight, line(out_bias),
        line(attn_gain), line(attn_shift))
    act, slope, l0, l1, l2, l3, dsec, dffn, stat2 = ffn_fwd(
        low, n1, line(attn_gain), line(attn_shift), up_weight, line(up_bias), down_weight,
        line(down_bias), line(ffn_gain), line(ffn_shift), cots)

    def core_swap(value):
        return swap(value, "dp", 1, ndp)

    def other_cols(value):
        size = value.shape[1] // 2
        return lax.dynamic_slice_in_dim(value, (1 - core) * size, size, 1)

    act_p = core_swap(other_cols(act))
    dffn_p = core_swap(dffn)
    layer_out = from_holder([l0, l1, l2, l3])
    dup, ubg, dres, dattn, dctx, stat1 = ffn_bwd(
        dffn, down_weight, slope, up_weight, dsec, n1, r1, line(attn_gain), out_weight)
    down_parts = wgrad(
        sc, act, act_p, dffn, dffn_p,
        (lambda j, s: (0, s[S_CORE] * 4 + (j % 2) * 2 + half_of(j, s)),
         lambda j, s: (0, (j % 2) * 2 + half_of(j, s)),
         lambda j, s: (0, 0), lambda j, s: (0, 0)), "wgrad_down")
    low_p = core_swap(low)
    dup_p = core_swap(other_cols(dup))
    hid_p = core_swap(hid)
    ctx_p = core_swap(ctx)
    up_parts = wgrad(
        sc, low, low_p, dup, dup_p,
        (lambda j, s: (0, half_of(j, s)), lambda j, s: (0, half_of(j, s)),
         lambda j, s: (0, s[S_CORE] * 2 + j % 2), lambda j, s: (0, j % 2)), "wgrad_up")
    dq, dk, dv, qbg, vbg, i0, i1, i2, i3 = attn_bwd(sc, q, k, v, dctx, lse, qkv_weight, dres, local)
    input_grad = from_holder([i0, i1, i2, i3])
    r1_p = core_swap(jnp.where(core == 0, dv, dq))
    r2_p = core_swap(jnp.where(core == 0, dattn, dk))
    mix_parts = wgrad_mix(sc, hid, hid_p, ctx, ctx_p, dq, dk, dv, dattn, r1_p, r2_p)

    small = jnp.concatenate(
        [stat2[0:3].reshape(-1), stat1[0:3].reshape(-1), qbg.reshape(-1), vbg.reshape(-1), ubg.reshape(-1)]
    ).reshape(-1, 128)
    mask = 1
    while mask < nseq:
        small = small + swap(small, "seq", mask, nseq)
        mask *= 2
    mask = 1
    while mask < ndp:
        small = small + swap(small, "dp", mask, ndp)
        mask *= 2
    small = small.reshape(-1)
    vec = [small[i * width:(i + 1) * width] for i in range(8)]
    up_bias_grad = small[8 * width:]

    def finish(parts):
        a, b = ring.gather(ring.reduce(*parts))
        pa = core_swap(a)
        pb = core_swap(b)
        return a, b, pa, pb

    def ordered(parts):
        a, b, pa, pb = parts
        lo = core == 0
        return (jnp.where(lo, a, pa), jnp.where(lo, b, pb), jnp.where(lo, pa, a), jnp.where(lo, pb, b))

    d_parts = ordered(finish(down_parts))
    u_parts = ordered(finish(up_parts))
    m_parts = ordered(finish(mix_parts))
    down_grad = jnp.concatenate(d_parts, 0).astype(F32)
    up_grad = jnp.concatenate(u_parts, 1).astype(F32)
    qkv_grad = jnp.concatenate(m_parts[:3], 1).astype(F32)
    out_grad = m_parts[3].astype(F32)
    return (
        layer_out,
        input_grad,
        qkv_grad,
        vec[6],
        vec[7],
        out_grad,
        vec[5],
        vec[3],
        vec[4],
        up_grad,
        up_bias_grad,
        down_grad,
        vec[2],
        vec[0],
        vec[1],
    )


def solution(mesh):
    split = P("dp", "seq", None)
    return jax.shard_map(
        body,
        mesh=mesh,
        in_specs=(split, P("dp")) + (P(),) * 13 + (split,),
        out_specs=(split, split) + (P(),) * 13,
        check_vma=False,
    )
```

time: 1460 us -> 336 us (0.23); the launches traced: 1440 us -> 335 us
  waiting for transfers between devices: 891 us -> 119 us
  local copies, waits for them, and re-layouts: 408 us -> 14.2 us
  Pallas kernels: 0 us -> 96.1 us
  matrix products: 73.4 us -> 0 us
  starting transfers between devices: 14.2 us -> 76 us
    unnamed x4 -> x0, waiting for transfers between devices: 862 us -> none
    unnamed x86 -> x80, local copies, waits for them, and re-layouts: 242 us -> 0.96 us
    ppermute x0 -> x67, waiting for transfers between devices: none -> 119 us  [the longest x55 101 us: swap(): return lax.ppermute(value, axis, [(i, i ^ mask) for i in range(size)])]
    pallas_call x0 -> x7, Pallas kernels: none -> 96.1 us  [the longest x1 20.9 us: attn_bwd(): pl.pallas_call(attn_bwd_body, grid_spec=grid, out_shape=[wide_bf, wide_bf...]
    ppermute x0 -> x67, starting transfers between devices: none -> 76 us  [the longest x55 43.5 us: swap(): return lax.ppermute(value, axis, [(i, i ^ mask) for i in range(size)])]
    dot_general x33 -> x0, matrix products: 73.4 us -> none  [the longest x1 14.9 us: body(): jnp.dot(first_low, up_weight, preferred_element_type=jnp.float32) + up_bias]
    slice x8 -> x4, local copies, waits for them, and re-layouts: 48.2 us -> 1.97 us  [the longest x1 0.74 us: body(): stat1[0:3].reshape(-1)]
    reshape x8 -> x10, local copies, waits for them, and re-layouts: 50.8 us -> 4.67 us  [the longest x8 4.64 us: body(): line = lambda vec: vec.reshape(1, -1)]
  transfers between devices with their start and end apart: 5 -> 67, of which waited for: 4 -> 28; matrix products, arithmetic and copies ran while one was open for 3% -> 10% of each run, Pallas kernels for 0% -> 29%
where the time goes in v1:
time: 336 us; the launch traced here: 335 us
  waiting for transfers between devices  119 us (35%)
  Pallas kernels  96.1 us (29%)
  starting transfers between devices  76 us (23%)
  other arithmetic  27.9 us (8%)
  local copies, waits for them, and re-layouts  14.2 us (4%)
    ppermute x55, waiting for transfers between devices, swap(): return lax.ppermute(value, axis, [(i, i ^ mask) for i in range(size)])  101 us
    ppermute x55, starting transfers between devices, swap(): return lax.ppermute(value, axis, [(i, i ^ mask) for i in range(size)])  43.5 us
    pallas_call x1, Pallas kernels, attn_bwd(): pl.pallas_call(attn_bwd_body, grid_spec=grid, out_shape=[wide_bf, wide_bf...  20.9 us
    pallas_call x1, Pallas kernels, attn_fwd(): pl.pallas_call(attn_fwd_body, grid_spec=grid, out_shape=[wide_bf, wide_bf...  19.3 us
    ppermute x6, starting transfers between devices, from_holder(): got.append(lax.ppermute(blocks[k], 'seq', pairs))  17.8 us
    pallas_call x2, Pallas kernels, wgrad(): pl.pallas_call(wgrad_body, grid_spec=grid, out_shape=[shape_of((half, uni...  16 us
    pallas_call x1, Pallas kernels, ffn_bwd(): pl.pallas_call(ffn_bwd_body, grid_spec=grid, out_shape=[shape_of((rows, i...  15.8 us
    pallas_call x1, Pallas kernels, ffn_fwd(): pl.pallas_call(ffn_fwd_body, grid_spec=grid, out_shape=[shape_of((rows, i...  15.2 us
  transfers between devices with their start and end apart: 67, of which 28 were waited for; matrix products, arithmetic and copies ran while one was open for 10% of the time, Pallas kernels for 29%

profile of v1, /device:TPU:0, one launch (start us, length us, event | category | flops | bytes accessed | tf_op | source)
XLA Modules:
  0.0 335.3 jit_solution(5051649306169674421)
XLA Ops:
  0.8 2.0 dynamic-slice_bitcast_fusion.3
  2.8 4.9 %collective-permute-start = (bf16[128,768]{1,0:T(8,128)(2,1)S(1)}, bf16[128,768]{1,0:T(8,128)(2,1)S(1)}, u32[]{:S(2)}, u32[]{:S(2)}) collective-permute-start(bf16[128,768]{1,0:T(8,128)(2,1)S(1)} %get-tuple-element.144), channel_id=1, source_target_pairs={{0,8},{8,0},{24,16},{1,9},{9,1},{25,17},{2,10},{10,2},{26,18},{3,1... | collective-permute-start | bytes 589832 | tf_op jit(solution)/shard_map/ppermute | solution.py:606
  7.7 1.9 collective-permute-start.1
  9.6 1.3 collective-permute-start.2
  17.5 2.6 collective-permute-done.1.h2
  21.0 3.4 %collective-permute-start.3 = (bf16[128,768]{1,0:T(8,128)(2,1)S(1)}, bf16[128,768]{1,0:T(8,128)(2,1)S(1)}, u32[]{:S(2)}, u32[]{:S(2)}) collective-permute-start(bf16[128,768]{1,0:T(8,128)(2,1)S(1)} %get-tuple-element.141), channel_id=1, source_target_pairs={{0,8},{8,0},{24,16},{1,9},{9,1},{25,17},{2,10},{10,2},{26,18},{3,1... | collective-permute-start | bytes 589832 | tf_op jit(solution)/shard_map/ppermute | solution.py:606
  24.4 1.9 collective-permute-start.4
  26.3 1.3 collective-permute-start.5
  27.7 19.3 %attn_fwd.1 = (bf16[512,768]{1,0:T(8,128)(2,1)}, bf16[512,768]{1,0:T(8,128)(2,1)}, bf16[512,768]{1,0:T(8,128)(2,1)}, bf16[512,768]{1,0:T(8,128)(2,1)}, bf16[512,...) custom-call(s32[8]{0:T(128)} %stack.77.sc, ...), custom_call_target="tpu_custom_call" | custom-call | flops 3221225472 | bytes 9437184 | tf_op jit(solution)/shard_map/attn_fwd/pallas_call | solution.py:147
  48.4 15.2 %ffn_fwd.1 = (bf16[512,3072]{1,0:T(8,128)(2,1)}, bf16[512,3072]{1,0:T(8,128)(2,1)}, bf16[128,768]{1,0:T(8,128)(2,1)}, bf16[128,768]{1,0:T(8,128)(2,1)}, bf16[128...) custom-call(bf16[512,768]{1,0:T(8,128)(2,1)} %get-tuple-element.69.l, ...), custom_call_target="tpu_custom_call" | custom-call | flops 4831838208 | bytes 15728640 | tf_op jit(solution)/shard_map/ffn_fwd/pallas_call | solution.py:226
  63.6 15.8 %ffn_bwd.1 = (bf16[512,3072]{1,0:T(8,128)(2,1)}, f32[1,3072]{1,0:T(1,128)}, f32[512,768]{1,0:T(8,128)}, bf16[512,768]{1,0:T(8,128)(2,1)}, bf16[512,768]{1,0:T(8,128)(2,1)}, /*index=5*/f32[8,768]{1,0:T(8,128)}) custom-call(bf16[512,768]{1,0:T(8,128)(2,1)} %get-tuple-element.79.dffn.ra, bf16[3072,768]{1,0:T(8,128)(2,1)} %wd.3, ...), custom_call_target="tpu_custom_call" | custom-call | flops 4831838208 | bytes 15728640 | tf_op jit(solution)/shard_map/ffn_bwd/pallas_call | solution.py:297
  80.2 20.9 %attn_bwd.1 = (bf16[512,768]{1,0:T(8,128)(2,1)}, bf16[512,768]{1,0:T(8,128)(2,1)}, bf16[512,768]{1,0:T(8,128)(2,1)}, f32[1,768]{1,0:T(1,128)}, f32[1,768]{1,0:T(...) custom-call(s32[8]{0:T(128)} %stack.77.sc, ...), custom_call_target="tpu_custom_call" | custom-call | flops 3825205248 | bytes 8257536 | tf_op jit(solution)/shard_map/attn_bwd/pallas_call | solution.py:404
  102.6 4.2 %collective-permute-start.30 = (f32[72,128]{1,0:T(8,128)S(1)}, f32[72,128]{1,0:T(8,128)S(1)}, u32[]{:S(2)}, u32[]{:S(2)}) collective-permute-start(f32[72,128]{1,0:T(8,128)S(1)} %bitcast.82), channel_id=1, source_target_pairs={{0,8},{8,0},{16,24},{24,16},{1,9},{9,1},{17,25},{25,17},{2,10},{10... | collective-permute-start | bytes 110600 | tf_op jit(solution)/shard_map/ppermute | solution.py:496
  109.3 3.7 %collective-permute-done.31 = f32[72,128]{1,0:T(8,128)S(1)} collective-permute-done((f32[72,128]{1,0:T(8,128)S(1)}, f32[72,128]{1,0:T(8,128)S(1)}, u32[]{:S(2)}, u32[]{:S(2)}) %collective-permute-start.31) | collective-permute-done | bytes 36896 | tf_op jit(solution)/shard_map/ppermute | solution.py:496
  114.3 1.5 collective-permute-start.33
  115.8 1.5 constant_dynamic-slice_fusion
  118.3 2.6 collective-permute-start.34
  120.9 8.9 %wgrad_mix.1 = (bf16[384,768]{1,0:T(8,128)(2,1)}, bf16[384,768]{1,0:T(8,128)(2,1)}, bf16[384,768]{1,0:T(8,128)(2,1)}, bf16[384,768]{1,0:T(8,128)(2,1)}) custom-call(s32[8]{0:T(128)} %stack.77.sc, bf16[512,768]{1,0:T(8,128)(2,1)} %get-tuple-element.90.hid, bf16[512,768]{1,0:T(8,128)(2,1)} %collective-permute-done.12.hidp, ...), custom_call_target="tpu_custom_call" | custom-call | flops 2415919104 | bytes 10223616 | tf_op jit(solution)/shard_map/wgrad_mix/pallas_call | solution.py:485
  130.2 1.4 collective-permute-start.16
  131.6 1.6 constant_dynamic-slice_fusion.3
  133.4 4.0 %collective-permute-start.10 = (bf16[128,768]{1,0:T(8,128)(2,1)S(1)}, bf16[128,768]{1,0:T(8,128)(2,1)S(1)}, u32[]{:S(2)}, u32[]{:S(2)}) collective-permute-start(bf16[128,768]{1,0:T(8,128)(2,1)S(1)} %copy-done.33), channel_id=1, source_target_pairs={{0,16},{8,24},{16,0},{1,17},{9,25},{17,1},{2,18},{10,26},{18,2},{3... | collective-permute-start | bytes 589832 | tf_op jit(solution)/shard_map/ppermute | solution.py:613
  138.6 11.0 %collective-permute-done.10 = bf16[128,768]{1,0:T(8,128)(2,1)S(1)} collective-permute-done((bf16[128,768]{1,0:T(8,128)(2,1)S(1)}, bf16[128,768]{1,0:T(8,128)(2,1)S(1)}, u32[]{:S(2)}, u32[]{:S(2)}) %collective-permute-start.10) | collective-permute-done | bytes 196640 | tf_op jit(solution)/shard_map/ppermute | solution.py:613
  149.6 1.9 collective-permute-start.11
  151.6 2.8 collective-permute-start.9
  154.5 2.7 collective-permute-start.19
  158.5 2.6 collective-permute-done.9
  161.0 3.2 collective-permute-start.17
  164.9 3.3 collective-permute-done.19
  168.3 1.5 collective-permute-done.17
  169.8 3.9 %collective-permute-start.6 = (bf16[128,768]{1,0:T(8,128)(2,1)}, bf16[128,768]{1,0:T(8,128)(2,1)}, u32[]{:S(2)}, u32[]{:S(2)}) collective-permute-start(bf16[128,768]{1,0:T(8,128)(2,1)} %get-tuple-element.72), channel_id=1, source_target_pairs={{0,24},{8,16},{16,8},{1,25},{9,17},{17,9},{2,26},{10,18},{18,10},{... | collective-permute-start | bytes 589832 | tf_op jit(solution)/shard_map/ppermute | solution.py:613
  174.6 3.2 collective-permute-start.7
  177.9 1.7 collective-permute-start.20
  179.7 7.6 %wgrad_down.1 = (bf16[384,768]{1,0:T(8,128)(2,1)}, bf16[384,768]{1,0:T(8,128)(2,1)}, bf16[384,768]{1,0:T(8,128)(2,1)}, bf16[384,768]{1,0:T(8,128)(2,1)}) custom-call(s32[8]{0:T(128)} %stack.77.sc, bf16[512,3072]{1,0:T(8,128)(2,1)} %get-tuple-element.110.la, bf16[512,1536]{1,0:T(8,128)(2,1)} %collective-permute-done.51.lp, ...), custom_call_target="tpu_custom_call" | custom-call | flops 2415919104 | bytes 5505024 | tf_op jit(solution)/shard_map/wgrad_down/pallas_call | solution.py:441
  187.3 1.9 collective-permute-start.8
  189.3 8.4 %wgrad_up.1 = (bf16[384,768]{1,0:T(8,128)(2,1)}, bf16[384,768]{1,0:T(8,128)(2,1)}, bf16[384,768]{1,0:T(8,128)(2,1)}, bf16[384,768]{1,0:T(8,128)(2,1)}) custom-call(s32[8]{0:T(128)} %stack.77.sc, bf16[512,768]{1,0:T(8,128)(2,1)} %get-tuple-element.69.low.la, bf16[512,768]{1,0:T(8,128)(2,1)} %collective-permute-done.35.lp, ...), custom_call_target="tpu_custom_call" | custom-call | flops 2415919104 | bytes 5505024 | tf_op jit(solution)/shard_map/wgrad_up/pallas_call | solution.py:441
  197.7 2.1 collective-permute-start.53
  200.0 1.8 collective-permute-start.39
  204.2 8.1 %collective-permute-done.21 = bf16[2,48,768]{2,1,0:T(8,128)(2,1)S(1)} collective-permute-done((bf16[2,48,768]{2,1,0:T(8,128)(2,1)S(1)}, bf16[2,48,768]{2,1,0:T(8,128)(2,1)S(1)}, u32[]{:S(2)}, u32[]{:S(2)}) %collective-permute-start.21) | collective-permute-done | bytes 147488 | tf_op jit(solution)/shard_map/ppermute | solution.py:496
  214.1 1.9 collective-permute-start.54
  216.1 1.5 collective-permute-done.39
  217.6 2.4 collective-permute-start.40
  220.0 6.7 %collective-permute-done.37 = bf16[384,768]{1,0:T(8,128)(2,1)S(1)} collective-permute-done((bf16[384,768]{1,0:T(8,128)(2,1)S(1)}, bf16[384,768]{1,0:T(8,128)(2,1)S(1)}, u32[]{:S(2)}, u32[]{:S(2)}) %collective-permute-start.37) | collective-permute-done | bytes 589856 | tf_op jit(solution)/shard_map/ppermute | solution.py:496
  226.8 1.9 collective-permute-start.38
  229.2 3.8 %collective-permute-done.56 = bf16[192,768]{1,0:T(8,128)(2,1)S(1)} collective-permute-done((bf16[192,768]{1,0:T(8,128)(2,1)S(1)}, bf16[192,768]{1,0:T(8,128)(2,1)S(1)}, u32[]{:S(2)}, u32[]{:S(2)}) %collective-permute-start.56) | collective-permute-done | bytes 294944 | tf_op jit(solution)/shard_map/ppermute | solution.py:496
  233.7 2.8 collective-permute-done.40
  237.5 1.2 collective-permute-start.27
  238.7 1.7 collective-permute-start.24
  240.4 4.3 %collective-permute-done.57 = bf16[2,96,768]{2,1,0:T(8,128)(2,1)S(1)} collective-permute-done((bf16[2,96,768]{2,1,0:T(8,128)(2,1)S(1)}, bf16[2,96,768]{2,1,0:T(8,128)(2,1)S(1)}, u32[]{:S(2)}, u32[]{:S(2)}) %collective-permute-start.57) | collective-permute-done | bytes 294944 | tf_op jit(solution)/shard_map/ppermute | solution.py:496
  244.9 3.0 collective-permute-done.41
  249.0 8.4 %collective-permute-done.58 = bf16[2,48,768]{2,1,0:T(8,128)(2,1)S(1)} collective-permute-done((bf16[2,48,768]{2,1,0:T(8,128)(2,1)S(1)}, bf16[2,48,768]{2,1,0:T(8,128)(2,1)S(1)}, u32[]{:S(2)}, u32[]{:S(2)}) %collective-permute-start.58) | collective-permute-done | bytes 147488 | tf_op jit(solution)/shard_map/ppermute | solution.py:496
  257.5 6.2 %collective-permute-done.42 = bf16[2,48,768]{2,1,0:T(8,128)(2,1)S(1)} collective-permute-done((bf16[2,48,768]{2,1,0:T(8,128)(2,1)S(1)}, bf16[2,48,768]{2,1,0:T(8,128)(2,1)S(1)}, u32[]{:S(2)}, u32[]{:S(2)}) %collective-permute-start.42) | collective-permute-done | bytes 147488 | tf_op jit(solution)/shard_map/ppermute | solution.py:496
  263.8 4.6 %collective-permute-done.59 = bf16[2,48,768]{2,1,0:T(8,128)(2,1)S(1)} collective-permute-done((bf16[2,48,768]{2,1,0:T(8,128)(2,1)S(1)}, bf16[2,48,768]{2,1,0:T(8,128)(2,1)S(1)}, u32[]{:S(2)}, u32[]{:S(2)}) %collective-permute-start.59) | collective-permute-done | bytes 147488 | tf_op jit(solution)/shard_map/ppermute | solution.py:496
  271.2 7.2 %collective-permute-done.60 = bf16[2,96,768]{2,1,0:T(8,128)(2,1)S(1)} collective-permute-done((bf16[2,96,768]{2,1,0:T(8,128)(2,1)S(1)}, bf16[2,96,768]{2,1,0:T(8,128)(2,1)S(1)}, u32[]{:S(2)}, u32[]{:S(2)}) %collective-permute-start.60) | collective-permute-done | bytes 294944 | tf_op jit(solution)/shard_map/ppermute | solution.py:496
  278.8 3.7 %collective-permute-done.44 = bf16[2,96,768]{2,1,0:T(8,128)(2,1)S(1)} collective-permute-done((bf16[2,96,768]{2,1,0:T(8,128)(2,1)S(1)}, bf16[2,96,768]{2,1,0:T(8,128)(2,1)S(1)}, u32[]{:S(2)}, u32[]{:S(2)}) %collective-permute-start.44) | collective-permute-done | bytes 294944 | tf_op jit(solution)/shard_map/ppermute | solution.py:496
  282.8 4.9 %collective-permute-done.61 = bf16[192,768]{1,0:T(8,128)(2,1)S(1)} collective-permute-done((bf16[192,768]{1,0:T(8,128)(2,1)S(1)}, bf16[192,768]{1,0:T(8,128)(2,1)S(1)}, u32[]{:S(2)}, u32[]{:S(2)}) %collective-permute-start.61) | collective-permute-done | bytes 294944 | tf_op jit(solution)/shard_map/ppermute | solution.py:496
  288.3 1.7 collective-permute-start.62
  292.4 5.3 %collective-permute-done.48 = bf16[192,768]{1,0:T(8,128)(2,1)S(1)} collective-permute-done((bf16[192,768]{1,0:T(8,128)(2,1)S(1)}, bf16[192,768]{1,0:T(8,128)(2,1)S(1)}, u32[]{:S(2)}, u32[]{:S(2)}) %collective-permute-start.48) | collective-permute-done | bytes 294944 | tf_op jit(solution)/shard_map/ppermute | solution.py:496
  298.2 12.1 %collective-permute-done.62 = bf16[384,768]{1,0:T(8,128)(2,1)S(1)} collective-permute-done((bf16[384,768]{1,0:T(8,128)(2,1)S(1)}, bf16[384,768]{1,0:T(8,128)(2,1)S(1)}, u32[]{:S(2)}, u32[]{:S(2)}) %collective-permute-start.62) | collective-permute-done | bytes 589856 | tf_op jit(solution)/shard_map/ppermute | solution.py:496
  313.3 4.1 %collective-permute-done.46 = bf16[384,768]{1,0:T(8,128)(2,1)S(1)} collective-permute-done((bf16[384,768]{1,0:T(8,128)(2,1)S(1)}, bf16[384,768]{1,0:T(8,128)(2,1)S(1)}, u32[]{:S(2)}, u32[]{:S(2)}) %collective-permute-start.46) | collective-permute-done | bytes 589856 | tf_op jit(solution)/shard_map/ppermute | solution.py:496
  317.9 2.3 collective-permute-done.49
  321.2 1.6 select_convert_fusion
  323.0 3.2 maximum_convert_fusion.2
  326.7 4.1 %maximum_convert_fusion.1 = f32[3072,768]{1,0:T(8,128)} fusion(bf16[768,768]{1,0:T(8,128)(2,1)S(1)} %get-tuple-element.118, bf16[768,768]{1,0:T(8,128)(2,1)S(1)} %get-tuple-element.116, bf16[768,768]{1,0:T(8,128)(2,1)S(1)} %get-tuple-element.117, bf16[768,768]{1,0:T(8,128)(2,1)S(1)} %get-tuple-element.115), kind=kLoop, calls=%fused_computation.1 | loop fusion | flops 18874368 | bytes 14155776 | tf_op jit(solution)/shard_map/convert_element_type | solution.py:694
  331.0 4.3 %maximum_convert_fusion = f32[768,3072]{1,0:T(8,128)} fusion(bf16[768,768]{1,0:T(8,128)(2,1)S(1)} %get-tuple-element.122, bf16[768,768]{1,0:T(8,128)(2,1)S(1)} %get-tuple-element.120, bf16[768,768]{1,0:T(8,128)(2,1)S(1)} %get-tuple-element.121, bf16[768,768]{1,0:T(8,128)(2,1)S(1)} %get-tuple-element.119), kind=kLoop, calls=%fused_computation | loop fusion | flops 18874368 | bytes 14155776 | tf_op jit(solution)/shard_map/convert_element_type | solution.py:695
  (246 shorter events, 40.0 us)
Async XLA Ops:
  2.8 14.7 %collective-permute-start = (bf16[128,768]{1,0:T(8,128)(2,1)S(1)}, bf16[128,768]{1,0:T(8,128)(2,1)S(1)}, u32[]{:S(2)}, u32[]{:S(2)}) collective-permute-start(bf16[128,768]{1,0:T(8,128)(2,1)S(1)} %get-tuple-element.144), channel_id=1, source_target_pairs={{0,8},{8,0},{24,16},{1,9},{9,1},{25,17},{2,10},{10,2},{26,18},{3,1... | collective-permute-start | bytes 589832 | tf_op jit(solution)/shard_map/ppermute | solution.py:606
  7.7 12.5 %collective-permute-start.1 = (bf16[128,768]{1,0:T(8,128)(2,1)S(1)}, bf16[128,768]{1,0:T(8,128)(2,1)S(1)}, u32[]{:S(2)}, u32[]{:S(2)}) collective-permute-start(bf16[128,768]{1,0:T(8,128)(2,1)S(1)} %get-tuple-element.146), channel_id=1, source_target_pairs={{0,16},{16,0},{24,8},{1,17},{17,1},{25,9},{2,18},{18,2},{26,10},{3... | collective-permute-start | bytes 589832 | tf_op jit(solution)/shard_map/ppermute | solution.py:606
  9.6 10.5 %collective-permute-start.2 = (bf16[128,768]{1,0:T(8,128)(2,1)S(1)}, bf16[128,768]{1,0:T(8,128)(2,1)S(1)}, u32[]{:S(2)}, u32[]{:S(2)}) collective-permute-start(bf16[128,768]{1,0:T(8,128)(2,1)S(1)} %get-tuple-element.143), channel_id=1, source_target_pairs={{8,16},{16,8},{24,0},{9,17},{17,9},{25,1},{10,18},{18,10},{26,2},{... | collective-permute-start | bytes 589832 | tf_op jit(solution)/shard_map/ppermute | solution.py:606
  21.0 26.6 %collective-permute-start.3 = (bf16[128,768]{1,0:T(8,128)(2,1)S(1)}, bf16[128,768]{1,0:T(8,128)(2,1)S(1)}, u32[]{:S(2)}, u32[]{:S(2)}) collective-permute-start(bf16[128,768]{1,0:T(8,128)(2,1)S(1)} %get-tuple-element.141), channel_id=1, source_target_pairs={{0,8},{8,0},{24,16},{1,9},{9,1},{25,17},{2,10},{10,2},{26,18},{3,1... | collective-permute-start | bytes 589832 | tf_op jit(solution)/shard_map/ppermute | solution.py:606
  24.4 23.2 %collective-permute-start.4 = (bf16[128,768]{1,0:T(8,128)(2,1)S(1)}, bf16[128,768]{1,0:T(8,128)(2,1)S(1)}, u32[]{:S(2)}, u32[]{:S(2)}) collective-permute-start(bf16[128,768]{1,0:T(8,128)(2,1)S(1)} %get-tuple-element.140), channel_id=1, source_target_pairs={{0,16},{16,0},{24,8},{1,17},{17,1},{25,9},{2,18},{18,2},{26,10},{3... | collective-permute-start | bytes 589832 | tf_op jit(solution)/shard_map/ppermute | solution.py:606
  26.3 21.3 %collective-permute-start.5 = (bf16[128,768]{1,0:T(8,128)(2,1)S(1)}, bf16[128,768]{1,0:T(8,128)(2,1)S(1)}, u32[]{:S(2)}, u32[]{:S(2)}) collective-permute-start(bf16[128,768]{1,0:T(8,128)(2,1)S(1)} %get-tuple-element.139), channel_id=1, source_target_pairs={{8,16},{16,8},{24,0},{9,17},{17,9},{25,1},{10,18},{18,10},{26,2},{... | collective-permute-start | bytes 589832 | tf_op jit(solution)/shard_map/ppermute | solution.py:606
  47.0 71.3 %collective-permute-start.12 = (bf16[512,768]{1,0:T(8,128)(2,1)}, bf16[512,768]{1,0:T(8,128)(2,1)}, u32[]{:S(2)}, u32[]{:S(2)}) collective-permute-start(bf16[512,768]{1,0:T(8,128)(2,1)} %get-tuple-element.90.hid), channel_id=1, source_target_pairs={{0,1},{1,0},{2,3},{3,2},{4,5},{5,4},{6,7},{7,6},{8,9},{9,8},{10,11... | collective-permute-start | bytes 2359304 | tf_op jit(solution)/shard_map/ppermute | solution.py:496
  47.1 73.8 %collective-permute-start.13 = (bf16[512,768]{1,0:T(8,128)(2,1)}, bf16[512,768]{1,0:T(8,128)(2,1)}, u32[]{:S(2)}, u32[]{:S(2)}) collective-permute-start(bf16[512,768]{1,0:T(8,128)(2,1)} %get-tuple-element.91.ctx), channel_id=1, source_target_pairs={{0,1},{1,0},{2,3},{3,2},{4,5},{5,4},{6,7},{7,6},{8,9},{9,8},{10,11... | collective-permute-start | bytes 2359304 | tf_op jit(solution)/shard_map/ppermute | solution.py:496
  102.6 6.4 %collective-permute-start.30 = (f32[72,128]{1,0:T(8,128)S(1)}, f32[72,128]{1,0:T(8,128)S(1)}, u32[]{:S(2)}, u32[]{:S(2)}) collective-permute-start(f32[72,128]{1,0:T(8,128)S(1)} %bitcast.82), channel_id=1, source_target_pairs={{0,8},{8,0},{16,24},{24,16},{1,9},{9,1},{17,25},{25,17},{2,10},{10... | collective-permute-start | bytes 110600 | tf_op jit(solution)/shard_map/ppermute | solution.py:496
  107.7 13.1 %collective-permute-start.15 = (bf16[512,768]{1,0:T(8,128)(2,1)}, bf16[512,768]{1,0:T(8,128)(2,1)}, u32[]{:S(2)}, u32[]{:S(2)}) collective-permute-start(bf16[512,768]{1,0:T(8,128)(2,1)} %broadcast_select_fusion.11), channel_id=1, source_target_pairs={{0,1},{1,0},{2,3},{3,2},{4,5},{5,4},{6,7},{7,6},{8,9},{9,8},{10,11... | collective-permute-start | bytes 2359304 | tf_op jit(solution)/shard_map/ppermute | solution.py:496
  108.9 12.0 %collective-permute-start.14 = (bf16[512,768]{1,0:T(8,128)(2,1)S(1)}, bf16[512,768]{1,0:T(8,128)(2,1)}, u32[]{:S(2)}, u32[]{:S(2)}) collective-permute-start(bf16[512,768]{1,0:T(8,128)(2,1)S(1)} %broadcast_select_fusion.12), channel_id=1, source_target_pairs={{0,1},{1,0},{2,3},{3,2},{4,5},{5,4},{6,7},{7,6},{8,9},{9,8},{10,11... | collective-permute-start | bytes 2359304 | tf_op jit(solution)/shard_map/ppermute | solution.py:496
  118.3 59.6 %collective-permute-start.51 = (bf16[512,1536]{1,0:T(8,128)(2,1)S(1)}, bf16[512,1536]{1,0:T(8,128)(2,1)}, u32[]{:S(2)}, u32[]{:S(2)}) collective-permute-start(bf16[512,1536]{1,0:T(8,128)(2,1)S(1)} %constant_dynamic-slice_fusion), channel_id=1, source_target_pairs={{0,1},{1,0},{2,3},{3,2},{4,5},{5,4},{6,7},{7,6},{8,9},{9,8},{10,11... | collective-permute-start | bytes 4718600 | tf_op jit(solution)/shard_map/ppermute | solution.py:496
  118.3 15.1 %collective-permute-start.34 = (f32[72,128]{1,0:T(8,128)S(1)}, f32[72,128]{1,0:T(8,128)S(1)}, u32[]{:S(2)}, u32[]{:S(2)}) collective-permute-start(f32[72,128]{1,0:T(8,128)S(1)} %add.185), channel_id=1, source_target_pairs={{0,4},{1,5},{2,6},{3,7},{4,0},{5,1},{6,2},{7,3},{8,12},{9,13},{10,... | collective-permute-start | bytes 110600 | tf_op jit(solution)/shard_map/ppermute | solution.py:496
  129.8 21.8 %collective-permute-start.18 = (bf16[384,768]{1,0:T(8,128)(2,1)}, bf16[384,768]{1,0:T(8,128)(2,1)S(1)}, u32[]{:S(2)}, u32[]{:S(2)}) collective-permute-start(bf16[384,768]{1,0:T(8,128)(2,1)} %get-tuple-element.99), channel_id=1, source_target_pairs={{0,16},{8,24},{16,0},{24,8},{1,17},{9,25},{17,1},{25,9},{2,18},{10... | collective-permute-start | bytes 1769480 | tf_op jit(solution)/shard_map/ppermute | solution.py:496
  130.2 24.3 %collective-permute-start.16 = (bf16[384,768]{1,0:T(8,128)(2,1)}, bf16[384,768]{1,0:T(8,128)(2,1)S(1)}, u32[]{:S(2)}, u32[]{:S(2)}) collective-permute-start(bf16[384,768]{1,0:T(8,128)(2,1)} %get-tuple-element.97), channel_id=1, source_target_pairs={{0,8},{8,0},{16,24},{24,16},{1,9},{9,1},{17,25},{25,17},{2,10},{10... | collective-permute-start | bytes 1769480 | tf_op jit(solution)/shard_map/ppermute | solution.py:496
  133.3 55.9 %collective-permute-start.36 = (bf16[512,1536]{1,0:T(8,128)(2,1)S(1)}, bf16[512,1536]{1,0:T(8,128)(2,1)}, u32[]{:S(2)}, u32[]{:S(2)}) collective-permute-start(bf16[512,1536]{1,0:T(8,128)(2,1)S(1)} %constant_dynamic-slice_fusion.3), channel_id=1, source_target_pairs={{0,1},{1,0},{2,3},{3,2},{4,5},{5,4},{6,7},{7,6},{8,9},{9,8},{10,11... | collective-permute-start | bytes 4718600 | tf_op jit(solution)/shard_map/ppermute | solution.py:496
  133.4 16.2 %collective-permute-start.10 = (bf16[128,768]{1,0:T(8,128)(2,1)S(1)}, bf16[128,768]{1,0:T(8,128)(2,1)S(1)}, u32[]{:S(2)}, u32[]{:S(2)}) collective-permute-start(bf16[128,768]{1,0:T(8,128)(2,1)S(1)} %copy-done.33), channel_id=1, source_target_pairs={{0,16},{8,24},{16,0},{1,17},{9,25},{17,1},{2,18},{10,26},{18,2},{3... | collective-permute-start | bytes 589832 | tf_op jit(solution)/shard_map/ppermute | solution.py:613
  149.6 8.8 %collective-permute-start.11 = (bf16[128,768]{1,0:T(8,128)(2,1)S(1)}, bf16[128,768]{1,0:T(8,128)(2,1)S(1)}, u32[]{:S(2)}, u32[]{:S(2)}) collective-permute-start(bf16[128,768]{1,0:T(8,128)(2,1)S(1)} %copy-done.32), channel_id=1, source_target_pairs={{0,8},{8,0},{16,24},{1,9},{9,1},{17,25},{2,10},{10,2},{18,26},{3,1... | collective-permute-start | bytes 589832 | tf_op jit(solution)/shard_map/ppermute | solution.py:613
  151.6 9.5 %collective-permute-start.9 = (bf16[128,768]{1,0:T(8,128)(2,1)S(1)}, bf16[128,768]{1,0:T(8,128)(2,1)S(1)}, u32[]{:S(2)}, u32[]{:S(2)}) collective-permute-start(bf16[128,768]{1,0:T(8,128)(2,1)S(1)} %copy-done.31), channel_id=1, source_target_pairs={{0,24},{8,16},{16,8},{1,25},{9,17},{17,9},{2,26},{10,18},{18,10},{... | collective-permute-start | bytes 589832 | tf_op jit(solution)/shard_map/ppermute | solution.py:613
  154.5 13.8 %collective-permute-start.19 = (bf16[192,768]{1,0:T(8,128)(2,1)S(1)}, bf16[192,768]{1,0:T(8,128)(2,1)S(1)}, u32[]{:S(2)}, u32[]{:S(2)}) collective-permute-start(bf16[192,768]{1,0:T(8,128)(2,1)S(1)} %add_convert_fusion.16), channel_id=1, source_target_pairs={{0,8},{8,0},{16,24},{24,16},{1,9},{9,1},{17,25},{25,17},{2,10},{10... | collective-permute-start | bytes 884744 | tf_op jit(solution)/shard_map/ppermute | solution.py:496
  158.5 16.2 %collective-permute-start.52 = (bf16[512,768]{1,0:T(8,128)(2,1)S(1)}, bf16[512,768]{1,0:T(8,128)(2,1)S(1)}, u32[]{:S(2)}, u32[]{:S(2)}) collective-permute-start(bf16[512,768]{1,0:T(8,128)(2,1)S(1)} %copy-done.1), channel_id=1, source_target_pairs={{0,1},{1,0},{2,3},{3,2},{4,5},{5,4},{6,7},{7,6},{8,9},{9,8},{10,11... | collective-permute-start | bytes 2359304 | tf_op jit(solution)/shard_map/ppermute | solution.py:496
  161.0 8.8 %collective-permute-start.17 = (bf16[192,768]{1,0:T(8,128)(2,1)S(1)}, bf16[192,768]{1,0:T(8,128)(2,1)S(1)}, u32[]{:S(2)}, u32[]{:S(2)}) collective-permute-start(bf16[192,768]{1,0:T(8,128)(2,1)S(1)} %add_convert_fusion.19), channel_id=1, source_target_pairs={{0,16},{8,24},{16,0},{24,8},{1,17},{9,25},{17,1},{25,9},{2,18},{10... | collective-permute-start | bytes 884744 | tf_op jit(solution)/shard_map/ppermute | solution.py:496
  168.2 19.1 %collective-permute-start.35 = (bf16[512,768]{1,0:T(8,128)(2,1)}, bf16[512,768]{1,0:T(8,128)(2,1)}, u32[]{:S(2)}, u32[]{:S(2)}) collective-permute-start(bf16[512,768]{1,0:T(8,128)(2,1)} %get-tuple-element.69.low.la), channel_id=1, source_target_pairs={{0,1},{1,0},{2,3},{3,2},{4,5},{5,4},{6,7},{7,6},{8,9},{9,8},{10,11... | collective-permute-start | bytes 2359304 | tf_op jit(solution)/shard_map/ppermute | solution.py:496
  169.8 30.2 %collective-permute-start.6 = (bf16[128,768]{1,0:T(8,128)(2,1)}, bf16[128,768]{1,0:T(8,128)(2,1)}, u32[]{:S(2)}, u32[]{:S(2)}) collective-permute-start(bf16[128,768]{1,0:T(8,128)(2,1)} %get-tuple-element.72), channel_id=1, source_target_pairs={{0,24},{8,16},{16,8},{1,25},{9,17},{17,9},{2,26},{10,18},{18,10},{... | collective-permute-start | bytes 589832 | tf_op jit(solution)/shard_map/ppermute | solution.py:613
  174.6 27.2 %collective-permute-start.7 = (bf16[128,768]{1,0:T(8,128)(2,1)}, bf16[128,768]{1,0:T(8,128)(2,1)}, u32[]{:S(2)}, u32[]{:S(2)}) collective-permute-start(bf16[128,768]{1,0:T(8,128)(2,1)} %get-tuple-element.73), channel_id=1, source_target_pairs={{0,16},{8,24},{16,0},{1,17},{9,25},{17,1},{2,18},{10,26},{18,2},{3... | collective-permute-start | bytes 589832 | tf_op jit(solution)/shard_map/ppermute | solution.py:613
  177.9 19.8 %collective-permute-start.20 = (bf16[2,96,768]{2,1,0:T(8,128)(2,1)}, bf16[2,96,768]{2,1,0:T(8,128)(2,1)S(1)}, u32[]{:S(2)}, u32[]{:S(2)}) collective-permute-start(bf16[2,96,768]{2,1,0:T(8,128)(2,1)} %fusion.10), channel_id=1, source_target_pairs={{0,2},{1,3},{2,0},{3,1},{4,6},{5,7},{6,4},{7,5},{8,10},{9,11},{10,... | collective-permute-start | bytes 884744 | tf_op jit(solution)/shard_map/ppermute | solution.py:496
  187.3 14.9 %collective-permute-start.8 = (bf16[128,768]{1,0:T(8,128)(2,1)}, bf16[128,768]{1,0:T(8,128)(2,1)S(1)}, u32[]{:S(2)}, u32[]{:S(2)}) collective-permute-start(bf16[128,768]{1,0:T(8,128)(2,1)} %get-tuple-element.74), channel_id=1, source_target_pairs={{0,8},{8,0},{16,24},{1,9},{9,1},{17,25},{2,10},{10,2},{18,26},{3,1... | collective-permute-start | bytes 589832 | tf_op jit(solution)/shard_map/ppermute | solution.py:613
  189.2 23.2 %collective-permute-start.55 = (bf16[384,768]{1,0:T(8,128)(2,1)}, bf16[384,768]{1,0:T(8,128)(2,1)S(1)}, u32[]{:S(2)}, u32[]{:S(2)}) collective-permute-start(bf16[384,768]{1,0:T(8,128)(2,1)} %get-tuple-element.114), channel_id=1, source_target_pairs={{0,16},{8,24},{16,0},{24,8},{1,17},{9,25},{17,1},{25,9},{2,18},{10... | collective-permute-start | bytes 1769480 | tf_op jit(solution)/shard_map/ppermute | solution.py:496
  197.7 16.3 %collective-permute-start.53 = (bf16[384,768]{1,0:T(8,128)(2,1)S(1)}, bf16[384,768]{1,0:T(8,128)(2,1)S(1)}, u32[]{:S(2)}, u32[]{:S(2)}) collective-permute-start(bf16[384,768]{1,0:T(8,128)(2,1)S(1)} %copy-done.28), channel_id=1, source_target_pairs={{0,8},{8,0},{16,24},{24,16},{1,9},{9,1},{17,25},{25,17},{2,10},{10... | collective-permute-start | bytes 1769480 | tf_op jit(solution)/shard_map/ppermute | solution.py:496
  200.0 17.5 %collective-permute-start.39 = (bf16[384,768]{1,0:T(8,128)(2,1)S(1)}, bf16[384,768]{1,0:T(8,128)(2,1)S(1)}, u32[]{:S(2)}, u32[]{:S(2)}) collective-permute-start(bf16[384,768]{1,0:T(8,128)(2,1)S(1)} %copy-done.30), channel_id=1, source_target_pairs={{0,16},{8,24},{16,0},{24,8},{1,17},{9,25},{17,1},{25,9},{2,18},{10... | collective-permute-start | bytes 1769480 | tf_op jit(solution)/shard_map/ppermute | solution.py:496
  201.9 10.5 %collective-permute-start.21 = (bf16[2,48,768]{2,1,0:T(8,128)(2,1)S(1)}, bf16[2,48,768]{2,1,0:T(8,128)(2,1)S(1)}, u32[]{:S(2)}, u32[]{:S(2)}) collective-permute-start(bf16[2,48,768]{2,1,0:T(8,128)(2,1)S(1)} %constant_dynamic-slice_fusion.4), channel_id=1, source_target_pairs={{0,4},{1,5},{2,6},{3,7},{4,0},{5,1},{6,2},{7,3},{8,12},{9,13},{10,... | collective-permute-start | bytes 442376 | tf_op jit(solution)/shard_map/ppermute | solution.py:496
  203.4 23.3 %collective-permute-start.37 = (bf16[384,768]{1,0:T(8,128)(2,1)S(1)}, bf16[384,768]{1,0:T(8,128)(2,1)S(1)}, u32[]{:S(2)}, u32[]{:S(2)}) collective-permute-start(bf16[384,768]{1,0:T(8,128)(2,1)S(1)} %copy-done.29), channel_id=1, source_target_pairs={{0,8},{8,0},{16,24},{24,16},{1,9},{9,1},{17,25},{25,17},{2,10},{10... | collective-permute-start | bytes 1769480 | tf_op jit(solution)/shard_map/ppermute | solution.py:496
  212.4 16.4 %collective-permute-start.22 = (bf16[2,48,768]{2,1,0:T(8,128)(2,1)S(1)}, bf16[2,48,768]{2,1,0:T(8,128)(2,1)S(1)}, u32[]{:S(2)}, u32[]{:S(2)}) collective-permute-start(bf16[2,48,768]{2,1,0:T(8,128)(2,1)S(1)} %add_convert_fusion.23), channel_id=1, source_target_pairs={{0,4},{1,5},{2,6},{3,7},{4,0},{5,1},{6,2},{7,3},{8,12},{9,13},{10,... | collective-permute-start | bytes 442376 | tf_op jit(solution)/shard_map/ppermute | solution.py:496
  212.6 20.4 %collective-permute-start.56 = (bf16[192,768]{1,0:T(8,128)(2,1)S(1)}, bf16[192,768]{1,0:T(8,128)(2,1)S(1)}, u32[]{:S(2)}, u32[]{:S(2)}) collective-permute-start(bf16[192,768]{1,0:T(8,128)(2,1)S(1)} %add_convert_fusion.2), channel_id=1, source_target_pairs={{0,8},{8,0},{16,24},{24,16},{1,9},{9,1},{17,25},{25,17},{2,10},{10... | collective-permute-start | bytes 884744 | tf_op jit(solution)/shard_map/ppermute | solution.py:496
  214.1 19.0 %collective-permute-start.54 = (bf16[192,768]{1,0:T(8,128)(2,1)S(1)}, bf16[192,768]{1,0:T(8,128)(2,1)S(1)}, u32[]{:S(2)}, u32[]{:S(2)}) collective-permute-start(bf16[192,768]{1,0:T(8,128)(2,1)S(1)} %add_convert_fusion.5), channel_id=1, source_target_pairs={{0,16},{8,24},{16,0},{24,8},{1,17},{9,25},{17,1},{25,9},{2,18},{10... | collective-permute-start | bytes 884744 | tf_op jit(solution)/shard_map/ppermute | solution.py:496
  217.6 18.9 %collective-permute-start.40 = (bf16[192,768]{1,0:T(8,128)(2,1)S(1)}, bf16[192,768]{1,0:T(8,128)(2,1)S(1)}, u32[]{:S(2)}, u32[]{:S(2)}) collective-permute-start(bf16[192,768]{1,0:T(8,128)(2,1)S(1)} %add_convert_fusion.9), channel_id=1, source_target_pairs={{0,8},{8,0},{16,24},{24,16},{1,9},{9,1},{17,25},{25,17},{2,10},{10... | collective-permute-start | bytes 884744 | tf_op jit(solution)/shard_map/ppermute | solution.py:496
  226.8 9.9 %collective-permute-start.38 = (bf16[192,768]{1,0:T(8,128)(2,1)S(1)}, bf16[192,768]{1,0:T(8,128)(2,1)S(1)}, u32[]{:S(2)}, u32[]{:S(2)}) collective-permute-start(bf16[192,768]{1,0:T(8,128)(2,1)S(1)} %add_convert_fusion.12), channel_id=1, source_target_pairs={{0,16},{8,24},{16,0},{24,8},{1,17},{9,25},{17,1},{25,9},{2,18},{10... | collective-permute-start | bytes 884744 | tf_op jit(solution)/shard_map/ppermute | solution.py:496
  228.8 8.5 %collective-permute-start.23 = (bf16[2,96,768]{2,1,0:T(8,128)(2,1)S(1)}, bf16[2,96,768]{2,1,0:T(8,128)(2,1)S(1)}, u32[]{:S(2)}, u32[]{:S(2)}) collective-permute-start(bf16[2,96,768]{2,1,0:T(8,128)(2,1)S(1)} %maximum_select_fusion.15), channel_id=1, source_target_pairs={{0,2},{1,3},{2,0},{3,1},{4,6},{5,7},{6,4},{7,5},{8,10},{9,11},{10,... | collective-permute-start | bytes 884744 | tf_op jit(solution)/shard_map/ppermute | solution.py:496
  233.3 11.4 %collective-permute-start.57 = (bf16[2,96,768]{2,1,0:T(8,128)(2,1)S(1)}, bf16[2,96,768]{2,1,0:T(8,128)(2,1)S(1)}, u32[]{:S(2)}, u32[]{:S(2)}) collective-permute-start(bf16[2,96,768]{2,1,0:T(8,128)(2,1)S(1)} %fusion.6), channel_id=1, source_target_pairs={{0,2},{1,3},{2,0},{3,1},{4,6},{5,7},{6,4},{7,5},{8,10},{9,11},{10,... | collective-permute-start | bytes 884744 | tf_op jit(solution)/shard_map/ppermute | solution.py:496
  236.8 11.0 %collective-permute-start.41 = (bf16[2,96,768]{2,1,0:T(8,128)(2,1)S(1)}, bf16[2,96,768]{2,1,0:T(8,128)(2,1)S(1)}, u32[]{:S(2)}, u32[]{:S(2)}) collective-permute-start(bf16[2,96,768]{2,1,0:T(8,128)(2,1)S(1)} %fusion.8), channel_id=1, source_target_pairs={{0,2},{1,3},{2,0},{3,1},{4,6},{5,7},{6,4},{7,5},{8,10},{9,11},{10,... | collective-permute-start | bytes 884744 | tf_op jit(solution)/shard_map/ppermute | solution.py:496
  237.5 31.0 %collective-permute-start.27 = (bf16[192,768]{1,0:T(8,128)(2,1)S(1)}, bf16[192,768]{1,0:T(8,128)(2,1)S(1)}, u32[]{:S(2)}, u32[]{:S(2)}) collective-permute-start(bf16[192,768]{1,0:T(8,128)(2,1)S(1)} %get-tuple-element.137), channel_id=1, source_target_pairs={{0,8},{8,0},{16,24},{24,16},{1,9},{9,1},{17,25},{25,17},{2,10},{10... | collective-permute-start | bytes 884744 | tf_op jit(solution)/shard_map/ppermute | solution.py:496
  238.7 30.1 %collective-permute-start.24 = (bf16[192,768]{1,0:T(8,128)(2,1)S(1)}, bf16[192,768]{1,0:T(8,128)(2,1)S(1)}, u32[]{:S(2)}, u32[]{:S(2)}) collective-permute-start(bf16[192,768]{1,0:T(8,128)(2,1)S(1)} %get-tuple-element.138), channel_id=1, source_target_pairs={{0,16},{8,24},{16,0},{24,8},{1,17},{9,25},{17,1},{25,9},{2,18},{10... | collective-permute-start | bytes 884744 | tf_op jit(solution)/shard_map/ppermute | solution.py:496
  244.8 12.5 %collective-permute-start.58 = (bf16[2,48,768]{2,1,0:T(8,128)(2,1)S(1)}, bf16[2,48,768]{2,1,0:T(8,128)(2,1)S(1)}, u32[]{:S(2)}, u32[]{:S(2)}) collective-permute-start(bf16[2,48,768]{2,1,0:T(8,128)(2,1)S(1)} %constant_dynamic-slice_fusion.2), channel_id=1, source_target_pairs={{0,4},{1,5},{2,6},{3,7},{4,0},{5,1},{6,2},{7,3},{8,12},{9,13},{10,... | collective-permute-start | bytes 442376 | tf_op jit(solution)/shard_map/ppermute | solution.py:496
  248.0 15.7 %collective-permute-start.42 = (bf16[2,48,768]{2,1,0:T(8,128)(2,1)S(1)}, bf16[2,48,768]{2,1,0:T(8,128)(2,1)S(1)}, u32[]{:S(2)}, u32[]{:S(2)}) collective-permute-start(bf16[2,48,768]{2,1,0:T(8,128)(2,1)S(1)} %constant_dynamic-slice_fusion.1), channel_id=1, source_target_pairs={{0,4},{1,5},{2,6},{3,7},{4,0},{5,1},{6,2},{7,3},{8,12},{9,13},{10,... | collective-permute-start | bytes 442376 | tf_op jit(solution)/shard_map/ppermute | solution.py:496
  257.4 11.0 %collective-permute-start.59 = (bf16[2,48,768]{2,1,0:T(8,128)(2,1)S(1)}, bf16[2,48,768]{2,1,0:T(8,128)(2,1)S(1)}, u32[]{:S(2)}, u32[]{:S(2)}) collective-permute-start(bf16[2,48,768]{2,1,0:T(8,128)(2,1)S(1)} %add_convert_fusion.21), channel_id=1, source_target_pairs={{0,4},{1,5},{2,6},{3,7},{4,0},{5,1},{6,2},{7,3},{8,12},{9,13},{10,... | collective-permute-start | bytes 442376 | tf_op jit(solution)/shard_map/ppermute | solution.py:496
  263.7 6.3 %collective-permute-start.43 = (bf16[2,48,768]{2,1,0:T(8,128)(2,1)S(1)}, bf16[2,48,768]{2,1,0:T(8,128)(2,1)S(1)}, u32[]{:S(2)}, u32[]{:S(2)}) collective-permute-start(bf16[2,48,768]{2,1,0:T(8,128)(2,1)S(1)} %add_convert_fusion.22), channel_id=1, source_target_pairs={{0,4},{1,5},{2,6},{3,7},{4,0},{5,1},{6,2},{7,3},{8,12},{9,13},{10,... | collective-permute-start | bytes 442376 | tf_op jit(solution)/shard_map/ppermute | solution.py:496
  268.5 9.9 %collective-permute-start.60 = (bf16[2,96,768]{2,1,0:T(8,128)(2,1)S(1)}, bf16[2,96,768]{2,1,0:T(8,128)(2,1)S(1)}, u32[]{:S(2)}, u32[]{:S(2)}) collective-permute-start(bf16[2,96,768]{2,1,0:T(8,128)(2,1)S(1)} %maximum_select_fusion.17), channel_id=1, source_target_pairs={{0,2},{1,3},{2,0},{3,1},{4,6},{5,7},{6,4},{7,5},{8,10},{9,11},{10,... | collective-permute-start | bytes 884744 | tf_op jit(solution)/shard_map/ppermute | solution.py:496
  268.7 19.5 %collective-permute-start.28 = (bf16[384,768]{1,0:T(8,128)(2,1)S(1)}, bf16[384,768]{1,0:T(8,128)(2,1)S(1)}, u32[]{:S(2)}, u32[]{:S(2)}) collective-permute-start(bf16[384,768]{1,0:T(8,128)(2,1)S(1)} %maximum_select_fusion.8), channel_id=1, source_target_pairs={{0,16},{8,24},{16,0},{24,8},{1,17},{9,25},{17,1},{25,9},{2,18},{10... | collective-permute-start | bytes 1769480 | tf_op jit(solution)/shard_map/ppermute | solution.py:496
  269.0 21.5 %collective-permute-start.25 = (bf16[384,768]{1,0:T(8,128)(2,1)S(1)}, bf16[384,768]{1,0:T(8,128)(2,1)S(1)}, u32[]{:S(2)}, u32[]{:S(2)}) collective-permute-start(bf16[384,768]{1,0:T(8,128)(2,1)S(1)} %maximum_select_fusion.7), channel_id=1, source_target_pairs={{0,8},{8,0},{16,24},{24,16},{1,9},{9,1},{17,25},{25,17},{2,10},{10... | collective-permute-start | bytes 1769480 | tf_op jit(solution)/shard_map/ppermute | solution.py:496
  270.0 12.5 %collective-permute-start.44 = (bf16[2,96,768]{2,1,0:T(8,128)(2,1)S(1)}, bf16[2,96,768]{2,1,0:T(8,128)(2,1)S(1)}, u32[]{:S(2)}, u32[]{:S(2)}) collective-permute-start(bf16[2,96,768]{2,1,0:T(8,128)(2,1)S(1)} %maximum_select_fusion.16), channel_id=1, source_target_pairs={{0,2},{1,3},{2,0},{3,1},{4,6},{5,7},{6,4},{7,5},{8,10},{9,11},{10,... | collective-permute-start | bytes 884744 | tf_op jit(solution)/shard_map/ppermute | solution.py:496
  278.6 9.1 %collective-permute-start.61 = (bf16[192,768]{1,0:T(8,128)(2,1)S(1)}, bf16[192,768]{1,0:T(8,128)(2,1)S(1)}, u32[]{:S(2)}, u32[]{:S(2)}) collective-permute-start(bf16[192,768]{1,0:T(8,128)(2,1)S(1)} %get-tuple-element.133), channel_id=1, source_target_pairs={{0,16},{8,24},{16,0},{24,8},{1,17},{9,25},{17,1},{25,9},{2,18},{10... | collective-permute-start | bytes 884744 | tf_op jit(solution)/shard_map/ppermute | solution.py:496
  278.7 12.3 %collective-permute-start.64 = (bf16[192,768]{1,0:T(8,128)(2,1)S(1)}, bf16[192,768]{1,0:T(8,128)(2,1)S(1)}, u32[]{:S(2)}, u32[]{:S(2)}) collective-permute-start(bf16[192,768]{1,0:T(8,128)(2,1)S(1)} %get-tuple-element.134), channel_id=1, source_target_pairs={{0,8},{8,0},{16,24},{24,16},{1,9},{9,1},{17,25},{25,17},{2,10},{10... | collective-permute-start | bytes 884744 | tf_op jit(solution)/shard_map/ppermute | solution.py:496
  282.8 9.1 %collective-permute-start.45 = (bf16[192,768]{1,0:T(8,128)(2,1)S(1)}, bf16[192,768]{1,0:T(8,128)(2,1)S(1)}, u32[]{:S(2)}, u32[]{:S(2)}) collective-permute-start(bf16[192,768]{1,0:T(8,128)(2,1)S(1)} %get-tuple-element.135), channel_id=1, source_target_pairs={{0,16},{8,24},{16,0},{24,8},{1,17},{9,25},{17,1},{25,9},{2,18},{10... | collective-permute-start | bytes 884744 | tf_op jit(solution)/shard_map/ppermute | solution.py:496
  287.7 9.9 %collective-permute-start.48 = (bf16[192,768]{1,0:T(8,128)(2,1)S(1)}, bf16[192,768]{1,0:T(8,128)(2,1)S(1)}, u32[]{:S(2)}, u32[]{:S(2)}) collective-permute-start(bf16[192,768]{1,0:T(8,128)(2,1)S(1)} %get-tuple-element.136), channel_id=1, source_target_pairs={{0,8},{8,0},{16,24},{24,16},{1,9},{9,1},{17,25},{25,17},{2,10},{10... | collective-permute-start | bytes 884744 | tf_op jit(solution)/shard_map/ppermute | solution.py:496
  288.3 22.0 %collective-permute-start.62 = (bf16[384,768]{1,0:T(8,128)(2,1)S(1)}, bf16[384,768]{1,0:T(8,128)(2,1)S(1)}, u32[]{:S(2)}, u32[]{:S(2)}) collective-permute-start(bf16[384,768]{1,0:T(8,128)(2,1)S(1)} %maximum_select_fusion.13), channel_id=1, source_target_pairs={{0,8},{8,0},{16,24},{24,16},{1,9},{9,1},{17,25},{25,17},{2,10},{10... | collective-permute-start | bytes 1769480 | tf_op jit(solution)/shard_map/ppermute | solution.py:496
  290.5 30.1 %collective-permute-start.29 = (bf16[768,768]{1,0:T(8,128)(2,1)S(1)}, bf16[768,768]{1,0:T(8,128)(2,1)S(1)}, u32[]{:S(2)}, u32[]{:S(2)}) collective-permute-start(bf16[768,768]{1,0:T(8,128)(2,1)S(1)} %maximum_select_fusion.1), channel_id=1, source_target_pairs={{0,1},{1,0},{2,3},{3,2},{4,5},{5,4},{6,7},{7,6},{8,9},{9,8},{10,11... | collective-permute-start | bytes 3538952 | tf_op jit(solution)/shard_map/ppermute | solution.py:496
  291.1 31.8 %collective-permute-start.26 = (bf16[768,768]{1,0:T(8,128)(2,1)S(1)}, bf16[768,768]{1,0:T(8,128)(2,1)S(1)}, u32[]{:S(2)}, u32[]{:S(2)}) collective-permute-start(bf16[768,768]{1,0:T(8,128)(2,1)S(1)} %maximum_select_fusion), channel_id=1, source_target_pairs={{0,1},{1,0},{2,3},{3,2},{4,5},{5,4},{6,7},{7,6},{8,9},{9,8},{10,11... | collective-permute-start | bytes 3538952 | tf_op jit(solution)/shard_map/ppermute | solution.py:496
  291.9 20.9 %collective-permute-start.65 = (bf16[384,768]{1,0:T(8,128)(2,1)S(1)}, bf16[384,768]{1,0:T(8,128)(2,1)S(1)}, u32[]{:S(2)}, u32[]{:S(2)}) collective-permute-start(bf16[384,768]{1,0:T(8,128)(2,1)S(1)} %maximum_select_fusion.14), channel_id=1, source_target_pairs={{0,16},{8,24},{16,0},{24,8},{1,17},{9,25},{17,1},{25,9},{2,18},{10... | collective-permute-start | bytes 1769480 | tf_op jit(solution)/shard_map/ppermute | solution.py:496
  297.6 19.8 %collective-permute-start.46 = (bf16[384,768]{1,0:T(8,128)(2,1)S(1)}, bf16[384,768]{1,0:T(8,128)(2,1)S(1)}, u32[]{:S(2)}, u32[]{:S(2)}) collective-permute-start(bf16[384,768]{1,0:T(8,128)(2,1)S(1)} %maximum_select_fusion.10), channel_id=1, source_target_pairs={{0,8},{8,0},{16,24},{24,16},{1,9},{9,1},{17,25},{25,17},{2,10},{10... | collective-permute-start | bytes 1769480 | tf_op jit(solution)/shard_map/ppermute | solution.py:496
  310.3 9.9 %collective-permute-start.49 = (bf16[384,768]{1,0:T(8,128)(2,1)S(1)}, bf16[384,768]{1,0:T(8,128)(2,1)S(1)}, u32[]{:S(2)}, u32[]{:S(2)}) collective-permute-start(bf16[384,768]{1,0:T(8,128)(2,1)S(1)} %maximum_select_fusion.11), channel_id=1, source_target_pairs={{0,16},{8,24},{16,0},{24,8},{1,17},{9,25},{17,1},{25,9},{2,18},{10... | collective-permute-start | bytes 1769480 | tf_op jit(solution)/shard_map/ppermute | solution.py:496
  312.8 13.4 %collective-permute-start.63 = (bf16[768,768]{1,0:T(8,128)(2,1)S(1)}, bf16[768,768]{1,0:T(8,128)(2,1)S(1)}, u32[]{:S(2)}, u32[]{:S(2)}) collective-permute-start(bf16[768,768]{1,0:T(8,128)(2,1)S(1)} %maximum_select_fusion.4), channel_id=1, source_target_pairs={{0,1},{1,0},{2,3},{3,2},{4,5},{5,4},{6,7},{7,6},{8,9},{9,8},{10,11... | collective-permute-start | bytes 3538952 | tf_op jit(solution)/shard_map/ppermute | solution.py:496
  317.4 9.0 %collective-permute-start.66 = (bf16[768,768]{1,0:T(8,128)(2,1)S(1)}, bf16[768,768]{1,0:T(8,128)(2,1)S(1)}, u32[]{:S(2)}, u32[]{:S(2)}) collective-permute-start(bf16[768,768]{1,0:T(8,128)(2,1)S(1)} %maximum_select_fusion.5), channel_id=1, source_target_pairs={{0,1},{1,0},{2,3},{3,2},{4,5},{5,4},{6,7},{7,6},{8,9},{9,8},{10,11... | collective-permute-start | bytes 3538952 | tf_op jit(solution)/shard_map/ppermute | solution.py:496
  320.1 6.4 %collective-permute-start.47 = (bf16[768,768]{1,0:T(8,128)(2,1)S(1)}, bf16[768,768]{1,0:T(8,128)(2,1)S(1)}, u32[]{:S(2)}, u32[]{:S(2)}) collective-permute-start(bf16[768,768]{1,0:T(8,128)(2,1)S(1)} %maximum_select_fusion.2), channel_id=1, source_target_pairs={{0,1},{1,0},{2,3},{3,2},{4,5},{5,4},{6,7},{7,6},{8,9},{9,8},{10,11... | collective-permute-start | bytes 3538952 | tf_op jit(solution)/shard_map/ppermute | solution.py:496
  320.6 10.2 %collective-permute-start.50 = (bf16[768,768]{1,0:T(8,128)(2,1)S(1)}, bf16[768,768]{1,0:T(8,128)(2,1)S(1)}, u32[]{:S(2)}, u32[]{:S(2)}) collective-permute-start(bf16[768,768]{1,0:T(8,128)(2,1)S(1)} %maximum_select_fusion.3), channel_id=1, source_target_pairs={{0,1},{1,0},{2,3},{3,2},{4,5},{5,4},{6,7},{7,6},{8,9},{9,8},{10,11... | collective-permute-start | bytes 3538952 | tf_op jit(solution)/shard_map/ppermute | solution.py:496
  (41 other events, 478.8 us)

commit v2 on v1

v2 whole, which is shorter than its diff:
```python
import functools
import math

import jax
import jax.numpy as jnp
from jax import lax
from jax.experimental import pallas as pl
from jax.experimental.pallas import tpu as pltpu
from jax.sharding import PartitionSpec as P

HEADS = 12
EPS = 1e-12
BF = jnp.bfloat16
F32 = jnp.float32
VMEM_LIMIT = 60 * 1024 * 1024
LOG2E = math.log2(math.e)
HALVINGS = 4
S_SEQ, S_LEN, S_CORE = range(3)
S_FIRST = 3
S_FIRST_MIX = S_FIRST + HALVINGS


def dot_nn(left, right):
    return lax.dot_general(left, right, (((1,), (0,)), ((), ())), preferred_element_type=F32)


def dot_nt(left, right):
    return lax.dot_general(left, right, (((1,), (1,)), ((), ())), preferred_element_type=F32)


def dot_tn(left, right):
    return lax.dot_general(left, right, (((0,), (0,)), ((), ())), preferred_element_type=F32)


def params(flag=None):
    return pltpu.CompilerParams(vmem_limit_bytes=VMEM_LIMIT)


def cost(flops, nbytes, trans=0):
    return pl.CostEstimate(flops=int(flops), bytes_accessed=int(nbytes), transcendentals=int(trans))


def full(shape):
    zeros = (0,) * len(shape)
    return pl.BlockSpec(shape, lambda *_: zeros)


def shape_of(shape, dtype):
    return jax.ShapeDtypeStruct(shape, dtype)


def attn_fwd_body(sc, h0, h1, h2, h3, wq, wk, wv, qb, vb, wo, ob, gain, shift,
                  hlc, q_o, k_o, v_o, lse_o, n1_o, r1_o, acc, lse_s):
    step = pl.program_id(0)
    steps = pl.num_programs(0)
    local, width = h0.shape
    rows = hlc.shape[0]
    head = wq.shape[1] // 2
    wide = 2 * head

    @pl.when(step == 0)
    def _():
        for at, ref in enumerate((h0, h1, h2, h3)):
            hlc[at * local:(at + 1) * local, width:2 * width] = ref[...]
        acc[...] = jnp.zeros_like(acc)
        lse_s[...] = jnp.zeros_like(lse_s)

    x = hlc[:, width:2 * width]
    w = jnp.concatenate([wq[...], wk[...], wv[...]], axis=1)
    both = dot_nn(x, w)
    q_o[...] = (both[:, :wide] + qb[...]).astype(BF)
    k_o[...] = both[:, wide:2 * wide].astype(BF)
    v_o[...] = (both[:, 2 * wide:] + vb[...]).astype(BF)
    k = k_o[...]
    v = v_o[...]
    key = lax.broadcasted_iota(jnp.int32, (1, rows), 1)
    place = ((key // local) ^ sc[S_SEQ]) * local + key % local
    mask = jnp.where(place < sc[S_LEN], 0.0, -1e30).astype(F32)
    scale = head ** (-0.5) * LOG2E
    chunk = rows
    lane = lax.broadcasted_iota(jnp.int32, (chunk, wide), 1)
    lane_l = lax.broadcasted_iota(jnp.int32, (chunk, lse_s.shape[1]), 1)
    for part in range(rows // chunk):
        span = pl.ds(part * chunk, chunk)
        q = q_o[span, :]
        outs = []
        tops = []
        for h in range(2):
            mine = (lane >= h * head) & (lane < (h + 1) * head)
            qh = jnp.where(mine, q, jnp.zeros_like(q))
            s = dot_nt(qh, k) * scale + mask
            top = jnp.max(s, -1, keepdims=True)
            e = jnp.exp2(s - top)
            total = jnp.sum(e, -1, keepdims=True)
            pv = dot_nn(e.astype(BF), v)
            outs.append(pv / total)
            tops.append(top + jnp.log2(total))
        ctx = jnp.where(lane < head, outs[0], outs[1]).astype(BF)
        hlc[span, pl.ds(pl.multiple_of(2 * width + step * wide, wide), wide)] = ctx
        acc[span, :] += dot_nn(ctx, wo[...])
        old = lse_s[span, :]
        old = jnp.where(lane_l == 2 * step, tops[0], old)
        lse_s[span, :] = jnp.where(lane_l == 2 * step + 1, tops[1], old)

    @pl.when(step == steps - 1)
    def _():
        lse_o[...] = jnp.transpose(lse_s[...])[:lse_o.shape[0], :]

        @pl.loop(0, rows // local)
        def _(part):
            span = pl.ds(pl.multiple_of(part * local, local), local)
            val = hlc[span, width:2 * width].astype(F32) + (acc[span, :] + ob[...])
            cen = val - jnp.mean(val, -1, keepdims=True)
            r = lax.rsqrt(jnp.mean(cen * cen, -1, keepdims=True) + EPS)
            n = cen * r
            n1_o[span, :] = n
            r1_o[span, :] = jnp.broadcast_to(r, (local, r1_o.shape[1]))
            hlc[span, :width] = (n * gain[...] + shift[...]).astype(BF)


def attn_fwd(sc, blocks, qkv_w, qb, vb, out_w, ob, gain, shift):
    local, width = blocks[0].shape
    rows = local * len(blocks)
    pairs = HEADS // 2
    wide = width // pairs
    row = lambda i, s: (0, i)
    grid = pltpu.PrefetchScalarGridSpec(
        num_scalar_prefetch=1,
        grid=(pairs,),
        in_specs=[full((local, width))] * 4 + [
            pl.BlockSpec((width, wide), lambda i, s: (0, i)),
            pl.BlockSpec((width, wide), lambda i, s: (0, pairs + i)),
            pl.BlockSpec((width, wide), lambda i, s: (0, 2 * pairs + i)),
            pl.BlockSpec((1, wide), row),
            pl.BlockSpec((1, wide), row),
            pl.BlockSpec((wide, width), lambda i, s: (i, 0)),
            full((1, width)), full((1, width)), full((1, width)),
        ],
        out_specs=[
            full((rows, 3 * width)),
            pl.BlockSpec((rows, wide), row),
            pl.BlockSpec((rows, wide), row),
            pl.BlockSpec((rows, wide), row),
            full((16, rows)),
            full((rows, width)),
            full((rows, 128)),
        ],
        scratch_shapes=[pltpu.VMEM((rows, width), F32), pltpu.VMEM((rows, 128), F32)],
    )
    wide_bf = shape_of((rows, width), BF)
    return pl.pallas_call(
        attn_fwd_body,
        grid_spec=grid,
        out_shape=[shape_of((rows, 3 * width), BF), wide_bf, wide_bf, wide_bf, shape_of((16, rows), F32),
                   shape_of((rows, width), F32), shape_of((rows, 128), F32)],
        compiler_params=params(),
        cost_estimate=cost(2 * rows * width * width * 4 + 4 * rows * rows * width, 12 * rows * width + 8 * width * width,
                           HEADS * rows * rows),
        name="attn_fwd",
    )(sc, *blocks, qkv_w, qkv_w, qkv_w, qb, vb, out_w, ob, gain, shift)


def ffn_fwd_body(sc, low, n1, gain1, shift1, wu, ub, wd, db, gain2, shift2, c0, c1, c2, c3,
                 act_o, slope_o, send_o, lo_o, dsec_o, stat_o, acc):
    step = pl.program_id(0)
    steps = pl.num_programs(0)
    local, width = c0.shape
    tile = wu.shape[1]
    up = dot_nn(low[...], wu[...]) + ub[...]
    cdf = 0.5 * (1.0 + lax.erf(up * (2.0 ** -0.5)))
    bell = jnp.exp2(up * up * (-0.5 * LOG2E)) * ((2.0 * math.pi) ** -0.5)
    act = (up * cdf).astype(BF)
    act_o[...] = act
    slope_o[...] = (cdf + up * bell).astype(BF)
    base = (1 - sc[S_CORE]) * (steps // 2)

    @pl.when((step >= base) & (step < base + steps // 2))
    def _():
        send_o[:, pl.ds(pl.multiple_of((step - base) * tile, tile), tile)] = act_o[...]

    term = dot_nn(act, wd[...])

    @pl.when(step == 0)
    def _():
        acc[...] = term

    @pl.when(step > 0)
    def _():
        acc[...] += term

    @pl.when(step == steps - 1)
    def _():
        stat_o[...] = jnp.zeros_like(stat_o)
        for at, cot in enumerate((c0, c1, c2, c3)):
            span = pl.ds(at * local, local)
            first = n1[span, :] * gain1[...] + shift1[...]
            val = first + (acc[span, :] + db[...])
            cen = val - jnp.mean(val, -1, keepdims=True)
            r = lax.rsqrt(jnp.mean(cen * cen, -1, keepdims=True) + EPS)
            n = cen * r
            lo_o[span, :] = (n * gain2[...] + shift2[...]).astype(BF)
            dy = cot[...].astype(F32)
            dn = dy * gain2[...]
            ds = r * (dn - jnp.mean(dn, -1, keepdims=True) - n * jnp.mean(dn * n, -1, keepdims=True))
            dsec_o[span, :] = ds
            dlow = ds.astype(BF)
            send_o[span, send_o.shape[1] - width:] = dlow
            stat_o[0:1, :] += jnp.sum(dy * n, 0, keepdims=True)
            stat_o[1:2, :] += jnp.sum(dy, 0, keepdims=True)
            stat_o[2:3, :] += jnp.sum(dlow.astype(F32), 0, keepdims=True)


def ffn_fwd(sc, hlc, n1, gain1, shift1, wu, ub, wd, db, gain2, shift2, cots):
    rows, width = n1.shape
    inner = wu.shape[1]
    tile = width
    steps = inner // tile
    local = cots[0].shape[0]
    one = full((1, width))
    wide = full((rows, width))
    quarter = full((local, width))
    col = pl.BlockSpec((rows, tile), lambda i, s: (0, i))
    grid = pltpu.PrefetchScalarGridSpec(
        num_scalar_prefetch=1,
        grid=(steps,),
        in_specs=[wide, wide, one, one, pl.BlockSpec((width, tile), lambda i, s: (0, i)),
                  pl.BlockSpec((1, tile), lambda i, s: (0, i)),
                  pl.BlockSpec((tile, width), lambda i, s: (i, 0)), one, one, one] + [quarter] * 4,
        out_specs=[col, col, full((rows, inner // 2 + width)), wide, wide, full((8, width))],
        scratch_shapes=[pltpu.VMEM((rows, width), F32)],
    )
    return pl.pallas_call(
        ffn_fwd_body,
        grid_spec=grid,
        out_shape=[shape_of((rows, inner), BF)] * 2 + [shape_of((rows, inner // 2 + width), BF),
                   shape_of((rows, width), BF), shape_of((rows, width), F32), shape_of((8, width), F32)],
        compiler_params=params(),
        cost_estimate=cost(4 * rows * width * inner, 4 * width * inner + 4 * rows * inner, 2 * rows * inner),
        name="ffn_fwd",
    )(sc, hlc, n1, gain1, shift1, wu, ub, wd, db, gain2, shift2, *cots)


def ffn_bwd_body(sc, dffn, wd, slope, wu, dsec, n1, r1, gain1, wo,
                 dup_o, send_o, dres_o, dattn_o, dctx_o, stat_o, acc):
    step = pl.program_id(0)
    steps = pl.num_programs(0)
    tile = wu.shape[1]
    dact = dot_nt(dffn[...], wd[...])
    dup = (dact * slope[...].astype(F32)).astype(BF)
    dup_o[...] = dup
    stat_o[pl.ds(4 + step, 1), :] = jnp.sum(dup.astype(F32), 0, keepdims=True)
    base = (1 - sc[S_CORE]) * (steps // 2)

    @pl.when((step >= base) & (step < base + steps // 2))
    def _():
        send_o[:, pl.ds(pl.multiple_of((step - base) * tile, tile), tile)] = dup_o[...]

    term = dot_nt(dup, wu[...])

    @pl.when(step == 0)
    def _():
        acc[...] = term

    @pl.when(step > 0)
    def _():
        acc[...] += term

    @pl.when(step == steps - 1)
    def _():
        rows, width = n1.shape
        local = 128
        stat_o[0:4, :] = jnp.zeros((4, width), F32)
        for at in range(rows // local):
            span = pl.ds(at * local, local)
            dfirst = dsec[span, :] + acc[span, :]
            n = n1[span, :]
            dn = dfirst * gain1[...]
            r = r1[span, 0:1]
            dres = r * (dn - jnp.mean(dn, -1, keepdims=True) - n * jnp.mean(dn * n, -1, keepdims=True))
            dres_o[span, :] = dres
            dlow = dres.astype(BF)
            dattn_o[span, :] = dlow
            stat_o[0:1, :] += jnp.sum(dfirst * n, 0, keepdims=True)
            stat_o[1:2, :] += jnp.sum(dfirst, 0, keepdims=True)
            stat_o[2:3, :] += jnp.sum(dlow.astype(F32), 0, keepdims=True)
        dctx_o[...] = dot_nt(dattn_o[...], wo[...]).astype(BF)


def ffn_bwd(sc, send, wd, slope, wu, dsec, n1, r1, gain1, wo):
    rows, width = dsec.shape
    inner = wu.shape[1]
    tile = width
    steps = inner // tile
    wide = full((rows, width))
    last = send.shape[1] // width - 1
    col = pl.BlockSpec((rows, tile), lambda i, s: (0, i))
    grid = pltpu.PrefetchScalarGridSpec(
        num_scalar_prefetch=1,
        grid=(steps,),
        in_specs=[pl.BlockSpec((rows, width), lambda i, s: (0, last)),
                  pl.BlockSpec((tile, width), lambda i, s: (i, 0)), col,
                  pl.BlockSpec((width, tile), lambda i, s: (0, i)), wide, wide, full((rows, 128)),
                  full((1, width)), full((width, width))],
        out_specs=[col, full((rows, inner // 2)), wide, wide, wide, full((8, width))],
        scratch_shapes=[pltpu.VMEM((rows, width), F32)],
    )
    return pl.pallas_call(
        ffn_bwd_body,
        grid_spec=grid,
        out_shape=[shape_of((rows, inner), BF), shape_of((rows, inner // 2), BF), shape_of((rows, width), F32),
                   shape_of((rows, width), BF), shape_of((rows, width), BF), shape_of((8, width), F32)],
        compiler_params=params(),
        cost_estimate=cost(4 * rows * width * inner, 4 * width * inner + 4 * rows * inner),
        name="ffn_bwd",
    )(sc, send, wd, slope, wu, dsec, n1, r1, gain1, wo)


def split_terms(value):
    high = value.astype(BF)
    return high, (value - high.astype(F32)).astype(BF)


def attn_bwd_body(sc, q_r, k_r, v_r, g_r, lse, wq, wk, wv, dres, da_r, lo, stat1, stat2,
                  dq_o, dk_o, dv_o, send_o, small_o, i0, i1, i2, i3, acc):
    step = pl.program_id(0)
    steps = pl.num_programs(0)
    rows, wide = q_r.shape
    head = wide // 2
    local = i0.shape[0] // 2
    scale = head ** (-0.5)
    q = q_r[...]
    g = g_r[...]
    k = k_r[...]
    v = v_r[...]
    lane = lax.broadcasted_iota(jnp.int32, (rows, wide), 1)
    chunk = rows
    nchunk = rows // chunk
    dks = [[None, None] for _ in range(nchunk)]
    dvs = [[None, None] for _ in range(nchunk)]
    dqs = []
    for h in range(2):
        mine = (lane >= h * head) & (lane < (h + 1) * head)
        qh = jnp.where(mine, q, jnp.zeros_like(q))
        gh = jnp.where(mine, g, jnp.zeros_like(g))
        row = lse[pl.ds(2 * step + h, 1), :]
        ps = []
        dps = []
        delta = jnp.zeros((1, rows), F32)
        for c in range(nchunk):
            kc = k[c * chunk:(c + 1) * chunk, :]
            vc = v[c * chunk:(c + 1) * chunk, :]
            key = lax.broadcasted_iota(jnp.int32, (chunk, 1), 0) + c * chunk
            place = ((key // local) ^ sc[S_SEQ]) * local + key % local
            mask = jnp.where(place < sc[S_LEN], 0.0, -1e30).astype(F32)
            s = dot_nt(kc, qh) * (scale * LOG2E) + mask
            p = jnp.exp2(s - row)
            dp = dot_nt(vc, gh)
            delta += jnp.sum(p * dp, 0, keepdims=True)
            dvs[c][h] = dot_nn(p.astype(BF), g)
            ps.append(p)
            dps.append(dp)
        dq = None
        for c in range(nchunk):
            ds = (ps[c] * (dps[c] - delta)).astype(BF)
            dks[c][h] = dot_nn(ds, q)
            term = dot_tn(ds, k[c * chunk:(c + 1) * chunk, :])
            dq = term if dq is None else dq + term
        dqs.append(dq)
    low = lane < head
    low_c = low[:chunk, :]
    dq_o[...] = (jnp.where(low, dqs[0], dqs[1]) * scale).astype(BF)
    for c in range(nchunk):
        span = pl.ds(c * chunk, chunk)
        dk_o[span, :] = (jnp.where(low_c, dks[c][0], dks[c][1]) * scale).astype(BF)
        dv_o[span, :] = jnp.where(low_c, dvs[c][0], dvs[c][1]).astype(BF)
    dqv = dq_o[...]
    dkv = dk_o[...]
    dvv = dv_o[...]
    here = pl.ds(pl.multiple_of(step * wide, wide), wide)
    small_o[6:7, here] = jnp.sum(dqv.astype(F32), 0, keepdims=True)
    small_o[7:8, here] = jnp.sum(dvv.astype(F32), 0, keepdims=True)

    @pl.when(sc[S_CORE] == 0)
    def _():
        send_o[0:rows, here] = dv_o[...]
        send_o[rows:2 * rows, here] = da_r[...]

    @pl.when(sc[S_CORE] != 0)
    def _():
        send_o[0:rows, here] = dq_o[...]
        send_o[rows:2 * rows, here] = dk_o[...]

    three = jnp.concatenate([dqv, dkv, dvv], axis=1)
    w = jnp.concatenate([wq[...], wk[...], wv[...]], axis=1)
    term = dot_nt(three, w)

    @pl.when(step == 0)
    def _():
        acc[...] = dres[...] + term

    @pl.when(step > 0)
    def _():
        acc[...] += term

    @pl.when(step == steps - 1)
    def _():
        for at, ref in enumerate((i0, i1, i2, i3)):
            ref[0:local, :] = lo[at * local:(at + 1) * local, :]
            ref[local:2 * local, :] = acc[pl.ds(at * local, local), :].astype(BF)
        small_o[0:3, :] = stat2[0:3, :]
        small_o[3:6, :] = stat1[0:3, :]
        small_o[8:12, :] = stat1[4:8, :]
        small_o[12:16, :] = jnp.zeros((4, small_o.shape[1]), F32)
        high, rest = split_terms(small_o[...])
        send_o[2 * rows:2 * rows + 16, :] = high
        send_o[2 * rows + 16:2 * rows + 32, :] = rest


def attn_bwd(sc, q, k, v, g, lse, qkv_w, dres, dattn, lo, stat1, stat2, local):
    rows, width = q.shape
    pairs = HEADS // 2
    wide = width // pairs
    col = pl.BlockSpec((rows, wide), lambda i, s: (0, i))
    quarter = full((2 * local, width))
    grid = pltpu.PrefetchScalarGridSpec(
        num_scalar_prefetch=1,
        grid=(pairs,),
        in_specs=[col, col, col, col, full(lse.shape),
                  pl.BlockSpec((width, wide), lambda i, s: (0, i)),
                  pl.BlockSpec((width, wide), lambda i, s: (0, pairs + i)),
                  pl.BlockSpec((width, wide), lambda i, s: (0, 2 * pairs + i)),
                  full((rows, width)), col, full((rows, width)), full((8, width)), full((8, width))],
        out_specs=[col, col, col, full((2 * rows + 32, width)), full((16, width))] + [quarter] * 4,
        scratch_shapes=[pltpu.VMEM((rows, width), F32)],
    )
    wide_bf = shape_of((rows, width), BF)
    return pl.pallas_call(
        attn_bwd_body,
        grid_spec=grid,
        out_shape=[wide_bf, wide_bf, wide_bf, shape_of((2 * rows + 32, width), BF),
                   shape_of((16, width), F32)] + [shape_of((2 * local, width), BF)] * 4,
        compiler_params=params(),
        cost_estimate=cost(6 * rows * width * width + 10 * rows * rows * width, 12 * rows * width + 6 * width * width,
                           HEADS * rows * rows),
        name="attn_bwd",
    )(sc, q, k, v, g, lse, qkv_w, qkv_w, qkv_w, dres, dattn, lo, stat1, stat2)


def wgrad_body(sc, la, lp, ra, rp, *refs):
    step = pl.program_id(0)
    send, keep = refs[-2:]
    val = (dot_tn(la[...], ra[...]) + dot_tn(lp[...], rp[...])).astype(BF)

    @pl.when(step < 2)
    def _():
        send[...] = val

    @pl.when(step >= 2)
    def _():
        keep[...] = val


def half_of(j, sc):
    return jnp.where(j < 2, 1 - sc[S_FIRST], sc[S_FIRST])


def wgrad(sc, la, lp, ra, rp, maps, at, units, into, name):
    rows = la.shape[0]
    unit = ra.shape[1] if ra.shape[1] < 768 else 768
    half = unit // 2
    m_la, m_lp, m_ra, m_rp = maps
    grid = pltpu.PrefetchScalarGridSpec(
        num_scalar_prefetch=1,
        grid=(4,),
        in_specs=[pl.BlockSpec((rows, half), m_la), pl.BlockSpec((rows, half), m_lp),
                  pl.BlockSpec((rows, unit), m_ra), pl.BlockSpec((rows, unit), m_rp)]
        + [pl.BlockSpec(memory_space=pl.ANY)] * len(into),
        out_specs=[pl.BlockSpec((half, unit), lambda j, s: (at + jnp.minimum(j, 1), 0)),
                   pl.BlockSpec((half, unit), lambda j, s: (at + jnp.maximum(j - 2, 0), 0))],
    )
    return pl.pallas_call(
        wgrad_body,
        grid_spec=grid,
        out_shape=[shape_of((units * half, unit), BF)] * 2,
        input_output_aliases={5 + i: i for i in range(len(into))},
        compiler_params=params(),
        cost_estimate=cost(2 * 4 * half * unit * rows * 2, 8 * half * unit + 8 * rows * unit),
        name=name,
    )(sc, la, lp, ra, rp, *into)


def wgrad_mix_body(sc, hid, hidp, ctx, ctxp, dq, dk, dv, da, peer, small, send, keep, small_o):
    step = pl.program_id(0)
    core = sc[S_CORE]
    rows, unit = dq.shape
    half = unit // 2

    def put(val):
        val = val.astype(BF)

        @pl.when(step < 2)
        def _():
            send[pl.ds(pl.multiple_of(step * half, half), half), :] = val

        @pl.when(step >= 2)
        def _():
            keep[pl.ds(pl.multiple_of((step - 2) * half, half), half), :] = val

    @pl.when(step % 2 == 0)
    def _():
        @pl.when(core == 0)
        def _():
            put(dot_tn(hid[...], dq[...]) + dot_tn(hidp[...], peer[0:rows, :]))

        @pl.when(core != 0)
        def _():
            put(dot_tn(hid[...], dv[...]) + dot_tn(hidp[...], peer[0:rows, :]))

    @pl.when(step % 2 == 1)
    def _():
        @pl.when(core == 0)
        def _():
            put(dot_tn(hid[...], dk[...]) + dot_tn(hidp[...], peer[rows:2 * rows, :]))

        @pl.when(core != 0)
        def _():
            put(dot_tn(ctx[...], da[...]) + dot_tn(ctxp[...], peer[rows:2 * rows, :]))

    @pl.when(step == 0)
    def _():
        got = peer[2 * rows:2 * rows + 16, :].astype(F32) + peer[2 * rows + 16:2 * rows + 32, :].astype(F32)
        val = small[...] + got
        small_o[...] = val
        high, rest = split_terms(val)
        send[unit:unit + 16, :] = high
        send[unit + 16:unit + 32, :] = rest


def wgrad_mix(sc, hlc, hlcp, dq, dk, dv, da, peer, small):
    rows, unit = dq.shape
    half = unit // 2

    def cut(at):
        return pl.BlockSpec((rows, half), lambda j, s: (0, at + jnp.where(j < 2, 1 - s[S_FIRST_MIX], s[S_FIRST_MIX])))

    wide = full((rows, unit))
    grid = pltpu.PrefetchScalarGridSpec(
        num_scalar_prefetch=1,
        grid=(4,),
        in_specs=[cut(2), cut(2), cut(4), cut(4)] + [wide] * 4 + [full(peer.shape), full(small.shape)],
        out_specs=[full((unit + 32, unit)), full((unit, unit)), full(small.shape)],
    )
    return pl.pallas_call(
        wgrad_mix_body,
        grid_spec=grid,
        out_shape=[shape_of((unit + 32, unit), BF), shape_of((unit, unit), BF), shape_of(small.shape, F32)],
        compiler_params=params(),
        cost_estimate=cost(2 * 4 * half * unit * rows * 2, 8 * half * unit + 20 * rows * unit),
        name="wgrad_mix",
    )(sc, hlc, hlcp, hlc, hlcp, dq, dk, dv, da, peer, small)


def fold_body(sc, keep, got, *refs, units, bit_at):
    last = bit_at is None
    small = refs[0] if len(refs) in (3, 4) and not last else None
    rows = keep.shape[0] // units
    if last:
        out = refs[-1] if len(refs) == 1 else refs[1]
        out[...] = (keep[...].astype(F32) + got[0:units * rows, :].astype(F32)).astype(BF)
        if len(refs) > 1:
            low = units * rows
            refs[2][...] = refs[0][...] + got[low:low + 16, :].astype(F32) + got[low + 16:low + 32, :].astype(F32)
        return
    half = rows // 2
    bit = sc[bit_at]
    if small is None:
        send_o, keep_o = refs
    else:
        send_o, keep_o, small_o = refs[1:]
    for u in range(units):
        go = pl.ds(pl.multiple_of(u * rows + (1 - bit) * half, 16), half)
        stay = pl.ds(pl.multiple_of(u * rows + bit * half, 16), half)
        send_o[u * half:(u + 1) * half, :] = (keep[go, :].astype(F32) + got[go, :].astype(F32)).astype(BF)
        keep_o[u * half:(u + 1) * half, :] = (keep[stay, :].astype(F32) + got[stay, :].astype(F32)).astype(BF)
    if small is not None:
        low = units * rows
        val = small[...] + (got[low:low + 16, :].astype(F32) + got[low + 16:low + 32, :].astype(F32))
        small_o[...] = val
        high, rest = split_terms(val)
        send_o[units * half:units * half + 16, :] = high
        send_o[units * half + 16:units * half + 32, :] = rest


def fold(sc, keep, got, small, units, bit_at):
    rows, width = keep.shape
    vmem = pl.BlockSpec(memory_space=pltpu.VMEM)
    extra = 0 if small is None else 32
    if bit_at is None:
        outs = [shape_of((rows, width), BF)]
    else:
        outs = [shape_of((rows // 2 + extra, width), BF), shape_of((rows // 2, width), BF)]
    args = [keep, got]
    if small is not None:
        outs.append(shape_of(small.shape, F32))
        args.append(small)
    return pl.pallas_call(
        functools.partial(fold_body, units=units, bit_at=bit_at),
        out_shape=outs,
        in_specs=[pl.BlockSpec(memory_space=pltpu.SMEM)] + [vmem] * len(args),
        out_specs=[vmem] * len(outs),
        compiler_params=params(),
        cost_estimate=cost(2 * rows * width, 6 * rows * width),
        name="fold",
    )(sc, *args)


def swap(value, axis, mask, size):
    return lax.ppermute(value, axis, [(i, i ^ mask) for i in range(size)])


def join(own, other, bit, units):
    rows = own.shape[0] // units
    own = own.reshape(units, rows, own.shape[1])
    other = other.reshape(units, rows, other.shape[1])
    both = jnp.where(
        bit == 0, jnp.concatenate([own, other], 1), jnp.concatenate([other, own], 1)
    )
    return both.reshape(2 * units * rows, own.shape[2])


class Piece:
    def __init__(self, units, masks, bits, at, members):
        self.units, self.masks, self.bits, self.at, self.members = units, masks, bits, at, members

    def permute(self, value, stage):
        pairs = [(i, i ^ self.masks[i & 1][stage]) for i in range(self.members)]
        return lax.ppermute(value, ("seq", "dp"), pairs)


def after(token, *values):
    return lax.optimization_barrier((token,) + values)[1:]


def corner(value):
    return value[:8, :128]


def body(
    hidden_in,
    lengths,
    qkv_weight,
    query_bias,
    value_bias,
    out_weight,
    out_bias,
    attn_gain,
    attn_shift,
    up_weight,
    up_bias,
    down_weight,
    down_bias,
    ffn_gain,
    ffn_shift,
    cotangent,
):
    count, local, width = hidden_in.shape
    nseq = lax.axis_size("seq")
    ndp = lax.axis_size("dp")
    seq = lax.axis_index("seq")
    dp = lax.axis_index("dp")
    core = dp & 1
    flat = seq * ndp + dp
    members = nseq * ndp
    line = lambda vec: vec.reshape(1, -1)

    x_mask, y_mask = ndp, 2 * ndp
    dp_masks = []
    mask = 2
    while mask < ndp:
        dp_masks.append(mask)
        mask *= 2
    z_mask, rest = dp_masks[0], dp_masks[1:]

    def piece(units, orders, at):
        masks = [list(order) + rest for order in orders]
        bits = []
        for stage in range(len(masks[0])):
            pick = jnp.where(core == 0, masks[0][stage], masks[1][stage])
            bits.append(jnp.where((flat & pick) != 0, 1, 0))
        return Piece(units, masks, bits, at, members)

    big = piece(4, [(x_mask, y_mask, z_mask), (y_mask, z_mask, x_mask)], S_FIRST)
    mix = piece(2, [(z_mask, x_mask, y_mask), (x_mask, z_mask, y_mask)], S_FIRST_MIX)

    holder = jnp.minimum(seq, count - 1)
    own_len = lax.dynamic_index_in_dim(lengths, holder, 0, False)
    own_len = jnp.where(seq < count, own_len, nseq * local)
    sc = jnp.stack([seq, own_len, core] + big.bits[:HALVINGS] + mix.bits[:HALVINGS]).astype(jnp.int32)

    def to_holder(value):
        blocks = [lax.dynamic_index_in_dim(value, holder, 0, False)]
        parts = [lax.dynamic_index_in_dim(value, jnp.minimum(seq ^ k, count - 1), 0, False) for k in range(1, nseq)]
        for k in range(1, nseq):
            pairs = [(i, i ^ k) for i in range(nseq) if (i ^ k) < count]
            blocks.append(lax.ppermute(parts[k - 1], "seq", pairs))
        return blocks

    hids = to_holder(hidden_in)
    cots = to_holder(cotangent)
    cots[0] = jnp.where(seq < count, cots[0], jnp.zeros_like(cots[0]))

    hlc, q, k, v, lse, n1, r1 = attn_fwd(
        sc, hids, qkv_weight, line(query_bias), line(value_bias), out_weight, line(out_bias),
        line(attn_gain), line(attn_shift))

    def core_swap(value):
        return swap(value, "dp", 1, ndp)

    hlc_p = core_swap(hlc)
    act, slope, send, lo, dsec, stat2 = ffn_fwd(
        sc, hlc, n1, line(attn_gain), line(attn_shift), up_weight, line(up_bias), down_weight,
        line(down_bias), line(ffn_gain), line(ffn_shift), cots)
    act_p = core_swap(send)
    dup, dup_send, dres, dattn, dctx, stat1 = ffn_bwd(
        sc, send, down_weight, slope, up_weight, dsec, n1, r1, line(attn_gain), out_weight)
    dup_p = core_swap(dup_send)
    last = send.shape[1] // width - 1
    into = wgrad(
        sc, act, act_p, send, act_p,
        (lambda j, s: (0, s[S_CORE] * 4 + (j % 2) * 2 + half_of(j, s)),
         lambda j, s: (0, (j % 2) * 2 + half_of(j, s)),
         lambda j, s: (0, last), lambda j, s: (0, last)), 0, 4, (), "wgrad_down")
    send1, keep1 = wgrad(
        sc, hlc, hlc_p, dup, dup_p,
        (lambda j, s: (0, half_of(j, s)), lambda j, s: (0, half_of(j, s)),
         lambda j, s: (0, s[S_CORE] * 2 + j % 2), lambda j, s: (0, j % 2)), 2, 4, into, "wgrad_up")
    got1 = big.permute(send1, 0)
    (dctx,) = after(corner(keep1), dctx)
    dq, dk, dv, peer_send, small, i0, i1, i2, i3 = attn_bwd(
        sc, q, k, v, dctx, lse, qkv_weight, dres, dattn, lo, stat1, stat2, local)
    peer = core_swap(peer_send)
    send2, keep2, small = wgrad_mix(sc, hlc, hlc_p, dq, dk, dv, dattn, peer, small)
    got2 = mix.permute(send2, 0)
    token = corner(keep2)

    big_stages = len(big.bits)
    done1, done2 = [], []
    for stage in range(big_stages):
        halve = stage + 1 < min(HALVINGS, big_stages)
        more = stage + 1 < big_stages
        keep1, got1 = after(token, keep1, got1)
        if halve:
            send1, keep1 = fold(sc, keep1, got1, None, big.units, big.at + stage + 1)
        else:
            (keep1,) = fold(sc, keep1, got1, None, big.units, None)
            send1 = keep1
        token = corner(keep1)
        if more:
            got1 = big.permute(send1, stage + 1)
        if stage == 0:
            blocks = after(token, i0, i1, i2, i3)
            back = [blocks[0]]
            for k_at in range(1, nseq):
                pairs = [(i, i ^ k_at) for i in range(nseq) if i < count]
                back.append(lax.ppermute(blocks[k_at], "seq", pairs))
        keep2, got2, small = after(token, keep2, got2, small)
        if halve:
            send2, keep2, small = fold(sc, keep2, got2, small, mix.units, mix.at + stage + 1)
        else:
            keep2, small = fold(sc, keep2, got2, small, mix.units, None)
            if more:
                high, low = split_terms(small)
                send2 = jnp.concatenate([keep2, high, low], 0)
        token = corner(keep2)
        if more:
            got2 = mix.permute(send2, stage + 1)

    for stage in reversed(range(min(HALVINGS, big_stages))):
        (keep1,) = after(token, keep1)
        other1 = big.permute(keep1, stage)
        other2 = mix.permute(keep2, stage)
        other1, keep1 = after(token, other1, keep1)
        keep1 = join(keep1, other1, big.bits[stage], big.units)
        token = corner(keep1)
        other2, keep2 = after(token, other2, keep2)
        keep2 = join(keep2, other2, mix.bits[stage], mix.units)
        token = corner(keep2)

    unit = lambda arr, u: arr[u * width:(u + 1) * width]
    peer1 = core_swap(keep1)
    peer2 = core_swap(keep2)
    is0 = core == 0
    lo1, hi1 = jnp.where(is0, keep1, peer1), jnp.where(is0, peer1, keep1)
    down_grad = jnp.concatenate([lo1[:2 * width], hi1[:2 * width]], 0).astype(F32)
    up_grad = jnp.concatenate([unit(lo1, 2), unit(lo1, 3), unit(hi1, 2), unit(hi1, 3)], 1).astype(F32)
    lo2, hi2 = jnp.where(is0, keep2, peer2), jnp.where(is0, peer2, keep2)
    qkv_grad = jnp.concatenate([unit(lo2, 0), unit(lo2, 1), unit(hi2, 0)], 1).astype(F32)
    out_grad = unit(hi2, 1).astype(F32)

    shown = []
    for p in range(count):
        value = back[0]
        for k_at in range(1, nseq):
            value = jnp.where((seq ^ p) == k_at, back[k_at], value)
        shown.append(value)
    layer_out = jnp.stack([value[:local] for value in shown])
    input_grad = jnp.stack([value[local:] for value in shown])
    return (
        layer_out,
        input_grad,
        qkv_grad,
        small[6],
        small[7],
        out_grad,
        small[5],
        small[3],
        small[4],
        up_grad,
        small[8:12].reshape(-1),
        down_grad,
        small[2],
        small[0],
        small[1],
    )


def solution(mesh):
    split = P("dp", "seq", None)
    return jax.shard_map(
        body,
        mesh=mesh,
        in_specs=(split, P("dp")) + (P(),) * 13 + (split,),
        out_specs=(split, split) + (P(),) * 13,
        check_vma=False,
    )
```

time: 336 us -> 369 us (1.098)
  starting transfers between devices: 76 us -> 46.2 us
  waiting for transfers between devices: 119 us -> 142 us
  Pallas kernels: 96.1 us -> 118 us
  other arithmetic: 27.9 us -> 39.4 us
  local copies, waits for them, and re-layouts: 14.2 us -> 20.8 us
    ppermute x12 -> x25, waiting for transfers between devices: 17.4 us -> 138 us  [the longest x16 125 us: permute(): return lax.ppermute(value, ('seq', 'dp'), pairs)]
    ppermute x55 -> x6, waiting for transfers between devices: 101 us -> 3.33 us  [swap(): return lax.ppermute(value, axis, [(i, i ^ mask) for i in range(size)])]
    ppermute x55 -> x6, starting transfers between devices: 43.5 us -> 3.52 us  [swap(): return lax.ppermute(value, axis, [(i, i ^ mask) for i in range(size)])]
    pallas_call x4 -> x12, Pallas kernels: 44.2 us -> 60.9 us  [the longest x8 19.9 us: fold(): pl.pallas_call(functools.partial(fold_body, units=units, bit_at=bit_at),...]
    select_n x25 -> x11, other arithmetic: 6.39 us -> 21.9 us  [the longest x8 14.4 us: join(): jnp.where(bit == 0, jnp.concatenate([own, other], 1), jnp.concatenate([ot...]
    ppermute x12 -> x25, starting transfers between devices: 32.5 us -> 42.7 us  [the longest x6 19.4 us: to_holder(): blocks.append(lax.ppermute(parts[k - 1], 'seq', pairs))]
    unnamed x80 -> x56, local copies, waits for them, and re-layouts: 0.96 us -> 11 us
    convert_element_type x16 -> x4, other arithmetic: 14.1 us -> 13.8 us  [the longest x1 4.48 us: body(): jnp.concatenate([lo1[:2 * width], hi1[:2 * width]], 0).astype(F32)]
  transfers between devices with their start and end apart: 67 -> 31, of which waited for: 28 -> 14; matrix products, arithmetic and copies ran while one was open for 10% -> 8% of each run, Pallas kernels for 29% -> 25%
where the time goes in v2:
time: 369 us; the launch traced here: 368 us
  waiting for transfers between devices  142 us (38%)
  Pallas kernels  118 us (32%)
  starting transfers between devices  46.2 us (13%)
  other arithmetic  39.4 us (11%)
  local copies, waits for them, and re-layouts  20.8 us (6%)
    ppermute x16, waiting for transfers between devices, permute(): return lax.ppermute(value, ('seq', 'dp'), pairs)  125 us
    pallas_call x1, Pallas kernels, attn_bwd(): pl.pallas_call(attn_bwd_body, grid_spec=grid, out_shape=[wide_bf, wide_bf...  22.4 us
    pallas_call x8, Pallas kernels, fold(): pl.pallas_call(functools.partial(fold_body, units=units, bit_at=bit_at),...  19.9 us
    ppermute x6, starting transfers between devices, to_holder(): blocks.append(lax.ppermute(parts[k - 1], 'seq', pairs))  19.4 us
    pallas_call x1, Pallas kernels, ffn_bwd(): pl.pallas_call(ffn_bwd_body, grid_spec=grid, out_shape=[shape_of((rows, i...  17.5 us
    pallas_call x1, Pallas kernels, ffn_fwd(): pl.pallas_call(ffn_fwd_body, grid_spec=grid, out_shape=[shape_of((rows, i...  17.4 us
    pallas_call x1, Pallas kernels, attn_fwd(): pl.pallas_call(attn_fwd_body, grid_spec=grid, out_shape=[shape_of((rows,...  16.7 us
    ppermute x16, starting transfers between devices, permute(): return lax.ppermute(value, ('seq', 'dp'), pairs)  15.5 us
  transfers between devices with their start and end apart: 31, of which 14 were waited for; matrix products, arithmetic and copies ran while one was open for 8% of the time, Pallas kernels for 25%

profile of v2, /device:TPU:0, one launch (start us, length us, event | category | flops | bytes accessed | tf_op | source)
XLA Modules:
  0.0 368.4 jit_solution(9154945169347890695)
XLA Ops:
  0.8 2.0 dynamic-slice_bitcast_fusion.3
  2.7 1.3 collective-permute-start.2
  4.0 7.0 %collective-permute-start = (bf16[128,768]{1,0:T(8,128)(2,1)S(1)}, bf16[128,768]{1,0:T(8,128)(2,1)S(1)}, u32[]{:S(2)}, u32[]{:S(2)}) collective-permute-start(bf16[128,768]{1,0:T(8,128)(2,1)S(1)} %get-tuple-element.235), channel_id=1, source_target_pairs={{0,8},{8,0},{24,16},{1,9},{9,1},{25,17},{2,10},{10,2},{26,18},{3,1... | collective-permute-start | bytes 589832 | tf_op jit(solution)/shard_map/ppermute | solution.py:705
  11.0 1.9 collective-permute-start.1
  12.9 2.0 dynamic-slice_bitcast_fusion
  14.9 1.3 collective-permute-start.6
  16.2 6.0 %collective-permute-start.4 = (bf16[128,768]{1,0:T(8,128)(2,1)S(1)}, bf16[128,768]{1,0:T(8,128)(2,1)S(1)}, u32[]{:S(2)}, u32[]{:S(2)}) collective-permute-start(bf16[128,768]{1,0:T(8,128)(2,1)S(1)} %get-tuple-element.231), channel_id=1, source_target_pairs={{0,8},{8,0},{24,16},{1,9},{9,1},{25,17},{2,10},{10,2},{26,18},{3,1... | collective-permute-start | bytes 589832 | tf_op jit(solution)/shard_map/ppermute | solution.py:705
  28.8 1.9 collective-permute-start.5
  31.5 16.7 %attn_fwd.1 = (bf16[512,2304]{1,0:T(8,128)(2,1)}, bf16[512,768]{1,0:T(8,128)(2,1)}, bf16[512,768]{1,0:T(8,128)(2,1)}, bf16[512,768]{1,0:T(8,128)(2,1)}, f32[16,5...) custom-call(s32[11]{0:T(128)} %stack.65.sc, bf16[128,768]{1,0:T(8,128)(2,1)} %get-tuple-element.236.h0, ...), custom_call_target="tpu_custom_call" | custom-call | flops 3221225472 | bytes 9437184 | tf_op jit(solution)/shard_map/attn_fwd/pallas_call | solution.py:151
  49.0 17.4 %ffn_fwd.1 = (bf16[512,3072]{1,0:T(8,128)(2,1)}, bf16[512,3072]{1,0:T(8,128)(2,1)}, bf16[512,2304]{1,0:T(8,128)(2,1)}, bf16[512,768]{1,0:T(8,128)(2,1)}, f32[512,768]{1,0:T(8,128)}, /*index=5*/f32[8,768]{1,0:T(8,128)}) custom-call(s32[11]{0:T(128)} %stack.65.sc, bf16[512,2304]{1,0:T(8,128)(2,1)} %get-tuple-element.111.low.la.hid.ctx, ...), custom_call_target="tpu_custom_call" | custom-call | flops 4831838208 | bytes 15728640 | tf_op jit(solution)/shard_map/ffn_fwd/pallas_call | solution.py:232
  67.0 17.5 %ffn_bwd.1 = (bf16[512,3072]{1,0:T(8,128)(2,1)}, bf16[512,1536]{1,0:T(8,128)(2,1)}, f32[512,768]{1,0:T(8,128)}, bf16[512,768]{1,0:T(8,128)(2,1)}, bf16[512,768]{1,0:T(8,128)(2,1)}, /*index=5*/f32[8,768]{1,0:T(8,128)}) custom-call(s32[11]{0:T(128)} %stack.65.sc, bf16[512,2304]{1,0:T(8,128)(2,1)} %get-tuple-element.113.dffn.ra, bf16[3072,768]{1,0:T(8,128)(2,1)} %wd.3, ...), custom_call_target="tpu_custom_call" | custom-call | flops 4831838208 | bytes 15728640 | tf_op jit(solution)/shard_map/ffn_bwd/pallas_call | solution.py:307
  84.6 7.4 %wgrad_down.1 = (bf16[1536,768]{1,0:T(8,128)(2,1)}, bf16[1536,768]{1,0:T(8,128)(2,1)}) custom-call(s32[11]{0:T(128)} %stack.65.sc, bf16[512,3072]{1,0:T(8,128)(2,1)} %get-tuple-element.119.la, bf16[512,2304]{1,0:T(8,128)(2,1)} %collective-permute-done.8.lp.rp, bf16[512,2304]{1,0:T(8,128)(2,1)} %get-tuple-element.113.dffn.ra, ...), custom_call_target="tpu_custom_call" | custom-call | flops 2415919104 | bytes 5505024 | tf_op jit(solution)/shard_map/wgrad_down/pallas_call | solution.py:481
  92.1 1.1 copy-done.4
  93.2 7.8 %wgrad_up.1 = (bf16[1536,768]{1,0:T(8,128)(2,1)}, bf16[1536,768]{1,0:T(8,128)(2,1)}) custom-call(s32[11]{0:T(128)} %stack.65.sc, bf16[512,2304]{1,0:T(8,128)(2,1)} %get-tuple-element.111.low.la.hid.ctx, bf16[512,2304]{1,0:T(8,128)(2,1)} %collective-permute-done.3.lp.hidp.ctxp, ...), custom_call_target="tpu_custom_call", output_to_operand_aliasing={{0}: (5, {}), {1}: (6, {})} | custom-call | flops 2415919104 | bytes 5505024 | tf_op jit(solution)/shard_map/wgrad_up/pallas_call | solution.py:481
  101.1 22.4 %attn_bwd.1 = (bf16[512,768]{1,0:T(8,128)(2,1)}, bf16[512,768]{1,0:T(8,128)(2,1)}, bf16[512,768]{1,0:T(8,128)(2,1)}, bf16[1056,768]{1,0:T(8,128)(2,1)}, f32[16,7...) custom-call(s32[11]{0:T(128)} %stack.65.sc, ...), custom_call_target="tpu_custom_call" | custom-call | flops 3825205248 | bytes 8257536 | tf_op jit(solution)/shard_map/attn_bwd/pallas_call | solution.py:437
  123.5 2.2 collective-permute-start.13
  125.7 3.3 collective-permute-done.13.peer
  129.1 1.2 copy-done.3
  130.2 9.1 %wgrad_mix.1 = (bf16[800,768]{1,0:T(8,128)(2,1)}, bf16[768,768]{1,0:T(8,128)(2,1)}, f32[16,768]{1,0:T(8,128)}) custom-call(s32[11]{0:T(128)} %stack.65.sc, bf16[512,2304]{1,0:T(8,128)(2,1)} %get-tuple-element.111.low.la.hid.ctx, bf16[512,2304]{1,0:T(8,128)(2,1)} %collective-permute-done.3.lp.hidp.ctxp, bf16[512,2304]{1,0:T(8,128)(2,1)} %get-tuple-element.111.low.la.hid.ctx, ...), custom_call_target="tpu_custom_call" | custom-call | flops 2415919104 | bytes 10223616 | tf_op jit(solution)/shard_map/wgrad_mix/pallas_call | solution.py:553
  139.3 1.6 collective-permute-start.14
  141.0 1.4 copy-done.2
  142.4 4.3 %fold.8 = (bf16[768,768]{1,0:T(8,128)(2,1)}, bf16[768,768]{1,0:T(8,128)(2,1)}) custom-call(s32[11]{0:T(128)} %stack.65.sc, bf16[1536,768]{1,0:T(8,128)(2,1)} %get-tuple-element.124.keep, bf16[1536,768]{1,0:T(8,128)(2,1)} %copy-done.2), custom_call_target="tpu_custom_call" | custom-call | flops 2359296 | bytes 7077888 | tf_op jit(solution)/shard_map/fold/pallas_call | solution.py:606
  146.9 17.5 %collective-permute-done.14.got = bf16[800,768]{1,0:T(8,128)(2,1)S(1)} collective-permute-done((bf16[800,768]{1,0:T(8,128)(2,1)}, bf16[800,768]{1,0:T(8,128)(2,1)S(1)}, u32[]{:S(2)}, u32[]{:S(2)}) %collective-permute-start.14) | collective-permute-done | bytes 1228832 | tf_op jit(solution)/shard_map/ppermute | solution.py:637
  164.4 1.0 copy-done.5
  165.4 2.9 fold.9
  168.4 1.0 copy-done.6
  169.4 2.9 fold.13
  172.2 1.6 collective-permute-start.24
  173.8 8.6 %collective-permute-done.15.got = bf16[416,768]{1,0:T(8,128)(2,1)S(1)} collective-permute-done((bf16[416,768]{1,0:T(8,128)(2,1)}, bf16[416,768]{1,0:T(8,128)(2,1)S(1)}, u32[]{:S(2)}, u32[]{:S(2)}) %collective-permute-start.15) | collective-permute-done | bytes 639008 | tf_op jit(solution)/shard_map/ppermute | solution.py:637
  183.3 2.2 fold.10
  186.6 2.2 fold.14
  188.8 2.6 collective-permute-start.25
  191.4 1.5 collective-permute-done.16.got
  193.6 1.9 fold.11
  195.5 2.6 collective-permute-start.17
  198.1 14.8 %collective-permute-done.17.got = bf16[128,768]{1,0:T(8,128)(2,1)S(1)} collective-permute-done((bf16[128,768]{1,0:T(8,128)(2,1)}, bf16[128,768]{1,0:T(8,128)(2,1)S(1)}, u32[]{:S(2)}, u32[]{:S(2)}) %collective-permute-start.17) | collective-permute-done | bytes 196640 | tf_op jit(solution)/shard_map/ppermute | solution.py:637
  213.5 1.7 fold.12
  216.0 1.8 fold.15
  217.8 2.9 collective-permute-start.18
  220.8 18.7 %collective-permute-done.18 = bf16[96,768]{1,0:T(8,128)(2,1)S(1)} collective-permute-done((bf16[96,768]{1,0:T(8,128)(2,1)}, bf16[96,768]{1,0:T(8,128)(2,1)S(1)}, u32[]{:S(2)}, u32[]{:S(2)}) %collective-permute-start.18) | collective-permute-done | bytes 147488 | tf_op jit(solution)/shard_map/ppermute | solution.py:637
  239.5 1.0 maximum_select_fusion.7
  240.6 1.2 maximum_select_fusion.6
  242.4 7.0 %collective-permute-done.19 = bf16[192,768]{1,0:T(8,128)(2,1)S(1)} collective-permute-done((bf16[192,768]{1,0:T(8,128)(2,1)S(1)}, bf16[192,768]{1,0:T(8,128)(2,1)S(1)}, u32[]{:S(2)}, u32[]{:S(2)}) %collective-permute-start.19) | collective-permute-done | bytes 294944 | tf_op jit(solution)/shard_map/ppermute | solution.py:637
  249.5 2.2 collective-permute-done.27
  252.7 2.0 collective-permute-start.20
  254.7 7.9 %collective-permute-done.20 = bf16[384,768]{1,0:T(8,128)(2,1)S(1)} collective-permute-done((bf16[384,768]{1,0:T(8,128)(2,1)S(1)}, bf16[384,768]{1,0:T(8,128)(2,1)S(1)}, u32[]{:S(2)}, u32[]{:S(2)}) %collective-permute-start.20) | collective-permute-done | bytes 589856 | tf_op jit(solution)/shard_map/ppermute | solution.py:637
  263.0 5.6 %collective-permute-done.28 = bf16[768,768]{1,0:T(8,128)(2,1)} collective-permute-done((bf16[768,768]{1,0:T(8,128)(2,1)S(1)}, bf16[768,768]{1,0:T(8,128)(2,1)}, u32[]{:S(2)}, u32[]{:S(2)}) %collective-permute-start.28) | collective-permute-done | bytes 1179680 | tf_op jit(solution)/shard_map/ppermute | solution.py:637
  268.6 2.9 maximum_select_fusion.2
  272.0 41.2 %collective-permute-done.29 = bf16[1536,768]{1,0:T(8,128)(2,1)} collective-permute-done((bf16[1536,768]{1,0:T(8,128)(2,1)S(1)}, bf16[1536,768]{1,0:T(8,128)(2,1)}, u32[]{:S(2)}, u32[]{:S(2)}) %collective-permute-start.29) | collective-permute-done | bytes 2359328 | tf_op jit(solution)/shard_map/ppermute | solution.py:637
  313.2 5.9 %maximum_select_fusion = bf16[4,768,768]{2,1,0:T(8,128)(2,1)} fusion(bf16[4,384,768]{2,1,0:T(8,128)(2,1)} %bitcast.47, bf16[4,384,768]{2,1,0:T(8,128)(2,1)S(1)} %maximum_select_fusion.2, pred[]{:T(512)S(6)} %eq.72), kind=kLoop, calls=%fused_computation | loop fusion | flops 21233664 | bytes 9437185 | tf_op jit(solution)/shard_map/jit(_where)/select_n | solution.py:625
  319.1 2.2 maximum_select_fusion.1
  321.9 3.8 %collective-permute-start.10 = (bf16[256,768]{1,0:T(8,128)(2,1)}, bf16[256,768]{1,0:T(8,128)(2,1)S(1)}, u32[]{:S(2)}, u32[]{:S(2)}) collective-permute-start(bf16[256,768]{1,0:T(8,128)(2,1)} %get-tuple-element.141), channel_id=1, source_target_pairs={{0,24},{8,16},{16,8},{1,25},{9,17},{17,9},{2,26},{10,18},{18,10},{... | collective-permute-start | bytes 1179656 | tf_op jit(solution)/shard_map/ppermute | solution.py:765
  325.7 1.9 collective-permute-start.11
  327.6 2.1 collective-permute-start.12
  329.8 5.7 %collective-permute-done.10 = bf16[256,768]{1,0:T(8,128)(2,1)S(1)} collective-permute-done((bf16[256,768]{1,0:T(8,128)(2,1)}, bf16[256,768]{1,0:T(8,128)(2,1)S(1)}, u32[]{:S(2)}, u32[]{:S(2)}) %collective-permute-start.10) | collective-permute-done | bytes 393248 | tf_op jit(solution)/shard_map/ppermute | solution.py:765
  335.5 6.9 %collective-permute-done.11 = bf16[256,768]{1,0:T(8,128)(2,1)S(1)} collective-permute-done((bf16[256,768]{1,0:T(8,128)(2,1)}, bf16[256,768]{1,0:T(8,128)(2,1)S(1)}, u32[]{:S(2)}, u32[]{:S(2)}) %collective-permute-start.11) | collective-permute-done | bytes 393248 | tf_op jit(solution)/shard_map/ppermute | solution.py:765
  342.4 1.0 collective-permute-done.12
  343.3 1.1 select_select_fusion.2
  347.6 2.0 broadcast_select_fusion.3
  349.6 1.8 slice_convert_fusion
  351.4 3.2 maximum_convert_fusion.2
  354.6 4.4 %broadcast_select_fusion.1 = (bf16[3072,768]{1,0:T(8,128)(2,1)S(1)}, bf16[3072,768]{1,0:T(8,128)(2,1)S(1)}) fusion(bf16[3072,768]{1,0:T(8,128)(2,1)} %collective-permute-done.30, pred[]{:T(512)S(6)} %eq.59, bf16[4,768,768]{2,1,0:T(8,128)(2,1)} %maximum_select_fusion), kind=kLoop, calls=%fused_computation.4 | loop fusion | flops 4718592 | bytes 18874368 | tf_op jit(solution)/shard_map/jit(_where)/select_n | solution.py:793
  359.6 4.5 %maximum_convert_fusion.1 = f32[3072,768]{1,0:T(8,128)} fusion(bf16[1536,768]{1,0:T(8,128)(2,1)S(1)} %slice.150, bf16[1536,768]{1,0:T(8,128)(2,1)S(1)} %slice.149), kind=kLoop, calls=%fused_computation.2 | loop fusion | flops 9437184 | bytes 14155776 | tf_op jit(solution)/shard_map/convert_element_type | solution.py:794
  364.1 4.3 %maximum_convert_fusion = f32[768,3072]{1,0:T(8,128)} fusion(bf16[768,768]{1,0:T(8,128)(2,1)S(1)} %get-tuple-element.248, bf16[768,768]{1,0:T(8,128)(2,1)S(1)} %get-tuple-element.249, bf16[768,768]{1,0:T(8,128)(2,1)S(1)} %get-tuple-element.218, bf16[768,768]{1,0:T(8,128)(2,1)S(1)} %get-tuple-element.217), kind=kLoop, calls=%fused_computation.1 | loop fusion | flops 18874368 | bytes 14155776 | tf_op jit(solution)/shard_map/convert_element_type | solution.py:795
  (106 shorter events, 19.5 us)
Async XLA Ops:
  0.6 21.6 %copy-start.27 = (s32[3]{0:T(128)S(1)}, s32[3]{0:T(128)}, u32[]{:S(2)}) copy-start(s32[3]{0:T(128)} %param.17) | copy-start | bytes 40
  0.7 22.2 %copy-start.16 = (f32[768]{0:T(1024)S(1)}, f32[768]{0:T(1024)}, u32[]{:S(2)}) copy-start(f32[768]{0:T(1024)} %param.23) | copy-start | bytes 9220
  0.7 22.8 %copy-start.17 = (f32[768]{0:T(1024)S(1)}, f32[768]{0:T(1024)}, u32[]{:S(2)}) copy-start(f32[768]{0:T(1024)} %param.24) | copy-start | bytes 9220
  0.7 23.4 %copy-start.18 = (f32[768]{0:T(1024)S(1)}, f32[768]{0:T(1024)}, u32[]{:S(2)}) copy-start(f32[768]{0:T(1024)} %param.19) | copy-start | bytes 9220
  0.7 23.9 %copy-start.19 = (f32[768]{0:T(1024)S(1)}, f32[768]{0:T(1024)}, u32[]{:S(2)}) copy-start(f32[768]{0:T(1024)} %param.20) | copy-start | bytes 9220
  0.7 24.5 %copy-start.20 = (f32[768]{0:T(1024)S(1)}, f32[768]{0:T(1024)}, u32[]{:S(2)}) copy-start(f32[768]{0:T(1024)} %param.22) | copy-start | bytes 9220
  0.7 25.1 %copy-start.21 = (f32[768]{0:T(1024)S(1)}, f32[768]{0:T(1024)}, u32[]{:S(2)}) copy-start(f32[768]{0:T(1024)} %param.28) | copy-start | bytes 9220
  0.7 25.6 %copy-start.22 = (f32[768]{0:T(1024)S(1)}, f32[768]{0:T(1024)}, u32[]{:S(2)}) copy-start(f32[768]{0:T(1024)} %param.29) | copy-start | bytes 9220
  0.7 26.2 %copy-start.23 = (f32[768]{0:T(1024)S(1)}, f32[768]{0:T(1024)}, u32[]{:S(2)}) copy-start(f32[768]{0:T(1024)} %param.30) | copy-start | bytes 9220
  2.7 26.1 %collective-permute-start.2 = (bf16[128,768]{1,0:T(8,128)(2,1)S(1)}, bf16[128,768]{1,0:T(8,128)(2,1)S(1)}, u32[]{:S(2)}, u32[]{:S(2)}) collective-permute-start(bf16[128,768]{1,0:T(8,128)(2,1)S(1)} %get-tuple-element.234), channel_id=1, source_target_pairs={{8,16},{16,8},{24,0},{9,17},{17,9},{25,1},{10,18},{18,10},{26,2},{... | collective-permute-start | bytes 589832 | tf_op jit(solution)/shard_map/ppermute | solution.py:705
  4.0 26.7 %collective-permute-start = (bf16[128,768]{1,0:T(8,128)(2,1)S(1)}, bf16[128,768]{1,0:T(8,128)(2,1)S(1)}, u32[]{:S(2)}, u32[]{:S(2)}) collective-permute-start(bf16[128,768]{1,0:T(8,128)(2,1)S(1)} %get-tuple-element.235), channel_id=1, source_target_pairs={{0,8},{8,0},{24,16},{1,9},{9,1},{25,17},{2,10},{10,2},{26,18},{3,1... | collective-permute-start | bytes 589832 | tf_op jit(solution)/shard_map/ppermute | solution.py:705
  11.0 19.8 %collective-permute-start.1 = (bf16[128,768]{1,0:T(8,128)(2,1)S(1)}, bf16[128,768]{1,0:T(8,128)(2,1)S(1)}, u32[]{:S(2)}, u32[]{:S(2)}) collective-permute-start(bf16[128,768]{1,0:T(8,128)(2,1)S(1)} %get-tuple-element.237), channel_id=1, source_target_pairs={{0,16},{16,0},{24,8},{1,17},{17,1},{25,9},{2,18},{18,2},{26,10},{3... | collective-permute-start | bytes 589832 | tf_op jit(solution)/shard_map/ppermute | solution.py:705
  14.9 33.3 %collective-permute-start.6 = (bf16[128,768]{1,0:T(8,128)(2,1)S(1)}, bf16[128,768]{1,0:T(8,128)(2,1)S(1)}, u32[]{:S(2)}, u32[]{:S(2)}) collective-permute-start(bf16[128,768]{1,0:T(8,128)(2,1)S(1)} %get-tuple-element.230), channel_id=1, source_target_pairs={{8,16},{16,8},{24,0},{9,17},{17,9},{25,1},{10,18},{18,10},{26,2},{... | collective-permute-start | bytes 589832 | tf_op jit(solution)/shard_map/ppermute | solution.py:705
  16.2 32.0 %collective-permute-start.4 = (bf16[128,768]{1,0:T(8,128)(2,1)S(1)}, bf16[128,768]{1,0:T(8,128)(2,1)S(1)}, u32[]{:S(2)}, u32[]{:S(2)}) collective-permute-start(bf16[128,768]{1,0:T(8,128)(2,1)S(1)} %get-tuple-element.231), channel_id=1, source_target_pairs={{0,8},{8,0},{24,16},{1,9},{9,1},{25,17},{2,10},{10,2},{26,18},{3,1... | collective-permute-start | bytes 589832 | tf_op jit(solution)/shard_map/ppermute | solution.py:705
  28.8 2.0 copy-start.12
  28.8 19.4 %collective-permute-start.5 = (bf16[128,768]{1,0:T(8,128)(2,1)S(1)}, bf16[128,768]{1,0:T(8,128)(2,1)S(1)}, u32[]{:S(2)}, u32[]{:S(2)}) collective-permute-start(bf16[128,768]{1,0:T(8,128)(2,1)S(1)} %get-tuple-element.233), channel_id=1, source_target_pairs={{0,16},{16,0},{24,8},{1,17},{17,1},{25,9},{2,18},{18,2},{26,10},{3... | collective-permute-start | bytes 589832 | tf_op jit(solution)/shard_map/ppermute | solution.py:705
  30.8 0.7 copy-start.13
  30.8 0.7 copy-start.14
  48.2 0.7 copy-start.24
  48.2 0.7 copy-start.25
  48.2 0.8 copy-start.26
  49.0 17.5 %copy-start = (bf16[512,2304]{1,0:T(8,128)(2,1)S(1)}, bf16[512,2304]{1,0:T(8,128)(2,1)}, u32[]{:S(2)}) copy-start(bf16[512,2304]{1,0:T(8,128)(2,1)} %get-tuple-element.111.low.la.hid.ctx) | copy-start | bytes 7077892
  66.4 18.3 %collective-permute-start.8 = (bf16[512,2304]{1,0:T(8,128)(2,1)}, bf16[512,2304]{1,0:T(8,128)(2,1)}, u32[]{:S(2)}, u32[]{:S(2)}) collective-permute-start(bf16[512,2304]{1,0:T(8,128)(2,1)} %get-tuple-element.113.dffn.ra), channel_id=1, source_target_pairs={{0,1},{1,0},{2,3},{3,2},{4,5},{5,4},{6,7},{7,6},{8,9},{9,8},{10,11... | collective-permute-start | bytes 7077896 | tf_op jit(solution)/shard_map/ppermute | solution.py:618
  66.5 25.6 %collective-permute-start.3 = (bf16[512,2304]{1,0:T(8,128)(2,1)S(1)}, bf16[512,2304]{1,0:T(8,128)(2,1)}, u32[]{:S(2)}, u32[]{:S(2)}) collective-permute-start(bf16[512,2304]{1,0:T(8,128)(2,1)S(1)} %copy-done), channel_id=1, source_target_pairs={{0,1},{1,0},{2,3},{3,2},{4,5},{5,4},{6,7},{7,6},{8,9},{9,8},{10,11... | collective-permute-start | bytes 7077896 | tf_op jit(solution)/shard_map/ppermute | solution.py:618
  84.5 7.6 %collective-permute-start.7 = (bf16[512,1536]{1,0:T(8,128)(2,1)}, bf16[512,1536]{1,0:T(8,128)(2,1)S(1)}, u32[]{:S(2)}, u32[]{:S(2)}) collective-permute-start(bf16[512,1536]{1,0:T(8,128)(2,1)} %get-tuple-element.118), channel_id=1, source_target_pairs={{0,1},{1,0},{2,3},{3,2},{4,5},{5,4},{6,7},{7,6},{8,9},{9,8},{10,11... | collective-permute-start | bytes 4718600 | tf_op jit(solution)/shard_map/ppermute | solution.py:618
  92.1 1.1 copy-start.4
  101.1 39.9 %collective-permute-start.9 = (bf16[1536,768]{1,0:T(8,128)(2,1)}, bf16[1536,768]{1,0:T(8,128)(2,1)S(1)}, u32[]{:S(2)}, u32[]{:S(2)}) collective-permute-start(bf16[1536,768]{1,0:T(8,128)(2,1)} %get-tuple-element.123), channel_id=1, source_target_pairs={{0,8},{1,17},{2,10},{3,19},{4,12},{5,21},{6,14},{7,23},{8,0},{9,25... | collective-permute-start | bytes 7077896 | tf_op jit(solution)/shard_map/ppermute | solution.py:637
  123.5 5.6 %collective-permute-start.13 = (bf16[1056,768]{1,0:T(8,128)(2,1)}, bf16[1056,768]{1,0:T(8,128)(2,1)S(1)}, u32[]{:S(2)}, u32[]{:S(2)}) collective-permute-start(bf16[1056,768]{1,0:T(8,128)(2,1)} %get-tuple-element.148), channel_id=1, source_target_pairs={{0,1},{1,0},{2,3},{3,2},{4,5},{5,4},{6,7},{7,6},{8,9},{9,8},{10,11... | collective-permute-start | bytes 4866056 | tf_op jit(solution)/shard_map/ppermute | solution.py:618
  129.1 1.2 copy-start.3
  139.3 25.1 %collective-permute-start.14 = (bf16[800,768]{1,0:T(8,128)(2,1)}, bf16[800,768]{1,0:T(8,128)(2,1)S(1)}, u32[]{:S(2)}, u32[]{:S(2)}) collective-permute-start(bf16[800,768]{1,0:T(8,128)(2,1)} %get-tuple-element.151), channel_id=1, source_target_pairs={{0,2},{1,9},{2,0},{3,11},{4,6},{5,13},{6,4},{7,15},{8,10},{9,1},{1... | collective-permute-start | bytes 3686408 | tf_op jit(solution)/shard_map/ppermute | solution.py:637
  141.0 1.4 copy-start.2
  146.6 21.7 %collective-permute-start.23 = (bf16[768,768]{1,0:T(8,128)(2,1)}, bf16[768,768]{1,0:T(8,128)(2,1)S(1)}, u32[]{:S(2)}, u32[]{:S(2)}) collective-permute-start(bf16[768,768]{1,0:T(8,128)(2,1)} %get-tuple-element.184), channel_id=1, source_target_pairs={{0,16},{1,3},{2,18},{3,1},{4,20},{5,7},{6,22},{7,5},{8,24},{9,11},... | collective-permute-start | bytes 3538952 | tf_op jit(solution)/shard_map/ppermute | solution.py:637
  164.4 1.0 copy-start.5
  168.3 14.1 %collective-permute-start.15 = (bf16[416,768]{1,0:T(8,128)(2,1)}, bf16[416,768]{1,0:T(8,128)(2,1)S(1)}, u32[]{:S(2)}, u32[]{:S(2)}) collective-permute-start(bf16[416,768]{1,0:T(8,128)(2,1)} %get-tuple-element.157), channel_id=1, source_target_pairs={{0,8},{1,3},{2,10},{3,1},{4,12},{5,7},{6,14},{7,5},{8,0},{9,11},{1... | collective-permute-start | bytes 1916936 | tf_op jit(solution)/shard_map/ppermute | solution.py:637
  168.3 1.0 copy-start.6
  172.2 13.5 %collective-permute-start.24 = (bf16[384,768]{1,0:T(8,128)(2,1)}, bf16[384,768]{1,0:T(8,128)(2,1)S(1)}, u32[]{:S(2)}, u32[]{:S(2)}) collective-permute-start(bf16[384,768]{1,0:T(8,128)(2,1)} %get-tuple-element.188), channel_id=1, source_target_pairs={{0,2},{1,9},{2,0},{3,11},{4,6},{5,13},{6,4},{7,15},{8,10},{9,1},{1... | collective-permute-start | bytes 1769480 | tf_op jit(solution)/shard_map/ppermute | solution.py:637
  182.4 0.8 copy-start.7
  185.4 7.5 %collective-permute-start.16 = (bf16[224,768]{1,0:T(8,128)(2,1)}, bf16[224,768]{1,0:T(8,128)(2,1)S(1)}, u32[]{:S(2)}, u32[]{:S(2)}) collective-permute-start(bf16[224,768]{1,0:T(8,128)(2,1)} %get-tuple-element.163), channel_id=1, source_target_pairs={{0,16},{1,17},{2,18},{3,19},{4,20},{5,21},{6,22},{7,23},{8,24},{9,... | collective-permute-start | bytes 1032200 | tf_op jit(solution)/shard_map/ppermute | solution.py:637
  185.8 0.8 copy-start.8
  188.8 26.5 %collective-permute-start.25 = (bf16[192,768]{1,0:T(8,128)(2,1)}, bf16[192,768]{1,0:T(8,128)(2,1)S(1)}, u32[]{:S(2)}, u32[]{:S(2)}) collective-permute-start(bf16[192,768]{1,0:T(8,128)(2,1)} %get-tuple-element.192), channel_id=1, source_target_pairs={{0,4},{1,5},{2,6},{3,7},{4,0},{5,1},{6,2},{7,3},{8,12},{9,13},{10,... | collective-permute-start | bytes 884744 | tf_op jit(solution)/shard_map/ppermute | solution.py:637
  192.9 0.7 copy-start.9
  195.5 17.4 %collective-permute-start.17 = (bf16[128,768]{1,0:T(8,128)(2,1)}, bf16[128,768]{1,0:T(8,128)(2,1)S(1)}, u32[]{:S(2)}, u32[]{:S(2)}) collective-permute-start(bf16[128,768]{1,0:T(8,128)(2,1)} %get-tuple-element.169), channel_id=1, source_target_pairs={{0,4},{1,5},{2,6},{3,7},{4,0},{5,1},{6,2},{7,3},{8,12},{9,13},{10,... | collective-permute-start | bytes 589832 | tf_op jit(solution)/shard_map/ppermute | solution.py:637
  212.9 0.7 copy-start.11
  215.3 0.7 copy-start.10
  217.8 22.7 %collective-permute-start.26 = (bf16[192,768]{1,0:T(8,128)(2,1)}, bf16[192,768]{1,0:T(8,128)(2,1)S(1)}, u32[]{:S(2)}, u32[]{:S(2)}) collective-permute-start(bf16[192,768]{1,0:T(8,128)(2,1)} %fold.15), channel_id=1, source_target_pairs={{0,4},{1,5},{2,6},{3,7},{4,0},{5,1},{6,2},{7,3},{8,12},{9,13},{10,... | collective-permute-start | bytes 884744 | tf_op jit(solution)/shard_map/ppermute | solution.py:637
  217.8 21.7 %collective-permute-start.18 = (bf16[96,768]{1,0:T(8,128)(2,1)}, bf16[96,768]{1,0:T(8,128)(2,1)S(1)}, u32[]{:S(2)}, u32[]{:S(2)}) collective-permute-start(bf16[96,768]{1,0:T(8,128)(2,1)} %get-tuple-element.175), channel_id=1, source_target_pairs={{0,4},{1,5},{2,6},{3,7},{4,0},{5,1},{6,2},{7,3},{8,12},{9,13},{10,... | collective-permute-start | bytes 442376 | tf_op jit(solution)/shard_map/ppermute | solution.py:637
  241.8 9.9 %collective-permute-start.27 = (bf16[384,768]{1,0:T(8,128)(2,1)S(1)}, bf16[384,768]{1,0:T(8,128)(2,1)S(1)}, u32[]{:S(2)}, u32[]{:S(2)}) collective-permute-start(bf16[384,768]{1,0:T(8,128)(2,1)S(1)} %bitcast.71), channel_id=1, source_target_pairs={{0,2},{1,9},{2,0},{3,11},{4,6},{5,13},{6,4},{7,15},{8,10},{9,1},{1... | collective-permute-start | bytes 1769480 | tf_op jit(solution)/shard_map/ppermute | solution.py:637
  241.9 7.5 %collective-permute-start.19 = (bf16[192,768]{1,0:T(8,128)(2,1)S(1)}, bf16[192,768]{1,0:T(8,128)(2,1)S(1)}, u32[]{:S(2)}, u32[]{:S(2)}) collective-permute-start(bf16[192,768]{1,0:T(8,128)(2,1)S(1)} %bitcast.74), channel_id=1, source_target_pairs={{0,16},{1,17},{2,18},{3,19},{4,20},{5,21},{6,22},{7,23},{8,24},{9,... | collective-permute-start | bytes 884744 | tf_op jit(solution)/shard_map/ppermute | solution.py:637
  252.2 16.4 %copy-start.1 = (bf16[4,192,768]{2,1,0:T(8,128)(2,1)}, bf16[4,192,768]{2,1,0:T(8,128)(2,1)S(1)}, u32[]{:S(2)}) copy-start(bf16[4,192,768]{2,1,0:T(8,128)(2,1)S(1)} %maximum_select_fusion.4) | copy-start | bytes 3538948
  252.2 16.4 %collective-permute-start.28 = (bf16[768,768]{1,0:T(8,128)(2,1)S(1)}, bf16[768,768]{1,0:T(8,128)(2,1)}, u32[]{:S(2)}, u32[]{:S(2)}) collective-permute-start(bf16[768,768]{1,0:T(8,128)(2,1)S(1)} %bitcast.70), channel_id=1, source_target_pairs={{0,16},{1,3},{2,18},{3,1},{4,20},{5,7},{6,22},{7,5},{8,24},{9,11},... | collective-permute-start | bytes 3538952 | tf_op jit(solution)/shard_map/ppermute | solution.py:637
  252.7 9.9 %collective-permute-start.20 = (bf16[384,768]{1,0:T(8,128)(2,1)S(1)}, bf16[384,768]{1,0:T(8,128)(2,1)S(1)}, u32[]{:S(2)}, u32[]{:S(2)}) collective-permute-start(bf16[384,768]{1,0:T(8,128)(2,1)S(1)} %bitcast.72), channel_id=1, source_target_pairs={{0,8},{1,3},{2,10},{3,1},{4,12},{5,7},{6,14},{7,5},{8,0},{9,11},{1... | collective-permute-start | bytes 1769480 | tf_op jit(solution)/shard_map/ppermute | solution.py:637
  271.6 41.7 %collective-permute-start.29 = (bf16[1536,768]{1,0:T(8,128)(2,1)S(1)}, bf16[1536,768]{1,0:T(8,128)(2,1)}, u32[]{:S(2)}, u32[]{:S(2)}) collective-permute-start(bf16[1536,768]{1,0:T(8,128)(2,1)S(1)} %bitcast.68), channel_id=1, source_target_pairs={{0,8},{1,17},{2,10},{3,19},{4,12},{5,21},{6,14},{7,23},{8,0},{9,25... | collective-permute-start | bytes 7077896 | tf_op jit(solution)/shard_map/ppermute | solution.py:637
  272.0 47.1 %collective-permute-start.21 = (bf16[768,768]{1,0:T(8,128)(2,1)S(1)}, bf16[768,768]{1,0:T(8,128)(2,1)}, u32[]{:S(2)}, u32[]{:S(2)}) collective-permute-start(bf16[768,768]{1,0:T(8,128)(2,1)S(1)} %bitcast.69), channel_id=1, source_target_pairs={{0,2},{1,9},{2,0},{3,11},{4,6},{5,13},{6,4},{7,15},{8,10},{9,1},{1... | collective-permute-start | bytes 3538952 | tf_op jit(solution)/shard_map/ppermute | solution.py:637
  319.1 35.5 %collective-permute-start.30 = (bf16[3072,768]{1,0:T(8,128)(2,1)}, bf16[3072,768]{1,0:T(8,128)(2,1)}, u32[]{:S(2)}, u32[]{:S(2)}) collective-permute-start(bf16[3072,768]{1,0:T(8,128)(2,1)} %bitcast.48), channel_id=1, source_target_pairs={{0,1},{1,0},{2,3},{3,2},{4,5},{5,4},{6,7},{7,6},{8,9},{9,8},{10,11... | collective-permute-start | bytes 14155784 | tf_op jit(solution)/shard_map/ppermute | solution.py:618
  321.3 26.3 %collective-permute-start.22 = (bf16[1536,768]{1,0:T(8,128)(2,1)S(1)}, bf16[1536,768]{1,0:T(8,128)(2,1)}, u32[]{:S(2)}, u32[]{:S(2)}) collective-permute-start(bf16[1536,768]{1,0:T(8,128)(2,1)S(1)} %bitcast.67), channel_id=1, source_target_pairs={{0,1},{1,0},{2,3},{3,2},{4,5},{5,4},{6,7},{7,6},{8,9},{9,8},{10,11... | collective-permute-start | bytes 7077896 | tf_op jit(solution)/shard_map/ppermute | solution.py:618
  321.9 13.6 %collective-permute-start.10 = (bf16[256,768]{1,0:T(8,128)(2,1)}, bf16[256,768]{1,0:T(8,128)(2,1)S(1)}, u32[]{:S(2)}, u32[]{:S(2)}) collective-permute-start(bf16[256,768]{1,0:T(8,128)(2,1)} %get-tuple-element.141), channel_id=1, source_target_pairs={{0,24},{8,16},{16,8},{1,25},{9,17},{17,9},{2,26},{10,18},{18,10},{... | collective-permute-start | bytes 1179656 | tf_op jit(solution)/shard_map/ppermute | solution.py:765
  325.7 16.7 %collective-permute-start.11 = (bf16[256,768]{1,0:T(8,128)(2,1)}, bf16[256,768]{1,0:T(8,128)(2,1)S(1)}, u32[]{:S(2)}, u32[]{:S(2)}) collective-permute-start(bf16[256,768]{1,0:T(8,128)(2,1)} %get-tuple-element.142), channel_id=1, source_target_pairs={{0,16},{8,24},{16,0},{1,17},{9,25},{17,1},{2,18},{10,26},{18,2},{3... | collective-permute-start | bytes 1179656 | tf_op jit(solution)/shard_map/ppermute | solution.py:765
  327.6 15.7 %collective-permute-start.12 = (bf16[256,768]{1,0:T(8,128)(2,1)}, bf16[256,768]{1,0:T(8,128)(2,1)S(1)}, u32[]{:S(2)}, u32[]{:S(2)}) collective-permute-start(bf16[256,768]{1,0:T(8,128)(2,1)} %get-tuple-element.143), channel_id=1, source_target_pairs={{0,8},{8,0},{16,24},{1,9},{9,1},{17,25},{2,10},{10,2},{18,26},{3,1... | collective-permute-start | bytes 1179656 | tf_op jit(solution)/shard_map/ppermute | solution.py:765
  344.5 1.9 copy-start.15

commit v3 on v0

v3 whole, which is shorter than its diff:
```python
import functools
import math

import jax
import jax.numpy as jnp
from jax import lax
from jax.experimental import pallas as pl
from jax.experimental.pallas import tpu as pltpu
from jax.sharding import PartitionSpec as P

HEADS = 12
EPS = 1e-12
BF = jnp.bfloat16
F32 = jnp.float32
VMEM_LIMIT = 60 * 1024 * 1024
LOG2E = math.log2(math.e)
S_SEQ, S_LEN, S_CORE, S_BITS = range(4)
ORDER = ((0, 1, 2), (1, 2, 0), (2, 0, 1))
COLORS = 3
LEAF = 16


def dot_nn(left, right):
    return lax.dot_general(left, right, (((1,), (0,)), ((), ())), preferred_element_type=F32)


def dot_nt(left, right):
    return lax.dot_general(left, right, (((1,), (1,)), ((), ())), preferred_element_type=F32)


def dot_tn(left, right):
    return lax.dot_general(left, right, (((0,), (0,)), ((), ())), preferred_element_type=F32)


def params(flag=None):
    return pltpu.CompilerParams(vmem_limit_bytes=VMEM_LIMIT)


def cost(flops, nbytes, trans=0):
    return pl.CostEstimate(flops=int(flops), bytes_accessed=int(nbytes), transcendentals=int(trans))


def full(shape):
    zeros = (0,) * len(shape)
    return pl.BlockSpec(shape, lambda *_: zeros)


def shape_of(shape, dtype):
    return jax.ShapeDtypeStruct(shape, dtype)


def attn_fwd_body(sc, h0, h1, h2, h3, wq, wk, wv, qb, vb, wo, ob, gain, shift,
                  hlc, q_o, k_o, v_o, lse_o, n1_o, r1_o, acc, lse_s):
    step = pl.program_id(0)
    steps = pl.num_programs(0)
    local, width = h0.shape
    rows = hlc.shape[0]
    head = wq.shape[1] // 2
    wide = 2 * head

    @pl.when(step == 0)
    def _():
        for at, ref in enumerate((h0, h1, h2, h3)):
            hlc[at * local:(at + 1) * local, width:2 * width] = ref[...]
        acc[...] = jnp.zeros_like(acc)
        lse_s[...] = jnp.zeros_like(lse_s)

    x = hlc[:, width:2 * width]
    w = jnp.concatenate([wq[...], wk[...], wv[...]], axis=1)
    both = dot_nn(x, w)
    q_o[...] = (both[:, :wide] + qb[...]).astype(BF)
    k_o[...] = both[:, wide:2 * wide].astype(BF)
    v_o[...] = (both[:, 2 * wide:] + vb[...]).astype(BF)
    k = k_o[...]
    v = v_o[...]
    key = lax.broadcasted_iota(jnp.int32, (1, rows), 1)
    place = ((key // local) ^ sc[S_SEQ]) * local + key % local
    mask = jnp.where(place < sc[S_LEN], 0.0, -1e30).astype(F32)
    scale = head ** (-0.5) * LOG2E
    chunk = rows
    lane = lax.broadcasted_iota(jnp.int32, (chunk, wide), 1)
    lane_l = lax.broadcasted_iota(jnp.int32, (chunk, lse_s.shape[1]), 1)
    for part in range(rows // chunk):
        span = pl.ds(part * chunk, chunk)
        q = q_o[span, :]
        outs = []
        tops = []
        for h in range(2):
            mine = (lane >= h * head) & (lane < (h + 1) * head)
            qh = jnp.where(mine, q, jnp.zeros_like(q))
            s = dot_nt(qh, k) * scale + mask
            top = jnp.max(s, -1, keepdims=True)
            e = jnp.exp2(s - top)
            total = jnp.sum(e, -1, keepdims=True)
            pv = dot_nn(e.astype(BF), v)
            outs.append(pv / total)
            tops.append(top + jnp.log2(total))
        ctx = jnp.where(lane < head, outs[0], outs[1]).astype(BF)
        hlc[span, pl.ds(pl.multiple_of(2 * width + step * wide, wide), wide)] = ctx
        acc[span, :] += dot_nn(ctx, wo[...])
        old = lse_s[span, :]
        old = jnp.where(lane_l == 2 * step, tops[0], old)
        lse_s[span, :] = jnp.where(lane_l == 2 * step + 1, tops[1], old)

    @pl.when(step == steps - 1)
    def _():
        lse_o[...] = jnp.transpose(lse_s[...])[:lse_o.shape[0], :]

        @pl.loop(0, rows // local)
        def _(part):
            span = pl.ds(pl.multiple_of(part * local, local), local)
            val = hlc[span, width:2 * width].astype(F32) + (acc[span, :] + ob[...])
            cen = val - jnp.mean(val, -1, keepdims=True)
            r = lax.rsqrt(jnp.mean(cen * cen, -1, keepdims=True) + EPS)
            n = cen * r
            n1_o[span, :] = n
            r1_o[span, :] = jnp.broadcast_to(r, (local, r1_o.shape[1]))
            hlc[span, :width] = (n * gain[...] + shift[...]).astype(BF)


def attn_fwd(sc, blocks, qkv_w, qb, vb, out_w, ob, gain, shift):
    local, width = blocks[0].shape
    rows = local * len(blocks)
    pairs = HEADS // 2
    wide = width // pairs
    row = lambda i, s: (0, i)
    grid = pltpu.PrefetchScalarGridSpec(
        num_scalar_prefetch=1,
        grid=(pairs,),
        in_specs=[full((local, width))] * 4 + [
            pl.BlockSpec((width, wide), lambda i, s: (0, i)),
            pl.BlockSpec((width, wide), lambda i, s: (0, pairs + i)),
            pl.BlockSpec((width, wide), lambda i, s: (0, 2 * pairs + i)),
            pl.BlockSpec((1, wide), row),
            pl.BlockSpec((1, wide), row),
            pl.BlockSpec((wide, width), lambda i, s: (i, 0)),
            full((1, width)), full((1, width)), full((1, width)),
        ],
        out_specs=[
            full((rows, 3 * width)),
            pl.BlockSpec((rows, wide), row),
            pl.BlockSpec((rows, wide), row),
            pl.BlockSpec((rows, wide), row),
            full((16, rows)),
            full((rows, width)),
            full((rows, 128)),
        ],
        scratch_shapes=[pltpu.VMEM((rows, width), F32), pltpu.VMEM((rows, 128), F32)],
    )
    wide_bf = shape_of((rows, width), BF)
    return pl.pallas_call(
        attn_fwd_body,
        grid_spec=grid,
        out_shape=[shape_of((rows, 3 * width), BF), wide_bf, wide_bf, wide_bf, shape_of((16, rows), F32),
                   shape_of((rows, width), F32), shape_of((rows, 128), F32)],
        compiler_params=params(),
        cost_estimate=cost(2 * rows * width * width * 4 + 4 * rows * rows * width, 12 * rows * width + 8 * width * width,
                           HEADS * rows * rows),
        name="attn_fwd",
    )(sc, *blocks, qkv_w, qkv_w, qkv_w, qb, vb, out_w, ob, gain, shift)


def start(copies):
    for copy in copies:
        copy.start()


def wait(copies):
    for copy in copies:
        copy.wait()


def ffn_body(sc, hlc, n1_h, wu_h, wd_h, wo_h, r1, c0, c1, c2, c3, gain1, shift1, ub, db, gain2, shift2,
             act_o, send_o, dup_o, dsend_o, lo_o, dres_o, dattn_o, dctx_o, stat_o,
             low, n1, wu, wd, wo, act, slope, acc, dsec, dffn, dup, sem_in, sem_w, sem_out):
    local, width = c0.shape
    rows, inner = act.shape
    tile = width
    steps = inner // tile
    side = inner // 2
    core = sc[S_CORE]
    mine = pl.ds(pl.multiple_of(core * side, side), side)
    theirs = pl.ds(pl.multiple_of((1 - core) * side, side), side)

    def cols(j):
        return pl.ds(pl.multiple_of(j * tile, tile), tile)

    def wu_copy(j):
        return pltpu.make_async_copy(wu_h.at[:, cols(j)], wu.at[:, cols(j)], sem_w.at[0, j])

    def wd_copy(j):
        return pltpu.make_async_copy(wd_h.at[cols(j), :], wd.at[cols(j), :], sem_w.at[1, j])

    low_copy = pltpu.make_async_copy(hlc.at[:, pl.ds(0, width)], low, sem_in.at[0])
    n1_copy = pltpu.make_async_copy(n1_h, n1, sem_in.at[1])
    wo_copy = pltpu.make_async_copy(wo_h, wo, sem_in.at[2])
    low_copy.start()
    for j in range(steps):
        wu_copy(j).start()
        wd_copy(j).start()
    start([n1_copy, wo_copy])
    low_copy.wait()
    stat_o[...] = jnp.zeros_like(stat_o)

    def forward(j, _):
        wu_copy(j).wait()
        wd_copy(j).wait()
        up = dot_nn(low[...], wu[:, cols(j)]) + ub[:, cols(j)]
        cdf = 0.5 * (1.0 + lax.erf(up * (2.0 ** -0.5)))
        bell = jnp.exp2(up * up * (-0.5 * LOG2E)) * ((2.0 * math.pi) ** -0.5)
        val = (up * cdf).astype(BF)
        act[:, cols(j)] = val
        slope[:, cols(j)] = (cdf + up * bell).astype(BF)
        term = dot_nn(val, wd[cols(j), :])

        @pl.when(j == 0)
        def _():
            acc[...] = term

        @pl.when(j > 0)
        def _():
            acc[...] += term
        return 0

    lax.fori_loop(0, steps, forward, 0)
    act_out = [pltpu.make_async_copy(act.at[:, mine], act_o, sem_out.at[0]),
               pltpu.make_async_copy(act.at[:, theirs], send_o.at[:, pl.ds(0, side)], sem_out.at[1])]
    start(act_out)
    n1_copy.wait()
    for at, cot in enumerate((c0, c1, c2, c3)):
        span = pl.ds(at * local, local)
        first = n1[span, :] * gain1[...] + shift1[...]
        val = first + (acc[span, :] + db[...])
        cen = val - jnp.mean(val, -1, keepdims=True)
        r = lax.rsqrt(jnp.mean(cen * cen, -1, keepdims=True) + EPS)
        n = cen * r
        lo_o[span, :] = (n * gain2[...] + shift2[...]).astype(BF)
        dy = cot[...].astype(F32)
        dn = dy * gain2[...]
        ds = r * (dn - jnp.mean(dn, -1, keepdims=True) - n * jnp.mean(dn * n, -1, keepdims=True))
        dsec[span, :] = ds
        dlow = ds.astype(BF)
        dffn[span, :] = dlow
        stat_o[0:1, :] += jnp.sum(dy * n, 0, keepdims=True)
        stat_o[1:2, :] += jnp.sum(dy, 0, keepdims=True)
        stat_o[2:3, :] += jnp.sum(dlow.astype(F32), 0, keepdims=True)
    dffn_out = pltpu.make_async_copy(dffn, send_o.at[:, pl.ds(side, width)], sem_out.at[2])
    dffn_out.start()

    def backward(j, _):
        dact = dot_nt(dffn[...], wd[cols(j), :])
        val = (dact * slope[:, cols(j)].astype(F32)).astype(BF)
        dup[:, cols(j)] = val
        stat_o[pl.ds(8 + j, 1), :] = jnp.sum(val.astype(F32), 0, keepdims=True)
        dsec[...] += dot_nt(val, wu[:, cols(j)])
        return 0

    lax.fori_loop(0, steps, backward, 0)
    dup_out = [pltpu.make_async_copy(dup.at[:, mine], dup_o, sem_out.at[3]),
               pltpu.make_async_copy(dup.at[:, theirs], dsend_o, sem_out.at[4])]
    start(dup_out)
    wo_copy.wait()

    @pl.loop(0, rows // local)
    def _(at):
        span = pl.ds(pl.multiple_of(at * local, local), local)
        dfirst = dsec[span, :]
        n = n1[span, :]
        dn = dfirst * gain1[...]
        r = r1[span, 0:1]
        dres = r * (dn - jnp.mean(dn, -1, keepdims=True) - n * jnp.mean(dn * n, -1, keepdims=True))
        dres_o[span, :] = dres
        dlow = dres.astype(BF)
        dattn_o[span, :] = dlow
        stat_o[3:4, :] += jnp.sum(dfirst * n, 0, keepdims=True)
        stat_o[4:5, :] += jnp.sum(dfirst, 0, keepdims=True)
        stat_o[5:6, :] += jnp.sum(dlow.astype(F32), 0, keepdims=True)

    dctx_o[...] = dot_nt(dattn_o[...], wo[...]).astype(BF)
    wait(act_out + [dffn_out] + dup_out)


def ffn(sc, hlc, n1, r1, wu, wd, wo, cots, gain1, shift1, ub, db, gain2, shift2):
    rows, width = n1.shape
    inner = wu.shape[1]
    steps = inner // width
    smem = pl.BlockSpec(memory_space=pltpu.SMEM)
    anywhere = pl.BlockSpec(memory_space=pl.ANY)
    vmem = pl.BlockSpec(memory_space=pltpu.VMEM)
    half = shape_of((rows, inner // 2), BF)
    wide = shape_of((rows, width), BF)
    return pl.pallas_call(
        ffn_body,
        in_specs=[smem] + [anywhere] * 5 + [vmem] * 11,
        out_specs=[anywhere] * 4 + [vmem] * 5,
        out_shape=[half, shape_of((rows, inner // 2 + width), BF), half, half, wide, shape_of((rows, width), F32),
                   wide, wide, shape_of((16, width), F32)],
        scratch_shapes=[pltpu.VMEM((rows, width), BF), pltpu.VMEM((rows, width), F32), pltpu.VMEM((width, inner), BF),
                        pltpu.VMEM((inner, width), BF), pltpu.VMEM((width, width), BF), pltpu.VMEM((rows, inner), BF),
                        pltpu.VMEM((rows, inner), BF), pltpu.VMEM((rows, width), F32), pltpu.VMEM((rows, width), F32),
                        pltpu.VMEM((rows, width), BF), pltpu.VMEM((rows, inner), BF), pltpu.SemaphoreType.DMA((3,)),
                        pltpu.SemaphoreType.DMA((2, steps)), pltpu.SemaphoreType.DMA((5,))],
        compiler_params=params(),
        cost_estimate=cost(8 * rows * width * inner, 4 * width * inner + 6 * rows * inner, 2 * rows * inner),
        name="ffn",
    )(sc, hlc, n1, wu, wd, wo, r1, *cots, gain1, shift1, ub, db, gain2, shift2)


def split_terms(value):
    high = value.astype(BF)
    return high, (value - high.astype(F32)).astype(BF)


def attn_bwd_body(sc, q_r, k_r, v_r, g_r, lse, wq, wk, wv, base, da_r, stat, lo, *refs, first, last):
    if first:
        dq_o, dk_o, dv_o, one_o, two_o, small_o, acc = refs
    else:
        dq_o, dk_o, dv_o, one_o, two_o, small_o, terms_o, i0, i1, i2, i3, acc = refs[5:]
    step = pl.program_id(0)
    steps = pl.num_programs(0)
    rows, wide = q_r.shape
    head = wide // 2
    local = rows // 4
    scale = head ** (-0.5)
    pair = step if first else step + steps
    q = q_r[...]
    g = g_r[...]
    k = k_r[...]
    v = v_r[...]
    lane = lax.broadcasted_iota(jnp.int32, (rows, wide), 1)
    key = lax.broadcasted_iota(jnp.int32, (rows, 1), 0)
    place = ((key // local) ^ sc[S_SEQ]) * local + key % local
    mask = jnp.where(place < sc[S_LEN], 0.0, -1e30).astype(F32)
    dks, dvs, dqs = [], [], []
    for h in range(2):
        mine = (lane >= h * head) & (lane < (h + 1) * head)
        qh = jnp.where(mine, q, jnp.zeros_like(q))
        gh = jnp.where(mine, g, jnp.zeros_like(g))
        row = lse[pl.ds(2 * pair + h, 1), :]
        s = dot_nt(k, qh) * (scale * LOG2E) + mask
        p = jnp.exp2(s - row)
        dp = dot_nt(v, gh)
        delta = jnp.sum(p * dp, 0, keepdims=True)
        dvs.append(dot_nn(p.astype(BF), g))
        ds = (p * (dp - delta)).astype(BF)
        dks.append(dot_nn(ds, q))
        dqs.append(dot_tn(ds, k))
    low = lane < head
    dq_o[...] = (jnp.where(low, dqs[0], dqs[1]) * scale).astype(BF)
    dk_o[...] = (jnp.where(low, dks[0], dks[1]) * scale).astype(BF)
    dv_o[...] = jnp.where(low, dvs[0], dvs[1]).astype(BF)
    dqv = dq_o[...]
    dkv = dk_o[...]
    dvv = dv_o[...]
    here = pl.ds(pl.multiple_of(pair * wide, wide), wide)

    @pl.when(step == 0)
    def _():
        small_o[...] = stat[...]

    small_o[6:7, here] = jnp.sum(dqv.astype(F32), 0, keepdims=True)
    small_o[7:8, here] = jnp.sum(dvv.astype(F32), 0, keepdims=True)

    @pl.when(sc[S_CORE] == 0)
    def _():
        one_o[...] = dv_o[...]
        two_o[...] = da_r[...]

    @pl.when(sc[S_CORE] != 0)
    def _():
        one_o[...] = dq_o[...]
        two_o[...] = dk_o[...]

    three = jnp.concatenate([dqv, dkv, dvv], axis=1)
    w = jnp.concatenate([wq[...], wk[...], wv[...]], axis=1)
    term = dot_nt(three, w)

    @pl.when(step == 0)
    def _():
        acc[...] = base[...] + term

    @pl.when(step > 0)
    def _():
        acc[...] += term

    if last:
        @pl.when(step == steps - 1)
        def _():
            for at, ref in enumerate((i0, i1, i2, i3)):
                ref[0:local, :] = lo[at * local:(at + 1) * local, :]
                ref[local:2 * local, :] = acc[pl.ds(at * local, local), :].astype(BF)
            high, rest = split_terms(small_o[...])
            terms_o[0:16, :] = high
            terms_o[16:32, :] = rest


def attn_bwd(sc, q, k, v, g, lse, qkv_w, base, dattn, stat, lo, into):
    rows, width = q.shape
    pairs = HEADS // 2
    wide = width // pairs
    first = not into
    steps = pairs // 2
    off = 0 if first else steps
    col = pl.BlockSpec((rows, wide), lambda i, s: (0, off + i))
    block = full((2 * (rows // 4), width))
    grid = pltpu.PrefetchScalarGridSpec(
        num_scalar_prefetch=1,
        grid=(steps,),
        in_specs=[col, col, col, col, full(lse.shape),
                  pl.BlockSpec((width, wide), lambda i, s: (0, off + i)),
                  pl.BlockSpec((width, wide), lambda i, s: (0, pairs + off + i)),
                  pl.BlockSpec((width, wide), lambda i, s: (0, 2 * pairs + off + i)),
                  full((rows, width)), col, full((16, width)), full((rows, width))]
        + [pl.BlockSpec(memory_space=pl.ANY)] * len(into),
        out_specs=[col] * 5 + [full((16, width))]
        + ([full((rows, width))] if first else [full((32, width))] + [block] * 4),
        scratch_shapes=[] if first else [pltpu.VMEM((rows, width), F32)],
    )
    wide_bf = shape_of((rows, width), BF)
    outs = [wide_bf] * 5 + [shape_of((16, width), F32)]
    if first:
        outs += [shape_of((rows, width), F32)]
    else:
        outs += [shape_of((32, width), BF)] + [shape_of((rows // 2, width), BF)] * 4
    return pl.pallas_call(
        functools.partial(attn_bwd_body, first=first, last=not first),
        grid_spec=grid,
        out_shape=outs,
        input_output_aliases={13 + i: i for i in range(len(into))},
        compiler_params=params(),
        cost_estimate=cost(3 * rows * width * width + 5 * rows * rows * width, 6 * rows * width + 3 * width * width,
                           HEADS * rows * rows // 2),
        name="attn_bwd",
    )(sc, q, k, v, g, lse, qkv_w, qkv_w, qkv_w, base, dattn, stat, lo, *into)


def cut_out(sc, buf, u, sends, keeps, sems):
    copies = []
    third = buf.shape[1] // COLORS
    half = third // 2
    for c in range(COLORS):
        bit = sc[S_BITS + ORDER[c][0]]
        for at, (ref, pick) in enumerate(((sends[c], 1 - bit), (keeps[c], bit))):
            src = buf.at[u, pl.ds(pl.multiple_of(c * third + pick * half, half), half), :]
            copies.append(pltpu.make_async_copy(src, ref.at[pl.ds(u * half, half), :], sems.at[u, 2 * c + at]))
    start(copies)
    return copies


def wgrad_body(sc, act_h, send_h, peer_h, hlc, hlcp, dup_h, dupp_h, s0, s1, s2, k0, k1, k2,
               act, actp, dffn, low, lowp, dup, dupp, buf, sem_in, sem_out):
    side = act.shape[1]
    width = dffn.shape[1]
    loads = [
        pltpu.make_async_copy(act_h, act, sem_in.at[0]),
        pltpu.make_async_copy(send_h.at[:, pl.ds(side, width)], dffn, sem_in.at[1]),
        pltpu.make_async_copy(peer_h, actp, sem_in.at[2]),
        pltpu.make_async_copy(hlc.at[:, pl.ds(0, width)], low, sem_in.at[3]),
        pltpu.make_async_copy(dup_h, dup, sem_in.at[4]),
        pltpu.make_async_copy(hlcp.at[:, pl.ds(0, width)], lowp, sem_in.at[5]),
        pltpu.make_async_copy(dupp_h, dupp, sem_in.at[6]),
    ]
    start(loads)
    sends, keeps = (s0, s1, s2), (k0, k1, k2)
    copies = []
    wait(loads[:3])
    for u in range(2):
        at = slice(u * width, (u + 1) * width)
        val = dot_tn(act[:, at], dffn[...]) + dot_tn(actp[:, at], actp[:, side:])
        buf[u] = val.astype(BF)
        copies += cut_out(sc, buf, u, sends, keeps, sem_out)
    wait(loads[3:])
    for u in range(2):
        at = slice(u * width, (u + 1) * width)
        val = dot_tn(low[...], dup[:, at]) + dot_tn(lowp[...], dupp[:, at])
        buf[2 + u] = val.astype(BF)
        copies += cut_out(sc, buf, 2 + u, sends, keeps, sem_out)
    wait(copies)


def wgrad(sc, act, send, peer, hlc, hlcp, dup, dupp):
    rows, side = act.shape
    width = hlc.shape[1] // 3
    units = 4
    half = width // COLORS // 2
    anywhere = pl.BlockSpec(memory_space=pl.ANY)
    part = shape_of((units * half, width), BF)
    return pl.pallas_call(
        wgrad_body,
        in_specs=[pl.BlockSpec(memory_space=pltpu.SMEM)] + [anywhere] * 7,
        out_specs=[anywhere] * 6,
        out_shape=[part] * 6,
        scratch_shapes=[pltpu.VMEM((rows, side), BF), pltpu.VMEM((rows, side + width), BF), pltpu.VMEM((rows, width), BF),
                        pltpu.VMEM((rows, width), BF), pltpu.VMEM((rows, width), BF), pltpu.VMEM((rows, side), BF),
                        pltpu.VMEM((rows, side), BF), pltpu.VMEM((units, width, width), BF),
                        pltpu.SemaphoreType.DMA((7,)), pltpu.SemaphoreType.DMA((units, 6))],
        compiler_params=params(),
        cost_estimate=cost(16 * rows * width * width, 26 * rows * width),
        name="wgrad",
    )(sc, act, send, peer, hlc, hlcp, dup, dupp)


def wgrad_mix_body(sc, hlc, hlcp, dq_h, dk_h, dv_h, da_h, p1_h, p2_h, terms, small, s0, s1, s2, k0, k1, k2, small_o,
                   l1, l1p, l2, l2p, r1, r1p, r2, r2p, buf, sem_in, sem_out):
    width = l1.shape[1]
    core = sc[S_CORE]
    second = pl.ds(pl.multiple_of((1 + core) * width, width), width)
    loads = [
        pltpu.make_async_copy(hlc.at[:, pl.ds(width, width)], l1, sem_in.at[0]),
        pltpu.make_async_copy(hlcp.at[:, pl.ds(width, width)], l1p, sem_in.at[1]),
        pltpu.make_async_copy(p1_h, r1p, sem_in.at[2]),
        pltpu.make_async_copy(hlc.at[:, second], l2, sem_in.at[3]),
        pltpu.make_async_copy(hlcp.at[:, second], l2p, sem_in.at[4]),
        pltpu.make_async_copy(p2_h, r2p, sem_in.at[5]),
    ]
    start(loads)

    @pl.when(core == 0)
    def _():
        start([pltpu.make_async_copy(dq_h, r1, sem_in.at[6]), pltpu.make_async_copy(dk_h, r2, sem_in.at[7])])

    @pl.when(core != 0)
    def _():
        start([pltpu.make_async_copy(dv_h, r1, sem_in.at[6]), pltpu.make_async_copy(da_h, r2, sem_in.at[7])])

    tail = [pltpu.make_async_copy(dq_h, r1, sem_in.at[6]), pltpu.make_async_copy(dk_h, r2, sem_in.at[7])]
    small_o[...] = small[...] + (terms[0:16, :].astype(F32) + terms[16:32, :].astype(F32))
    sends, keeps = (s0, s1, s2), (k0, k1, k2)
    wait(loads[:3] + tail[:1])
    buf[0] = (dot_tn(l1[...], r1[...]) + dot_tn(l1p[...], r1p[...])).astype(BF)
    copies = cut_out(sc, buf, 0, sends, keeps, sem_out)
    wait(loads[3:] + tail[1:])
    buf[1] = (dot_tn(l2[...], r2[...]) + dot_tn(l2p[...], r2p[...])).astype(BF)
    copies += cut_out(sc, buf, 1, sends, keeps, sem_out)
    wait(copies)


def wgrad_mix(sc, hlc, hlcp, dq, dk, dv, da, p1, p2, terms, small):
    rows, width = dq.shape
    units = 2
    half = width // COLORS // 2
    anywhere = pl.BlockSpec(memory_space=pl.ANY)
    vmem = pl.BlockSpec(memory_space=pltpu.VMEM)
    part = shape_of((units * half, width), BF)
    return pl.pallas_call(
        wgrad_mix_body,
        in_specs=[pl.BlockSpec(memory_space=pltpu.SMEM)] + [anywhere] * 8 + [vmem] * 2,
        out_specs=[anywhere] * 6 + [vmem],
        out_shape=[part] * 6 + [shape_of(small.shape, F32)],
        scratch_shapes=[pltpu.VMEM((rows, width), BF)] * 8 + [pltpu.VMEM((units, width, width), BF),
                        pltpu.SemaphoreType.DMA((8,)), pltpu.SemaphoreType.DMA((units, 6))],
        compiler_params=params(),
        cost_estimate=cost(8 * rows * width * width, 20 * rows * width),
        name="wgrad_mix",
    )(sc, hlc, hlcp, dq, dk, dv, da, p1, p2, terms, small)


def add_rows(one, two):
    return (one.astype(F32) + two.astype(F32)).astype(BF)


def fold_body(sc, *refs, units, stage, small):
    keeps, gots = refs[:COLORS], refs[COLORS:2 * COLORS]
    outs = refs[2 * COLORS + small:]
    rows = keeps[0].shape[0] // units
    half = rows // 2
    merged = stage == 2
    for c in range(COLORS):
        bit = sc[S_BITS + (3 if merged else ORDER[c][stage + 1])]
        for u in range(units):
            go = pl.ds(pl.multiple_of(u * rows + (1 - bit) * half, LEAF), half)
            stay = pl.ds(pl.multiple_of(u * rows + bit * half, LEAF), half)
            send, keep = (outs[0], outs[1]) if merged else (outs[c], outs[COLORS + c])
            at = (c * units + u) * half if merged else u * half
            send[at:at + half, :] = add_rows(keeps[c][go, :], gots[c][go, :])
            keep[at:at + half, :] = add_rows(keeps[c][stay, :], gots[c][stay, :])
    if small:
        old, new, send = refs[2 * COLORS], outs[-1], outs[0]
        low = units * rows
        val = old[...] + (gots[0][low:low + 16, :].astype(F32) + gots[0][low + 16:low + 32, :].astype(F32))
        new[...] = val
        high, rest = split_terms(val)
        at = send.shape[0] - 32
        send[at:at + 16, :] = high
        send[at + 16:at + 32, :] = rest


def fold(sc, keeps, gots, small, units, stage):
    rows, width = keeps[0].shape
    vmem = pl.BlockSpec(memory_space=pltpu.VMEM)
    has = small is not None
    extra = 32 if has else 0
    if stage == 2:
        outs = [shape_of((COLORS * rows // 2 + extra, width), BF), shape_of((COLORS * rows // 2, width), BF)]
    else:
        outs = [shape_of((rows // 2 + (extra if c == 0 else 0), width), BF) for c in range(COLORS)]
        outs += [shape_of((rows // 2, width), BF)] * COLORS
    args = list(keeps) + list(gots)
    if has:
        args.append(small)
        outs.append(shape_of(small.shape, F32))
    got = pl.pallas_call(
        functools.partial(fold_body, units=units, stage=stage, small=has),
        out_shape=outs,
        in_specs=[pl.BlockSpec(memory_space=pltpu.SMEM)] + [vmem] * len(args),
        out_specs=[vmem] * len(outs),
        compiler_params=params(),
        cost_estimate=cost(6 * rows * width, 18 * rows * width),
        name="fold",
    )(sc, *args)
    if has:
        small = got[-1]
    if stage == 2:
        return [got[0]], [got[1]], small
    return got[:COLORS], got[COLORS:2 * COLORS], small


def total_body(keep, got, *refs):
    rows = keep.shape[0]
    refs[-1 if len(refs) == 1 else 1][...] = add_rows(keep[...], got[0:rows, :])
    if len(refs) > 1:
        refs[2][...] = refs[0][...] + (
            got[rows:rows + 16, :].astype(F32) + got[rows + 16:rows + 32, :].astype(F32))


def total(keep, got, small):
    vmem = pl.BlockSpec(memory_space=pltpu.VMEM)
    args = [keep, got]
    outs = [shape_of(keep.shape, BF)]
    if small is not None:
        args.append(small)
        outs.append(shape_of(small.shape, F32))
    res = pl.pallas_call(
        total_body,
        out_shape=outs,
        in_specs=[vmem] * len(args),
        out_specs=[vmem] * len(outs),
        compiler_params=params(),
        cost_estimate=cost(keep.size, 6 * keep.size),
        name="total",
    )(*args)
    return res[0], (res[1] if small is not None else None)


def join_body(sc, *refs, units, stage):
    outs = refs[-COLORS:]
    n = (len(refs) - COLORS) // 2
    owns, gots = refs[:n], refs[n:2 * n]
    rows = outs[0].shape[0] // units
    half = rows // 2
    for c in range(COLORS):
        bit = sc[S_BITS + (3 if stage == 3 else ORDER[c][stage])]
        own, got = (owns[0], gots[0]) if n == 1 else (owns[c], gots[c])
        for u in range(units):
            at = (c * units + u) * half if n == 1 else u * half
            outs[c][pl.ds(pl.multiple_of(u * rows + bit * half, LEAF), half), :] = own[at:at + half, :]
            outs[c][pl.ds(pl.multiple_of(u * rows + (1 - bit) * half, LEAF), half), :] = got[at:at + half, :]


def joined(sc, owns, gots, units, stage):
    width = owns[0].shape[1]
    rows = 2 * owns[0].shape[0] // (COLORS if len(owns) == 1 else 1)
    vmem = pl.BlockSpec(memory_space=pltpu.VMEM)
    args = list(owns) + list(gots)
    return pl.pallas_call(
        functools.partial(join_body, units=units, stage=stage),
        out_shape=[shape_of((rows, width), BF)] * COLORS,
        in_specs=[pl.BlockSpec(memory_space=pltpu.SMEM)] + [vmem] * len(args),
        out_specs=[vmem] * COLORS,
        compiler_params=params(),
        cost_estimate=cost(rows * width, 12 * rows * width),
        name="join",
    )(sc, *args)


def final_body(sc, *refs, mixed):
    j = pl.program_id(0)
    ins, outs = refs[:4 * COLORS], refs[4 * COLORS:]
    third = outs[0].shape[0] // COLORS
    half = third // 2

    def write(out, owns, gots):
        for c in range(COLORS):
            bit = sc[S_BITS + ORDER[c][0]]
            out[pl.ds(pl.multiple_of(c * third + bit * half, half), half), :] = owns[c][...].astype(F32)
            out[pl.ds(pl.multiple_of(c * third + (1 - bit) * half, half), half), :] = gots[c][...].astype(F32)

    for side in range(2):
        owns = ins[2 * side * COLORS:(2 * side + 1) * COLORS]
        gots = ins[(2 * side + 1) * COLORS:(2 * side + 2) * COLORS]
        here = (j >= 2) if side else (j < 2)
        if not mixed:
            @pl.when(here)
            def _():
                write(outs[0], owns, gots)
        else:
            other = (j % 2 == 1) & ((sc[S_CORE] == 0) if side else (sc[S_CORE] != 0))

            @pl.when(here & jnp.logical_not(other))
            def _():
                write(outs[0], owns, gots)

            @pl.when(here & other)
            def _():
                write(outs[1], owns, gots)


def final(sc, mine, theirs, first, kind):
    width = mine[0].shape[1]
    half = width // COLORS // 2
    own = pl.BlockSpec((half, width), lambda j, s: (first + jnp.minimum(j, 1), 0))
    far = pl.BlockSpec((half, width), lambda j, s: (first + jnp.maximum(j - 2, 0), 0))

    def place(j, s):
        return jnp.where(j < 2, s[S_CORE], 1 - s[S_CORE]) * 2 + j % 2

    if kind == "rows":
        specs = [pl.BlockSpec((width, width), lambda j, s: (place(j, s), 0))]
        outs = [shape_of((4 * width, width), F32)]
    elif kind == "cols":
        specs = [pl.BlockSpec((width, width), lambda j, s: (0, place(j, s)))]
        outs = [shape_of((width, 4 * width), F32)]
    else:
        specs = [pl.BlockSpec((width, width), lambda j, s: (0, jnp.minimum(place(j, s), 2))), full((width, width))]
        outs = [shape_of((width, 3 * width), F32), shape_of((width, width), F32)]
    grid = pltpu.PrefetchScalarGridSpec(
        num_scalar_prefetch=1,
        grid=(4,),
        in_specs=[own] * (2 * COLORS) + [far] * (2 * COLORS),
        out_specs=specs,
    )
    return pl.pallas_call(
        functools.partial(final_body, mixed=len(outs) == 2),
        grid_spec=grid,
        out_shape=outs,
        compiler_params=params(),
        cost_estimate=cost(4 * width * width, 24 * width * width),
        name="final",
    )(sc, *mine, *theirs)


def after(token, *values):
    return lax.optimization_barrier((token,) + values)[1:]


def corner(value):
    return value[:8, :128]


def body(
    hidden_in,
    lengths,
    qkv_weight,
    query_bias,
    value_bias,
    out_weight,
    out_bias,
    attn_gain,
    attn_shift,
    up_weight,
    up_bias,
    down_weight,
    down_bias,
    ffn_gain,
    ffn_shift,
    cotangent,
):
    count, local, width = hidden_in.shape
    nseq = lax.axis_size("seq")
    ndp = lax.axis_size("dp")
    seq = lax.axis_index("seq")
    dp = lax.axis_index("dp")
    core = dp & 1
    flat = seq * ndp + dp
    members = nseq * ndp
    line = lambda vec: vec.reshape(1, -1)

    axes = [ndp, 2 * ndp]
    mask = 2
    while mask < ndp:
        axes.append(mask)
        mask *= 2
    later = axes[4:]

    def permute(value, mask):
        return lax.ppermute(value, ("seq", "dp"), [(i, i ^ mask) for i in range(members)])

    def over(values, stage):
        if stage == 3:
            return [permute(values[0], axes[3])]
        return [permute(values[c], axes[ORDER[c][stage]]) for c in range(COLORS)]

    def core_swap(value):
        return permute(value, 1)

    holder = jnp.minimum(seq, count - 1)
    own_len = lax.dynamic_index_in_dim(lengths, holder, 0, False)
    own_len = jnp.where(seq < count, own_len, nseq * local)
    bits = [jnp.where((flat & mask) != 0, 1, 0) for mask in axes[:4]]
    sc = jnp.stack([seq, own_len, core] + bits + [core]).astype(jnp.int32)

    def to_holder(value):
        blocks = [lax.dynamic_index_in_dim(value, holder, 0, False)]
        parts = [lax.dynamic_index_in_dim(value, jnp.minimum(seq ^ k, count - 1), 0, False) for k in range(1, nseq)]
        for k in range(1, nseq):
            pairs = [(i, i ^ k) for i in range(nseq) if (i ^ k) < count]
            blocks.append(lax.ppermute(parts[k - 1], "seq", pairs))
        return blocks

    hids = to_holder(hidden_in)
    *hids, cot_in = lax.optimization_barrier(tuple(hids) + (cotangent,))
    cots = to_holder(cot_in)
    cots[0] = jnp.where(seq < count, cots[0], jnp.zeros_like(cots[0]))

    hlc, q, k, v, lse, n1, r1 = attn_fwd(
        sc, hids, qkv_weight, line(query_bias), line(value_bias), out_weight, line(out_bias),
        line(attn_gain), line(attn_shift))
    hlc_p = core_swap(hlc)
    act, send, dup, dup_send, lo, dres, dattn, dctx, stat = ffn(
        sc, hlc, n1, r1, up_weight, down_weight, out_weight, cots, line(attn_gain), line(attn_shift),
        line(up_bias), line(down_bias), line(ffn_gain), line(ffn_shift))
    send_p = core_swap(send)
    dup_p = core_swap(dup_send)
    *part, base = attn_bwd(sc, q, k, v, dctx, lse, qkv_weight, dres, dattn, stat, lo, ())
    send_p, dup_p = after(corner(base), send_p, dup_p)
    got = wgrad(sc, act, send, send_p, hlc, hlc_p, dup, dup_p)
    sends1, keeps1 = got[:COLORS], got[COLORS:]
    gots1 = over(sends1, 0)
    (base,) = after(corner(keeps1[0]), base)
    dq, dk, dv, one, two, small, terms, i0, i1, i2, i3 = attn_bwd(
        sc, q, k, v, dctx, lse, qkv_weight, base, dattn, part[5], lo, tuple(part[:5]))
    one_p, two_p, terms_p = core_swap(one), core_swap(two), core_swap(terms)
    token = corner(terms)

    keeps1 = after(token, *keeps1, *gots1)
    keeps1, gots1 = keeps1[:COLORS], keeps1[COLORS:]
    sends1, keeps1, _ = fold(sc, keeps1, gots1, None, 4, 0)
    gots1 = over(sends1, 1)
    one_p, two_p, terms_p = after(corner(keeps1[0]), one_p, two_p, terms_p)
    *got, small = wgrad_mix(sc, hlc, hlc_p, dq, dk, dv, dattn, one_p, two_p, terms_p, small)
    sends2, keeps2 = list(got[:COLORS]), got[COLORS:]
    high, rest = split_terms(small)
    sends2[0] = jnp.concatenate([sends2[0], high, rest], 0)
    gots2 = over(sends2, 0)
    token = corner(keeps2[0])

    def step(kind, token, keeps, gots, small, units, stage):
        held = [] if small is None else [small]
        vals = after(token, *keeps, *gots, *held)
        n = len(keeps)
        keeps, gots = vals[:n], vals[n:2 * n]
        small = vals[2 * n] if held else None
        if kind == "fold":
            if stage < 3:
                sends, keeps, small = fold(sc, keeps, gots, small, units, stage)
            else:
                whole, small = total(keeps[0], gots[0], small)
                for mask in later:
                    if small is None:
                        whole = add_rows(whole, permute(whole, mask))
                    else:
                        high, rest = split_terms(small)
                        more = permute(jnp.concatenate([whole, high, rest], 0), mask)
                        size = whole.shape[0]
                        whole = add_rows(whole, more[:size])
                        small = small + (more[size:size + 16].astype(F32) + more[size + 16:].astype(F32))
                sends = keeps = [whole]
        else:
            sends = keeps = joined(sc, keeps, gots, units, stage)
        return sends, keeps, small, corner(keeps[0])

    plan = [("fold", 1, 1), ("fold", 2, 0), ("fold", 1, 2), ("fold", 2, 1), ("fold", 1, 3), ("fold", 2, 2),
            ("join", 1, 3), ("fold", 2, 3), ("join", 1, 2), ("join", 2, 3), ("join", 1, 1), ("join", 2, 2),
            ("join", 2, 1)]
    state = {1: (keeps1, gots1, None, 4), 2: (keeps2, gots2, small, 2)}
    far = {}
    for at, (kind, piece, stage) in enumerate(plan):
        keeps, gots, small, units = state[piece]
        sends, keeps, small, token = step(kind, token, keeps, gots, small, units, stage)
        if kind == "fold":
            upcoming = stage + 1 if stage < 3 else 3
        else:
            upcoming = stage - 1
        gots = over(sends, upcoming)
        state[piece] = (keeps, gots, small, units)
        if kind == "join" and stage == 1:
            far[piece] = [core_swap(value) for value in keeps]
        if at == 0:
            blocks = after(token, i0, i1, i2, i3)
            back = [blocks[0]]
            for k_at in range(1, nseq):
                pairs = [(i, i ^ k_at) for i in range(nseq) if i < count]
                back.append(lax.ppermute(blocks[k_at], "seq", pairs))

    keeps1, gots1 = state[1][:2]
    vals = after(token, *keeps1, *gots1)
    keeps1, gots1 = vals[:COLORS], vals[COLORS:]
    far1 = far[1] + [core_swap(value) for value in gots1]
    back = after(corner(gots1[0]), *back)
    shown = []
    for p in range(count):
        value = back[0]
        for k_at in range(1, nseq):
            value = jnp.where((seq ^ p) == k_at, back[k_at], value)
        shown.append(value)
    layer_out = jnp.stack([value[:local] for value in shown])
    input_grad = jnp.stack([value[local:] for value in shown])
    mine1 = list(keeps1) + list(gots1)
    (down_grad,) = final(sc, mine1, far1, 0, "rows")
    (up_grad,) = final(sc, mine1, far1, 2, "cols")
    keeps2, gots2, small, _ = state[2]
    vals = after(corner(up_grad), corner(down_grad), *keeps2, *gots2)[1:]
    keeps2, gots2 = vals[:COLORS], vals[COLORS:]
    far2 = far[2] + [core_swap(value) for value in gots2]
    qkv_grad, out_grad = final(sc, list(keeps2) + list(gots2), far2, 0, "mixed")
    return (
        layer_out,
        input_grad,
        qkv_grad,
        small[6],
        small[7],
        out_grad,
        small[5],
        small[3],
        small[4],
        up_grad,
        small[8:12].reshape(-1),
        down_grad,
        small[2],
        small[0],
        small[1],
    )


def solution(mesh):
    split = P("dp", "seq", None)
    return jax.shard_map(
        body,
        mesh=mesh,
        in_specs=(split, P("dp")) + (P(),) * 13 + (split,),
        out_specs=(split, split) + (P(),) * 13,
        check_vma=False,
    )
```

time: 1460 us -> 339 us (0.23); the launches traced: 1440 us -> 337 us
  waiting for transfers between devices: 891 us -> 75.7 us
  local copies, waits for them, and re-layouts: 408 us -> 28.3 us
  Pallas kernels: 0 us -> 144 us
  matrix products: 73.4 us -> 0 us
  starting transfers between devices: 14.2 us -> 82.5 us
  other arithmetic: 21.1 us -> 5.29 us
    unnamed x4 -> x0, waiting for transfers between devices: 862 us -> none
    unnamed x86 -> x120, local copies, waits for them, and re-layouts: 242 us -> 13 us
    pallas_call x0 -> x23, Pallas kernels: none -> 144 us  [the longest x2 26.8 us: attn_bwd(): pl.pallas_call(functools.partial(attn_bwd_body, first=first, last=not fir...]
    ppermute x0 -> x67, starting transfers between devices: none -> 82.5 us  [the longest x58 54 us: permute(): lax.ppermute(value, ('seq', 'dp'), [(i, i ^ mask) for i in range(members)])]
    ppermute x0 -> x67, waiting for transfers between devices: none -> 75.7 us  [the longest x58 75.7 us: permute(): lax.ppermute(value, ('seq', 'dp'), [(i, i ^ mask) for i in range(members)])]
    dot_general x33 -> x0, matrix products: 73.4 us -> none  [the longest x1 14.9 us: body(): jnp.dot(first_low, up_weight, preferred_element_type=jnp.float32) + up_bias]
    slice x8 -> x2, local copies, waits for them, and re-layouts: 48.2 us -> 0.66 us  [the longest x1 0.66 us: body(): small[1]]
    reshape x8 -> x9, local copies, waits for them, and re-layouts: 50.8 us -> 10.7 us  [the longest x8 10.1 us: body(): line = lambda vec: vec.reshape(1, -1)]
  transfers between devices with their start and end apart: 5 -> 67, of which waited for: 4 -> 21; matrix products, arithmetic and copies ran while one was open for 3% -> 5% of each run, Pallas kernels for 0% -> 29%
where the time goes in v3:
time: 339 us; the launch traced here: 337 us
  Pallas kernels  144 us (42%)
  starting transfers between devices  82.5 us (24%)
  waiting for transfers between devices  75.7 us (22%)
  local copies, waits for them, and re-layouts  28.3 us (8%)
  other arithmetic  5.29 us (2%)
    ppermute x58, waiting for transfers between devices, permute(): lax.ppermute(value, ('seq', 'dp'), [(i, i ^ mask) for i in range(members)])  75.7 us
    ppermute x58, starting transfers between devices, permute(): lax.ppermute(value, ('seq', 'dp'), [(i, i ^ mask) for i in range(members)])  54 us
    pallas_call x2, Pallas kernels, attn_bwd(): pl.pallas_call(functools.partial(attn_bwd_body, first=first, last=not fir...  26.8 us
    pallas_call x1, Pallas kernels, ffn(): pl.pallas_call(ffn_body, in_specs=[smem] + [anywhere] * 5 + [vmem] * 11,...  24.2 us
    pallas_call x3, Pallas kernels, final(): pl.pallas_call(functools.partial(final_body, mixed=len(outs) == 2), grid_...  23.5 us
    ppermute x6, starting transfers between devices, to_holder(): blocks.append(lax.ppermute(parts[k - 1], 'seq', pairs))  18.8 us
    pallas_call x1, Pallas kernels, attn_fwd(): pl.pallas_call(attn_fwd_body, grid_spec=grid, out_shape=[shape_of((rows,...  16.7 us
    pallas_call x6, Pallas kernels, fold(): pl.pallas_call(functools.partial(fold_body, units=units, stage=stage, sma...  16.6 us
  transfers between devices with their start and end apart: 67, of which 21 were waited for; matrix products, arithmetic and copies ran while one was open for 5% of the time, Pallas kernels for 29%

profile of v3, /device:TPU:0, one launch (start us, length us, event | category | flops | bytes accessed | tf_op | source)
XLA Modules:
  0.0 337.3 jit_solution(6108909760126098144)
XLA Ops:
  0.7 2.0 dynamic-slice_bitcast_fusion.3
  2.6 1.3 collective-permute-start.2
  3.9 7.0 %collective-permute-start = (bf16[128,768]{1,0:T(8,128)(2,1)S(1)}, bf16[128,768]{1,0:T(8,128)(2,1)S(1)}, u32[]{:S(2)}, u32[]{:S(2)}) collective-permute-start(bf16[128,768]{1,0:T(8,128)(2,1)S(1)} %get-tuple-element.443), channel_id=1, source_target_pairs={{0,8},{8,0},{24,16},{1,9},{9,1},{25,17},{2,10},{10,2},{26,18},{3,1... | collective-permute-start | bytes 589832 | tf_op jit(solution)/shard_map/ppermute | solution.py:807
  10.9 1.9 collective-permute-start.1
  25.5 2.1 dynamic-slice_bitcast_fusion
  27.7 1.3 collective-permute-start.5
  28.9 4.6 %collective-permute-start.4 = (bf16[128,768]{1,0:T(8,128)(2,1)S(1)}, bf16[128,768]{1,0:T(8,128)(2,1)S(1)}, u32[]{:S(2)}, u32[]{:S(2)}) collective-permute-start(bf16[128,768]{1,0:T(8,128)(2,1)S(1)} %get-tuple-element.439), channel_id=1, source_target_pairs={{0,16},{16,0},{24,8},{1,17},{17,1},{25,9},{2,18},{18,2},{26,10},{3... | collective-permute-start | bytes 589832 | tf_op jit(solution)/shard_map/ppermute | solution.py:807
  33.5 2.7 collective-permute-start.3
  36.3 16.7 %attn_fwd.1 = (bf16[512,2304]{1,0:T(8,128)(2,1)}, bf16[512,768]{1,0:T(8,128)(2,1)}, bf16[512,768]{1,0:T(8,128)(2,1)}, bf16[512,768]{1,0:T(8,128)(2,1)}, f32[16,5...) custom-call(s32[8]{0:T(128)} %stack.56.sc, bf16[128,768]{1,0:T(8,128)(2,1)} %get-tuple-element.220.h0, ...), custom_call_target="tpu_custom_call" | custom-call | flops 3221225472 | bytes 9437184 | tf_op jit(solution)/shard_map/attn_fwd/pallas_call | solution.py:151
  53.8 24.2 %ffn.1 = (bf16[512,1536]{1,0:T(8,128)(2,1)}, bf16[512,2304]{1,0:T(8,128)(2,1)}, bf16[512,1536]{1,0:T(8,128)(2,1)}, bf16[512,1536]{1,0:T(8,128)(2,1)}, bf16[512,7...) custom-call(s32[8]{0:T(128)} %stack.56.sc, ...), custom_call_target="tpu_custom_call" | custom-call | flops 9663676416 | bytes 18874368 | tf_op jit(solution)/shard_map/ffn/pallas_call | solution.py:292
  78.7 13.2 %attn_bwd.2 = (bf16[512,768]{1,0:T(8,128)(2,1)}, bf16[512,768]{1,0:T(8,128)(2,1)}, bf16[512,768]{1,0:T(8,128)(2,1)}, bf16[512,768]{1,0:T(8,128)(2,1)}, bf16[512,...) custom-call(s32[8]{0:T(128)} %stack.56.sc, bf16[512,768]{1,0:T(8,128)(2,1)} %get-tuple-element.259.q_r, ...), custom_call_target="tpu_custom_call" | custom-call | flops 1912602624 | bytes 4128768 | tf_op jit(solution)/shard_map/attn_bwd/pallas_call | solution.py:425
  91.9 13.6 %attn_bwd.3 = (bf16[512,768]{1,0:T(8,128)(2,1)}, bf16[512,768]{1,0:T(8,128)(2,1)}, bf16[512,768]{1,0:T(8,128)(2,1)}, bf16[512,768]{1,0:T(8,128)(2,1)}, bf16[512,...) custom-call(s32[8]{0:T(128)} %stack.56.sc, ...), custom_call_target="tpu_custom_call", output_to_operand_aliasing={{0}: (13, {}), {1}: (14, {}), {2}: (15, {}), {3}: (16, {}),... | custom-call | flops 1912602624 | bytes 4128768 | tf_op jit(solution)/shard_map/attn_bwd/pallas_call | solution.py:425
  106.6 9.7 %wgrad.1 = (bf16[512,768]{1,0:T(8,128)(2,1)}, bf16[512,768]{1,0:T(8,128)(2,1)}, bf16[512,768]{1,0:T(8,128)(2,1)}, bf16[512,768]{1,0:T(8,128)(2,1)}, bf16[512,768]{1,0:T(8,128)(2,1)}, /*index=5*/bf16[512,768]{1,0:T(8,128)(2,1)}) custom-call(s32[8]{0:T(128)} %stack.56.sc, bf16[512,1536]{1,0:T(8,128)(2,1)} %get-tuple-element.228.act_h, ...), custom_call_target="tpu_custom_call" | custom-call | flops 4831838208 | bytes 10223616 | tf_op jit(solution)/shard_map/wgrad/pallas_call | solution.py:488
  118.4 1.6 collective-permute-start.11
  121.1 8.8 %wgrad_mix.1 = (bf16[256,768]{1,0:T(8,128)(2,1)}, bf16[256,768]{1,0:T(8,128)(2,1)}, bf16[256,768]{1,0:T(8,128)(2,1)}, bf16[256,768]{1,0:T(8,128)(2,1)}, bf16[256...) custom-call(s32[8]{0:T(128)} %stack.56.sc, bf16[512,2304]{1,0:T(8,128)(2,1)} %get-tuple-element.224.hlc, ...), custom_call_target="tpu_custom_call" | custom-call | flops 2415919104 | bytes 7864320 | tf_op jit(solution)/shard_map/wgrad_mix/pallas_call | solution.py:545
  130.0 6.1 %collective-permute-done.9.refs_3_ = bf16[512,768]{1,0:T(8,128)(2,1)S(1)} collective-permute-done((bf16[512,768]{1,0:T(8,128)(2,1)}, bf16[512,768]{1,0:T(8,128)(2,1)S(1)}, u32[]{:S(2)}, u32[]{:S(2)}) %collective-permute-start.9) | collective-permute-done | bytes 786464 | tf_op jit(solution)/shard_map/ppermute | solution.py:786
  138.5 4.3 %fold.6 = (bf16[256,768]{1,0:T(8,128)(2,1)}, bf16[256,768]{1,0:T(8,128)(2,1)}, bf16[256,768]{1,0:T(8,128)(2,1)}, bf16[256,768]{1,0:T(8,128)(2,1)}, bf16[256,768]{1,0:T(8,128)(2,1)}, /*index=5*/bf16[256,768]{1,0:T(8,128)(2,1)}) custom-call(s32[8]{0:T(128)} %stack.56.sc, bf16[512,768]{1,0:T(8,128)(2,1)} %get-tuple-element.240.refs_0_, ...), custom_call_target="tpu_custom_call" | custom-call | flops 2359296 | bytes 7077888 | tf_op jit(solution)/shard_map/fold/pallas_call | solution.py:602
  144.0 1.7 collective-permute-start.13
  148.6 6.4 %collective-permute-done.12.refs_3_ = bf16[256,768]{1,0:T(8,128)(2,1)S(1)} collective-permute-done((bf16[256,768]{1,0:T(8,128)(2,1)}, bf16[256,768]{1,0:T(8,128)(2,1)S(1)}, u32[]{:S(2)}, u32[]{:S(2)}) %collective-permute-start.12) | collective-permute-done | bytes 393248 | tf_op jit(solution)/shard_map/ppermute | solution.py:786
  155.0 1.6 collective-permute-start.23
  158.6 2.8 fold.7
  163.3 1.7 collective-permute-done.23.refs_5_
  164.9 1.7 collective-permute-done.21.refs_3_
  167.3 2.9 fold.8
  173.1 2.3 fold.11
  175.4 2.6 collective-permute-start.50
  178.8 2.3 fold.9
  181.1 1.6 collective-permute-start.27
  185.1 2.4 collective-permute-done.28.refs_4_
  189.4 2.0 fold.10
  191.4 2.4 collective-permute-start.30
  194.5 1.9 total.3.refs_0_
  196.9 10.8 %collective-permute-done.30.got = bf16[128,768]{1,0:T(8,128)(2,1)S(1)} collective-permute-done((bf16[128,768]{1,0:T(8,128)(2,1)}, bf16[128,768]{1,0:T(8,128)(2,1)S(1)}, u32[]{:S(2)}, u32[]{:S(2)}) %collective-permute-start.30) | collective-permute-done | bytes 196640 | tf_op jit(solution)/shard_map/ppermute | solution.py:786
  208.4 1.7 total.2
  210.1 7.3 %collective-permute-done.31.refs_1_ = bf16[96,768]{1,0:T(8,128)(2,1)S(1)} collective-permute-done((bf16[96,768]{1,0:T(8,128)(2,1)}, bf16[96,768]{1,0:T(8,128)(2,1)S(1)}, u32[]{:S(2)}, u32[]{:S(2)}) %collective-permute-start.31) | collective-permute-done | bytes 147488 | tf_op jit(solution)/shard_map/ppermute | solution.py:786
  218.1 1.7 join.6
  220.5 1.9 join.9
  222.5 2.0 collective-permute-start.52
  226.5 1.3 collective-permute-start.33
  228.5 2.9 collective-permute-done.33.refs_4_
  231.4 2.3 collective-permute-done.34.refs_5_
  234.4 2.0 join.7
  236.4 1.5 collective-permute-start.35
  239.3 2.4 join.10
  242.3 1.4 collective-permute-start.57
  243.7 2.0 collective-permute-start.36
  246.3 6.0 %collective-permute-done.36.refs_4_ = bf16[128,768]{1,0:T(8,128)(2,1)S(1)} collective-permute-done((bf16[128,768]{1,0:T(8,128)(2,1)}, bf16[128,768]{1,0:T(8,128)(2,1)S(1)}, u32[]{:S(2)}, u32[]{:S(2)}) %collective-permute-start.36) | collective-permute-done | bytes 196640 | tf_op jit(solution)/shard_map/ppermute | solution.py:786
  252.3 3.3 collective-permute-start.15
  255.6 2.0 collective-permute-done.37.refs_5_
  257.7 3.2 collective-permute-start.16
  260.9 2.4 join.8
  263.3 3.3 collective-permute-start.17
  268.0 3.1 join.11
  271.1 2.2 collective-permute-start.39
  274.1 1.3 collective-permute-start.58
  276.2 3.1 collective-permute-start.59
  279.3 2.8 collective-permute-start.60
  282.1 3.5 %collective-permute-done.38.refs_3_ = bf16[256,768]{1,0:T(8,128)(2,1)} collective-permute-done((bf16[256,768]{1,0:T(8,128)(2,1)}, bf16[256,768]{1,0:T(8,128)(2,1)}, u32[]{:S(2)}, u32[]{:S(2)}) %collective-permute-start.38) | collective-permute-done | bytes 393248 | tf_op jit(solution)/shard_map/ppermute | solution.py:786
  285.5 2.9 collective-permute-start.40
  288.4 16.8 %collective-permute-done.40.refs_5_ = bf16[256,768]{1,0:T(8,128)(2,1)} collective-permute-done((bf16[256,768]{1,0:T(8,128)(2,1)}, bf16[256,768]{1,0:T(8,128)(2,1)}, u32[]{:S(2)}, u32[]{:S(2)}) %collective-permute-start.40) | collective-permute-done | bytes 393248 | tf_op jit(solution)/shard_map/ppermute | solution.py:786
  306.5 1.4 select_select_fusion.2
  313.8 7.8 %final.3 = (f32[768,2304]{1,0:T(8,128)}, f32[768,768]{1,0:T(8,128)}) custom-call(s32[8]{0:T(128)} %stack.56.sc, bf16[256,768]{1,0:T(8,128)(2,1)} %get-tuple-element.372.refs_0_, bf16[256,768]{1,0:T(8,128)(2,1)} %get-tuple-element.373.refs_1_, bf16[256,768]{1,0:T(8,128)(2,1)} %get-tuple-element.374.refs_2_, bf16[256,768]{1,0:T(8,128)(2,1)} %collective-permute-done.38.refs_3_, ...), custom_call_target="tpu_custom_call" | custom-call | flops 2359296 | bytes 14155776 | tf_op jit(solution)/shard_map/final/pallas_call | solution.py:732
  321.6 7.8 %final.5 = f32[3072,768]{1,0:T(8,128)} custom-call(s32[8]{0:T(128)} %stack.56.sc, bf16[512,768]{1,0:T(8,128)(2,1)} %get-tuple-element.419.refs_0_, bf16[512,768]{1,0:T(8,128)(2,1)} %get-tuple-element.420.refs_1_, bf16[512,768]{1,0:T(8,128)(2,1)} %get-tuple-element.421.refs_2_, bf16[512,768]{1,0:T(8,128)(2,1)} %copy-done.2, bf16[512,768]{1,0:T(8,128)(2,1)} %copy-done.3, ...), custom_call_target="tpu_custom_call" | custom-call | flops 2359296 | bytes 14155776 | tf_op jit(solution)/shard_map/final/pallas_call | solution.py:732
  329.5 7.8 %final.4 = f32[768,3072]{1,0:T(8,128)} custom-call(s32[8]{0:T(128)} %stack.56.sc, bf16[512,768]{1,0:T(8,128)(2,1)} %get-tuple-element.419.refs_0_, bf16[512,768]{1,0:T(8,128)(2,1)} %get-tuple-element.420.refs_1_, bf16[512,768]{1,0:T(8,128)(2,1)} %get-tuple-element.421.refs_2_, bf16[512,768]{1,0:T(8,128)(2,1)} %copy-done.2, bf16[512,768]{1,0:T(8,128)(2,1)} %copy-done.3, ...), custom_call_target="tpu_custom_call" | custom-call | flops 2359296 | bytes 14155776 | tf_op jit(solution)/shard_map/final/pallas_call | solution.py:732
  (235 shorter events, 56.1 us)
Async XLA Ops:
  2.6 22.8 %collective-permute-start.2 = (bf16[128,768]{1,0:T(8,128)(2,1)S(1)}, bf16[128,768]{1,0:T(8,128)(2,1)S(1)}, u32[]{:S(2)}, u32[]{:S(2)}) collective-permute-start(bf16[128,768]{1,0:T(8,128)(2,1)S(1)} %get-tuple-element.442), channel_id=1, source_target_pairs={{8,16},{16,8},{24,0},{9,17},{17,9},{25,1},{10,18},{18,10},{26,2},{... | collective-permute-start | bytes 589832 | tf_op jit(solution)/shard_map/ppermute | solution.py:807
  3.9 21.6 %collective-permute-start = (bf16[128,768]{1,0:T(8,128)(2,1)S(1)}, bf16[128,768]{1,0:T(8,128)(2,1)S(1)}, u32[]{:S(2)}, u32[]{:S(2)}) collective-permute-start(bf16[128,768]{1,0:T(8,128)(2,1)S(1)} %get-tuple-element.443), channel_id=1, source_target_pairs={{0,8},{8,0},{24,16},{1,9},{9,1},{25,17},{2,10},{10,2},{26,18},{3,1... | collective-permute-start | bytes 589832 | tf_op jit(solution)/shard_map/ppermute | solution.py:807
  10.9 14.6 %collective-permute-start.1 = (bf16[128,768]{1,0:T(8,128)(2,1)S(1)}, bf16[128,768]{1,0:T(8,128)(2,1)S(1)}, u32[]{:S(2)}, u32[]{:S(2)}) collective-permute-start(bf16[128,768]{1,0:T(8,128)(2,1)S(1)} %get-tuple-element.445), channel_id=1, source_target_pairs={{0,16},{16,0},{24,8},{1,17},{17,1},{25,9},{2,18},{18,2},{26,10},{3... | collective-permute-start | bytes 589832 | tf_op jit(solution)/shard_map/ppermute | solution.py:807
  27.7 25.3 %collective-permute-start.5 = (bf16[128,768]{1,0:T(8,128)(2,1)S(1)}, bf16[128,768]{1,0:T(8,128)(2,1)S(1)}, u32[]{:S(2)}, u32[]{:S(2)}) collective-permute-start(bf16[128,768]{1,0:T(8,128)(2,1)S(1)} %get-tuple-element.438), channel_id=1, source_target_pairs={{8,16},{16,8},{24,0},{9,17},{17,9},{25,1},{10,18},{18,10},{26,2},{... | collective-permute-start | bytes 589832 | tf_op jit(solution)/shard_map/ppermute | solution.py:807
  28.9 24.1 %collective-permute-start.4 = (bf16[128,768]{1,0:T(8,128)(2,1)S(1)}, bf16[128,768]{1,0:T(8,128)(2,1)S(1)}, u32[]{:S(2)}, u32[]{:S(2)}) collective-permute-start(bf16[128,768]{1,0:T(8,128)(2,1)S(1)} %get-tuple-element.439), channel_id=1, source_target_pairs={{0,16},{16,0},{24,8},{1,17},{17,1},{25,9},{2,18},{18,2},{26,10},{3... | collective-permute-start | bytes 589832 | tf_op jit(solution)/shard_map/ppermute | solution.py:807
  33.5 19.5 %collective-permute-start.3 = (bf16[128,768]{1,0:T(8,128)(2,1)S(1)}, bf16[128,768]{1,0:T(8,128)(2,1)S(1)}, u32[]{:S(2)}, u32[]{:S(2)}) collective-permute-start(bf16[128,768]{1,0:T(8,128)(2,1)S(1)} %get-tuple-element.440), channel_id=1, source_target_pairs={{0,8},{8,0},{24,16},{1,9},{9,1},{25,17},{2,10},{10,2},{26,18},{3,1... | collective-permute-start | bytes 589832 | tf_op jit(solution)/shard_map/ppermute | solution.py:807
  78.1 28.6 %collective-permute-start.6 = (bf16[512,2304]{1,0:T(8,128)(2,1)}, bf16[512,2304]{1,0:T(8,128)(2,1)}, u32[]{:S(2)}, u32[]{:S(2)}) collective-permute-start(bf16[512,2304]{1,0:T(8,128)(2,1)} %get-tuple-element.229.send_h), channel_id=1, source_target_pairs={{0,1},{1,0},{2,3},{3,2},{4,5},{5,4},{6,7},{7,6},{8,9},{9,8},{10,11... | collective-permute-start | bytes 7077896 | tf_op jit(solution)/shard_map/ppermute | solution.py:786
  78.1 28.5 %collective-permute-start.8 = (bf16[512,2304]{1,0:T(8,128)(2,1)S(1)}, bf16[512,2304]{1,0:T(8,128)(2,1)}, u32[]{:S(2)}, u32[]{:S(2)}) collective-permute-start(bf16[512,2304]{1,0:T(8,128)(2,1)S(1)} %copy-done.4), channel_id=1, source_target_pairs={{0,1},{1,0},{2,3},{3,2},{4,5},{5,4},{6,7},{7,6},{8,9},{9,8},{10,11... | collective-permute-start | bytes 7077896 | tf_op jit(solution)/shard_map/ppermute | solution.py:786
  78.6 27.6 %collective-permute-start.7 = (bf16[512,1536]{1,0:T(8,128)(2,1)}, bf16[512,1536]{1,0:T(8,128)(2,1)}, u32[]{:S(2)}, u32[]{:S(2)}) collective-permute-start(bf16[512,1536]{1,0:T(8,128)(2,1)} %get-tuple-element.230), channel_id=1, source_target_pairs={{0,1},{1,0},{2,3},{3,2},{4,5},{5,4},{6,7},{7,6},{8,9},{9,8},{10,11... | collective-permute-start | bytes 4718600 | tf_op jit(solution)/shard_map/ppermute | solution.py:786
  105.6 12.9 %collective-permute-start.20 = (bf16[32,768]{1,0:T(8,128)(2,1)}, bf16[32,768]{1,0:T(8,128)(2,1)S(1)}, u32[]{:S(2)}, u32[]{:S(2)}) collective-permute-start(bf16[32,768]{1,0:T(8,128)(2,1)} %get-tuple-element.292), channel_id=1, source_target_pairs={{0,1},{1,0},{2,3},{3,2},{4,5},{5,4},{6,7},{7,6},{8,9},{9,8},{10,11... | collective-permute-start | bytes 147464 | tf_op jit(solution)/shard_map/ppermute | solution.py:786
  106.1 13.9 %collective-permute-start.18 = (bf16[512,768]{1,0:T(8,128)(2,1)}, bf16[512,768]{1,0:T(8,128)(2,1)S(1)}, u32[]{:S(2)}, u32[]{:S(2)}) collective-permute-start(bf16[512,768]{1,0:T(8,128)(2,1)} %get-tuple-element.290), channel_id=1, source_target_pairs={{0,1},{1,0},{2,3},{3,2},{4,5},{5,4},{6,7},{7,6},{8,9},{9,8},{10,11... | collective-permute-start | bytes 2359304 | tf_op jit(solution)/shard_map/ppermute | solution.py:786
  106.2 13.8 %collective-permute-start.19 = (bf16[512,768]{1,0:T(8,128)(2,1)}, bf16[512,768]{1,0:T(8,128)(2,1)S(1)}, u32[]{:S(2)}, u32[]{:S(2)}) collective-permute-start(bf16[512,768]{1,0:T(8,128)(2,1)} %get-tuple-element.291), channel_id=1, source_target_pairs={{0,1},{1,0},{2,3},{3,2},{4,5},{5,4},{6,7},{7,6},{8,9},{9,8},{10,11... | collective-permute-start | bytes 2359304 | tf_op jit(solution)/shard_map/ppermute | solution.py:786
  116.3 19.8 %collective-permute-start.9 = (bf16[512,768]{1,0:T(8,128)(2,1)}, bf16[512,768]{1,0:T(8,128)(2,1)S(1)}, u32[]{:S(2)}, u32[]{:S(2)}) collective-permute-start(bf16[512,768]{1,0:T(8,128)(2,1)} %get-tuple-element.237), channel_id=1, source_target_pairs={{0,8},{1,9},{2,10},{3,11},{4,12},{5,13},{6,14},{7,15},{8,0},{9,1},... | collective-permute-start | bytes 2359304 | tf_op jit(solution)/shard_map/ppermute | solution.py:786
  117.6 19.5 %collective-permute-start.10 = (bf16[512,768]{1,0:T(8,128)(2,1)}, bf16[512,768]{1,0:T(8,128)(2,1)S(1)}, u32[]{:S(2)}, u32[]{:S(2)}) collective-permute-start(bf16[512,768]{1,0:T(8,128)(2,1)} %get-tuple-element.238), channel_id=1, source_target_pairs={{0,16},{1,17},{2,18},{3,19},{4,20},{5,21},{6,22},{7,23},{8,24},{9,... | collective-permute-start | bytes 2359304 | tf_op jit(solution)/shard_map/ppermute | solution.py:786
  118.4 19.2 %collective-permute-start.11 = (bf16[512,768]{1,0:T(8,128)(2,1)}, bf16[512,768]{1,0:T(8,128)(2,1)S(1)}, u32[]{:S(2)}, u32[]{:S(2)}) collective-permute-start(bf16[512,768]{1,0:T(8,128)(2,1)} %get-tuple-element.239), channel_id=1, source_target_pairs={{0,2},{1,3},{2,0},{3,1},{4,6},{5,7},{6,4},{7,5},{8,10},{9,11},{10,... | collective-permute-start | bytes 2359304 | tf_op jit(solution)/shard_map/ppermute | solution.py:786
  142.8 12.2 %collective-permute-start.12 = (bf16[256,768]{1,0:T(8,128)(2,1)}, bf16[256,768]{1,0:T(8,128)(2,1)S(1)}, u32[]{:S(2)}, u32[]{:S(2)}) collective-permute-start(bf16[256,768]{1,0:T(8,128)(2,1)} %get-tuple-element.249), channel_id=1, source_target_pairs={{0,16},{1,17},{2,18},{3,19},{4,20},{5,21},{6,22},{7,23},{8,24},{9,... | collective-permute-start | bytes 1179656 | tf_op jit(solution)/shard_map/ppermute | solution.py:786
  144.0 12.6 %collective-permute-start.13 = (bf16[256,768]{1,0:T(8,128)(2,1)}, bf16[256,768]{1,0:T(8,128)(2,1)S(1)}, u32[]{:S(2)}, u32[]{:S(2)}) collective-permute-start(bf16[256,768]{1,0:T(8,128)(2,1)} %get-tuple-element.250), channel_id=1, source_target_pairs={{0,2},{1,3},{2,0},{3,1},{4,6},{5,7},{6,4},{7,5},{8,10},{9,11},{10,... | collective-permute-start | bytes 1179656 | tf_op jit(solution)/shard_map/ppermute | solution.py:786
  145.7 12.2 %collective-permute-start.14 = (bf16[256,768]{1,0:T(8,128)(2,1)}, bf16[256,768]{1,0:T(8,128)(2,1)S(1)}, u32[]{:S(2)}, u32[]{:S(2)}) collective-permute-start(bf16[256,768]{1,0:T(8,128)(2,1)} %get-tuple-element.251), channel_id=1, source_target_pairs={{0,8},{1,9},{2,10},{3,11},{4,12},{5,13},{6,14},{7,15},{8,0},{9,1},... | collective-permute-start | bytes 1179656 | tf_op jit(solution)/shard_map/ppermute | solution.py:786
  146.5 20.1 %collective-permute-start.21 = (bf16[288,768]{1,0:T(8,128)(2,1)S(1)}, bf16[288,768]{1,0:T(8,128)(2,1)S(1)}, u32[]{:S(2)}, u32[]{:S(2)}) collective-permute-start(bf16[288,768]{1,0:T(8,128)(2,1)S(1)} %pad_maximum_fusion.2), channel_id=1, source_target_pairs={{0,8},{1,9},{2,10},{3,11},{4,12},{5,13},{6,14},{7,15},{8,0},{9,1},... | collective-permute-start | bytes 1327112 | tf_op jit(solution)/shard_map/ppermute | solution.py:786
  147.8 14.9 %collective-permute-start.22 = (bf16[256,768]{1,0:T(8,128)(2,1)S(1)}, bf16[256,768]{1,0:T(8,128)(2,1)S(1)}, u32[]{:S(2)}, u32[]{:S(2)}) collective-permute-start(bf16[256,768]{1,0:T(8,128)(2,1)S(1)} %copy-done.56), channel_id=1, source_target_pairs={{0,16},{1,17},{2,18},{3,19},{4,20},{5,21},{6,22},{7,23},{8,24},{9,... | collective-permute-start | bytes 1179656 | tf_op jit(solution)/shard_map/ppermute | solution.py:786
  155.0 9.9 %collective-permute-start.23 = (bf16[256,768]{1,0:T(8,128)(2,1)S(1)}, bf16[256,768]{1,0:T(8,128)(2,1)S(1)}, u32[]{:S(2)}, u32[]{:S(2)}) collective-permute-start(bf16[256,768]{1,0:T(8,128)(2,1)S(1)} %copy-done.55), channel_id=1, source_target_pairs={{0,2},{1,3},{2,0},{3,1},{4,6},{5,7},{6,4},{7,5},{8,10},{9,11},{10,... | collective-permute-start | bytes 1179656 | tf_op jit(solution)/shard_map/ppermute | solution.py:786
  161.4 10.1 %collective-permute-start.47 = (bf16[128,768]{1,0:T(8,128)(2,1)}, bf16[128,768]{1,0:T(8,128)(2,1)S(1)}, u32[]{:S(2)}, u32[]{:S(2)}) collective-permute-start(bf16[128,768]{1,0:T(8,128)(2,1)} %get-tuple-element.383), channel_id=1, source_target_pairs={{0,2},{1,3},{2,0},{3,1},{4,6},{5,7},{6,4},{7,5},{8,10},{9,11},{10,... | collective-permute-start | bytes 589832 | tf_op jit(solution)/shard_map/ppermute | solution.py:786
  161.9 10.4 %collective-permute-start.48 = (bf16[128,768]{1,0:T(8,128)(2,1)}, bf16[128,768]{1,0:T(8,128)(2,1)S(1)}, u32[]{:S(2)}, u32[]{:S(2)}) collective-permute-start(bf16[128,768]{1,0:T(8,128)(2,1)} %get-tuple-element.384), channel_id=1, source_target_pairs={{0,8},{1,9},{2,10},{3,11},{4,12},{5,13},{6,14},{7,15},{8,0},{9,1},... | collective-permute-start | bytes 589832 | tf_op jit(solution)/shard_map/ppermute | solution.py:786
  162.7 9.6 %collective-permute-start.49 = (bf16[128,768]{1,0:T(8,128)(2,1)}, bf16[128,768]{1,0:T(8,128)(2,1)S(1)}, u32[]{:S(2)}, u32[]{:S(2)}) collective-permute-start(bf16[128,768]{1,0:T(8,128)(2,1)} %get-tuple-element.385), channel_id=1, source_target_pairs={{0,16},{1,17},{2,18},{3,19},{4,20},{5,21},{6,22},{7,23},{8,24},{9,... | collective-permute-start | bytes 589832 | tf_op jit(solution)/shard_map/ppermute | solution.py:786
  170.2 7.8 %collective-permute-start.24 = (bf16[160,768]{1,0:T(8,128)(2,1)}, bf16[160,768]{1,0:T(8,128)(2,1)S(1)}, u32[]{:S(2)}, u32[]{:S(2)}) collective-permute-start(bf16[160,768]{1,0:T(8,128)(2,1)} %get-tuple-element.314), channel_id=1, source_target_pairs={{0,16},{1,17},{2,18},{3,19},{4,20},{5,21},{6,22},{7,23},{8,24},{9,... | collective-permute-start | bytes 737288 | tf_op jit(solution)/shard_map/ppermute | solution.py:786
  171.1 6.9 %collective-permute-start.25 = (bf16[128,768]{1,0:T(8,128)(2,1)}, bf16[128,768]{1,0:T(8,128)(2,1)S(1)}, u32[]{:S(2)}, u32[]{:S(2)}) collective-permute-start(bf16[128,768]{1,0:T(8,128)(2,1)} %get-tuple-element.315), channel_id=1, source_target_pairs={{0,2},{1,3},{2,0},{3,1},{4,6},{5,7},{6,4},{7,5},{8,10},{9,11},{10,... | collective-permute-start | bytes 589832 | tf_op jit(solution)/shard_map/ppermute | solution.py:786
  171.5 6.4 %collective-permute-start.26 = (bf16[128,768]{1,0:T(8,128)(2,1)}, bf16[128,768]{1,0:T(8,128)(2,1)S(1)}, u32[]{:S(2)}, u32[]{:S(2)}) collective-permute-start(bf16[128,768]{1,0:T(8,128)(2,1)} %get-tuple-element.316), channel_id=1, source_target_pairs={{0,8},{1,9},{2,10},{3,11},{4,12},{5,13},{6,14},{7,15},{8,0},{9,1},... | collective-permute-start | bytes 589832 | tf_op jit(solution)/shard_map/ppermute | solution.py:786
  175.4 18.4 %collective-permute-start.50 = (bf16[192,768]{1,0:T(8,128)(2,1)}, bf16[192,768]{1,0:T(8,128)(2,1)S(1)}, u32[]{:S(2)}, u32[]{:S(2)}) collective-permute-start(bf16[192,768]{1,0:T(8,128)(2,1)} %get-tuple-element.393), channel_id=1, source_target_pairs={{0,4},{1,5},{2,6},{3,7},{4,0},{5,1},{6,2},{7,3},{8,12},{9,13},{10,... | collective-permute-start | bytes 884744 | tf_op jit(solution)/shard_map/ppermute | solution.py:786
  181.1 7.6 %collective-permute-start.27 = (bf16[96,768]{1,0:T(8,128)(2,1)}, bf16[96,768]{1,0:T(8,128)(2,1)S(1)}, u32[]{:S(2)}, u32[]{:S(2)}) collective-permute-start(bf16[96,768]{1,0:T(8,128)(2,1)} %get-tuple-element.328), channel_id=1, source_target_pairs={{0,2},{1,3},{2,0},{3,1},{4,6},{5,7},{6,4},{7,5},{8,10},{9,11},{10,... | collective-permute-start | bytes 442376 | tf_op jit(solution)/shard_map/ppermute | solution.py:786
  182.7 4.8 %collective-permute-start.28 = (bf16[64,768]{1,0:T(8,128)(2,1)}, bf16[64,768]{1,0:T(8,128)(2,1)S(1)}, u32[]{:S(2)}, u32[]{:S(2)}) collective-permute-start(bf16[64,768]{1,0:T(8,128)(2,1)} %get-tuple-element.329), channel_id=1, source_target_pairs={{0,8},{1,9},{2,10},{3,11},{4,12},{5,13},{6,14},{7,15},{8,0},{9,1},... | collective-permute-start | bytes 294920 | tf_op jit(solution)/shard_map/ppermute | solution.py:786
  183.9 4.8 %collective-permute-start.29 = (bf16[64,768]{1,0:T(8,128)(2,1)}, bf16[64,768]{1,0:T(8,128)(2,1)S(1)}, u32[]{:S(2)}, u32[]{:S(2)}) collective-permute-start(bf16[64,768]{1,0:T(8,128)(2,1)} %get-tuple-element.330), channel_id=1, source_target_pairs={{0,16},{1,17},{2,18},{3,19},{4,20},{5,21},{6,22},{7,23},{8,24},{9,... | collective-permute-start | bytes 294920 | tf_op jit(solution)/shard_map/ppermute | solution.py:786
  191.4 16.3 %collective-permute-start.30 = (bf16[128,768]{1,0:T(8,128)(2,1)}, bf16[128,768]{1,0:T(8,128)(2,1)S(1)}, u32[]{:S(2)}, u32[]{:S(2)}) collective-permute-start(bf16[128,768]{1,0:T(8,128)(2,1)} %get-tuple-element.340), channel_id=1, source_target_pairs={{0,4},{1,5},{2,6},{3,7},{4,0},{5,1},{6,2},{7,3},{8,12},{9,13},{10,... | collective-permute-start | bytes 589832 | tf_op jit(solution)/shard_map/ppermute | solution.py:786
  196.3 23.5 %collective-permute-start.51 = (bf16[192,768]{1,0:T(8,128)(2,1)}, bf16[192,768]{1,0:T(8,128)(2,1)S(1)}, u32[]{:S(2)}, u32[]{:S(2)}) collective-permute-start(bf16[192,768]{1,0:T(8,128)(2,1)} %total.3.refs_0_), channel_id=1, source_target_pairs={{0,4},{1,5},{2,6},{3,7},{4,0},{5,1},{6,2},{7,3},{8,12},{9,13},{10,... | collective-permute-start | bytes 884744 | tf_op jit(solution)/shard_map/ppermute | solution.py:786
  210.1 7.4 %collective-permute-start.31 = (bf16[96,768]{1,0:T(8,128)(2,1)}, bf16[96,768]{1,0:T(8,128)(2,1)S(1)}, u32[]{:S(2)}, u32[]{:S(2)}) collective-permute-start(bf16[96,768]{1,0:T(8,128)(2,1)} %get-tuple-element.347.refs_0_), channel_id=1, source_target_pairs={{0,4},{1,5},{2,6},{3,7},{4,0},{5,1},{6,2},{7,3},{8,12},{9,13},{10,... | collective-permute-start | bytes 442376 | tf_op jit(solution)/shard_map/ppermute | solution.py:786
  219.8 8.0 %collective-permute-start.32 = (bf16[64,768]{1,0:T(8,128)(2,1)}, bf16[64,768]{1,0:T(8,128)(2,1)S(1)}, u32[]{:S(2)}, u32[]{:S(2)}) collective-permute-start(bf16[64,768]{1,0:T(8,128)(2,1)} %get-tuple-element.353.refs_0_), channel_id=1, source_target_pairs={{0,2},{1,3},{2,0},{3,1},{4,6},{5,7},{6,4},{7,5},{8,10},{9,11},{10,... | collective-permute-start | bytes 294920 | tf_op jit(solution)/shard_map/ppermute | solution.py:786
  222.5 15.4 %collective-permute-start.52 = (bf16[128,768]{1,0:T(8,128)(2,1)}, bf16[128,768]{1,0:T(8,128)(2,1)S(1)}, u32[]{:S(2)}, u32[]{:S(2)}) collective-permute-start(bf16[128,768]{1,0:T(8,128)(2,1)} %get-tuple-element.401.refs_0_), channel_id=1, source_target_pairs={{0,2},{1,3},{2,0},{3,1},{4,6},{5,7},{6,4},{7,5},{8,10},{9,11},{10,... | collective-permute-start | bytes 589832 | tf_op jit(solution)/shard_map/ppermute | solution.py:786
  224.5 13.4 %collective-permute-start.53 = (bf16[128,768]{1,0:T(8,128)(2,1)}, bf16[128,768]{1,0:T(8,128)(2,1)S(1)}, u32[]{:S(2)}, u32[]{:S(2)}) collective-permute-start(bf16[128,768]{1,0:T(8,128)(2,1)} %get-tuple-element.402.refs_1_), channel_id=1, source_target_pairs={{0,8},{1,9},{2,10},{3,11},{4,12},{5,13},{6,14},{7,15},{8,0},{9,1},... | collective-permute-start | bytes 589832 | tf_op jit(solution)/shard_map/ppermute | solution.py:786
  225.3 12.6 %collective-permute-start.54 = (bf16[128,768]{1,0:T(8,128)(2,1)}, bf16[128,768]{1,0:T(8,128)(2,1)S(1)}, u32[]{:S(2)}, u32[]{:S(2)}) collective-permute-start(bf16[128,768]{1,0:T(8,128)(2,1)} %get-tuple-element.403.refs_2_), channel_id=1, source_target_pairs={{0,16},{1,17},{2,18},{3,19},{4,20},{5,21},{6,22},{7,23},{8,24},{9,... | collective-permute-start | bytes 589832 | tf_op jit(solution)/shard_map/ppermute | solution.py:786
  226.5 4.9 %collective-permute-start.33 = (bf16[64,768]{1,0:T(8,128)(2,1)}, bf16[64,768]{1,0:T(8,128)(2,1)S(1)}, u32[]{:S(2)}, u32[]{:S(2)}) collective-permute-start(bf16[64,768]{1,0:T(8,128)(2,1)} %get-tuple-element.354.refs_1_), channel_id=1, source_target_pairs={{0,8},{1,9},{2,10},{3,11},{4,12},{5,13},{6,14},{7,15},{8,0},{9,1},... | collective-permute-start | bytes 294920 | tf_op jit(solution)/shard_map/ppermute | solution.py:786
  227.8 5.9 %collective-permute-start.34 = (bf16[64,768]{1,0:T(8,128)(2,1)}, bf16[64,768]{1,0:T(8,128)(2,1)S(1)}, u32[]{:S(2)}, u32[]{:S(2)}) collective-permute-start(bf16[64,768]{1,0:T(8,128)(2,1)} %get-tuple-element.355.refs_2_), channel_id=1, source_target_pairs={{0,16},{1,17},{2,18},{3,19},{4,20},{5,21},{6,22},{7,23},{8,24},{9,... | collective-permute-start | bytes 294920 | tf_op jit(solution)/shard_map/ppermute | solution.py:786
  236.4 9.3 %collective-permute-start.35 = (bf16[128,768]{1,0:T(8,128)(2,1)}, bf16[128,768]{1,0:T(8,128)(2,1)S(1)}, u32[]{:S(2)}, u32[]{:S(2)}) collective-permute-start(bf16[128,768]{1,0:T(8,128)(2,1)} %get-tuple-element.363.refs_0_), channel_id=1, source_target_pairs={{0,16},{1,17},{2,18},{3,19},{4,20},{5,21},{6,22},{7,23},{8,24},{9,... | collective-permute-start | bytes 589832 | tf_op jit(solution)/shard_map/ppermute | solution.py:786
  241.7 21.6 %collective-permute-start.55 = (bf16[256,768]{1,0:T(8,128)(2,1)}, bf16[256,768]{1,0:T(8,128)(2,1)S(1)}, u32[]{:S(2)}, u32[]{:S(2)}) collective-permute-start(bf16[256,768]{1,0:T(8,128)(2,1)} %get-tuple-element.410.refs_0_), channel_id=1, source_target_pairs={{0,16},{1,17},{2,18},{3,19},{4,20},{5,21},{6,22},{7,23},{8,24},{9,... | collective-permute-start | bytes 1179656 | tf_op jit(solution)/shard_map/ppermute | solution.py:786
  242.3 24.3 %collective-permute-start.56 = (bf16[256,768]{1,0:T(8,128)(2,1)}, bf16[256,768]{1,0:T(8,128)(2,1)S(1)}, u32[]{:S(2)}, u32[]{:S(2)}) collective-permute-start(bf16[256,768]{1,0:T(8,128)(2,1)} %get-tuple-element.411.refs_1_), channel_id=1, source_target_pairs={{0,2},{1,3},{2,0},{3,1},{4,6},{5,7},{6,4},{7,5},{8,10},{9,11},{10,... | collective-permute-start | bytes 1179656 | tf_op jit(solution)/shard_map/ppermute | solution.py:786
  242.3 24.4 %collective-permute-start.57 = (bf16[256,768]{1,0:T(8,128)(2,1)}, bf16[256,768]{1,0:T(8,128)(2,1)S(1)}, u32[]{:S(2)}, u32[]{:S(2)}) collective-permute-start(bf16[256,768]{1,0:T(8,128)(2,1)} %get-tuple-element.412.refs_2_), channel_id=1, source_target_pairs={{0,8},{1,9},{2,10},{3,11},{4,12},{5,13},{6,14},{7,15},{8,0},{9,1},... | collective-permute-start | bytes 1179656 | tf_op jit(solution)/shard_map/ppermute | solution.py:786
  243.7 8.7 %collective-permute-start.36 = (bf16[128,768]{1,0:T(8,128)(2,1)}, bf16[128,768]{1,0:T(8,128)(2,1)S(1)}, u32[]{:S(2)}, u32[]{:S(2)}) collective-permute-start(bf16[128,768]{1,0:T(8,128)(2,1)} %get-tuple-element.364.refs_1_), channel_id=1, source_target_pairs={{0,2},{1,3},{2,0},{3,1},{4,6},{5,7},{6,4},{7,5},{8,10},{9,11},{10,... | collective-permute-start | bytes 589832 | tf_op jit(solution)/shard_map/ppermute | solution.py:786
  245.7 12.0 %collective-permute-start.37 = (bf16[128,768]{1,0:T(8,128)(2,1)}, bf16[128,768]{1,0:T(8,128)(2,1)S(1)}, u32[]{:S(2)}, u32[]{:S(2)}) collective-permute-start(bf16[128,768]{1,0:T(8,128)(2,1)} %get-tuple-element.365.refs_2_), channel_id=1, source_target_pairs={{0,8},{1,9},{2,10},{3,11},{4,12},{5,13},{6,14},{7,15},{8,0},{9,1},... | collective-permute-start | bytes 589832 | tf_op jit(solution)/shard_map/ppermute | solution.py:786
  252.3 18.8 %collective-permute-start.15 = (bf16[256,768]{1,0:T(8,128)(2,1)}, bf16[256,768]{1,0:T(8,128)(2,1)S(1)}, u32[]{:S(2)}, u32[]{:S(2)}) collective-permute-start(bf16[256,768]{1,0:T(8,128)(2,1)} %get-tuple-element.280), channel_id=1, source_target_pairs={{0,8},{8,0},{16,24},{1,9},{9,1},{17,25},{2,10},{10,2},{18,26},{3,1... | collective-permute-start | bytes 1179656 | tf_op jit(solution)/shard_map/ppermute | solution.py:893
  257.7 15.7 %collective-permute-start.16 = (bf16[256,768]{1,0:T(8,128)(2,1)}, bf16[256,768]{1,0:T(8,128)(2,1)S(1)}, u32[]{:S(2)}, u32[]{:S(2)}) collective-permute-start(bf16[256,768]{1,0:T(8,128)(2,1)} %get-tuple-element.281), channel_id=1, source_target_pairs={{0,16},{8,24},{16,0},{1,17},{9,25},{17,1},{2,18},{10,26},{18,2},{3... | collective-permute-start | bytes 1179656 | tf_op jit(solution)/shard_map/ppermute | solution.py:893
  263.3 12.1 %collective-permute-start.17 = (bf16[256,768]{1,0:T(8,128)(2,1)S(1)}, bf16[256,768]{1,0:T(8,128)(2,1)S(1)}, u32[]{:S(2)}, u32[]{:S(2)}) collective-permute-start(bf16[256,768]{1,0:T(8,128)(2,1)S(1)} %copy-done.54), channel_id=1, source_target_pairs={{0,24},{8,16},{16,8},{1,25},{9,17},{17,9},{2,26},{10,18},{18,10},{... | collective-permute-start | bytes 1179656 | tf_op jit(solution)/shard_map/ppermute | solution.py:893
  266.6 12.7 %collective-permute-start.41 = (bf16[256,768]{1,0:T(8,128)(2,1)}, bf16[256,768]{1,0:T(8,128)(2,1)}, u32[]{:S(2)}, u32[]{:S(2)}) collective-permute-start(bf16[256,768]{1,0:T(8,128)(2,1)} %get-tuple-element.372.refs_0_), channel_id=1, source_target_pairs={{0,1},{1,0},{2,3},{3,2},{4,5},{5,4},{6,7},{7,6},{8,9},{9,8},{10,11... | collective-permute-start | bytes 1179656 | tf_op jit(solution)/shard_map/ppermute | solution.py:786
  266.7 18.8 %collective-permute-start.38 = (bf16[256,768]{1,0:T(8,128)(2,1)}, bf16[256,768]{1,0:T(8,128)(2,1)}, u32[]{:S(2)}, u32[]{:S(2)}) collective-permute-start(bf16[256,768]{1,0:T(8,128)(2,1)} %get-tuple-element.372.refs_0_), channel_id=1, source_target_pairs={{0,8},{1,9},{2,10},{3,11},{4,12},{5,13},{6,14},{7,15},{8,0},{9,1},... | collective-permute-start | bytes 1179656 | tf_op jit(solution)/shard_map/ppermute | solution.py:786
  271.1 17.3 %collective-permute-start.39 = (bf16[256,768]{1,0:T(8,128)(2,1)S(1)}, bf16[256,768]{1,0:T(8,128)(2,1)}, u32[]{:S(2)}, u32[]{:S(2)}) collective-permute-start(bf16[256,768]{1,0:T(8,128)(2,1)S(1)} %copy-done.12), channel_id=1, source_target_pairs={{0,16},{1,17},{2,18},{3,19},{4,20},{5,21},{6,22},{7,23},{8,24},{9,... | collective-permute-start | bytes 1179656 | tf_op jit(solution)/shard_map/ppermute | solution.py:786
  274.1 31.6 %collective-permute-start.58 = (bf16[512,768]{1,0:T(8,128)(2,1)}, bf16[512,768]{1,0:T(8,128)(2,1)S(1)}, u32[]{:S(2)}, u32[]{:S(2)}) collective-permute-start(bf16[512,768]{1,0:T(8,128)(2,1)} %get-tuple-element.419.refs_0_), channel_id=1, source_target_pairs={{0,8},{1,9},{2,10},{3,11},{4,12},{5,13},{6,14},{7,15},{8,0},{9,1},... | collective-permute-start | bytes 2359304 | tf_op jit(solution)/shard_map/ppermute | solution.py:786
  276.2 29.6 %collective-permute-start.59 = (bf16[512,768]{1,0:T(8,128)(2,1)}, bf16[512,768]{1,0:T(8,128)(2,1)S(1)}, u32[]{:S(2)}, u32[]{:S(2)}) collective-permute-start(bf16[512,768]{1,0:T(8,128)(2,1)} %get-tuple-element.420.refs_1_), channel_id=1, source_target_pairs={{0,16},{1,17},{2,18},{3,19},{4,20},{5,21},{6,22},{7,23},{8,24},{9,... | collective-permute-start | bytes 2359304 | tf_op jit(solution)/shard_map/ppermute | solution.py:786
  279.3 27.2 %collective-permute-start.60 = (bf16[512,768]{1,0:T(8,128)(2,1)}, bf16[512,768]{1,0:T(8,128)(2,1)}, u32[]{:S(2)}, u32[]{:S(2)}) collective-permute-start(bf16[512,768]{1,0:T(8,128)(2,1)} %get-tuple-element.421.refs_2_), channel_id=1, source_target_pairs={{0,2},{1,3},{2,0},{3,1},{4,6},{5,7},{6,4},{7,5},{8,10},{9,11},{10,... | collective-permute-start | bytes 2359304 | tf_op jit(solution)/shard_map/ppermute | solution.py:786
  285.5 19.7 %collective-permute-start.40 = (bf16[256,768]{1,0:T(8,128)(2,1)}, bf16[256,768]{1,0:T(8,128)(2,1)}, u32[]{:S(2)}, u32[]{:S(2)}) collective-permute-start(bf16[256,768]{1,0:T(8,128)(2,1)} %get-tuple-element.374.refs_2_), channel_id=1, source_target_pairs={{0,2},{1,3},{2,0},{3,1},{4,6},{5,7},{6,4},{7,5},{8,10},{9,11},{10,... | collective-permute-start | bytes 1179656 | tf_op jit(solution)/shard_map/ppermute | solution.py:786
  288.4 16.8 %collective-permute-start.42 = (bf16[256,768]{1,0:T(8,128)(2,1)S(1)}, bf16[256,768]{1,0:T(8,128)(2,1)S(1)}, u32[]{:S(2)}, u32[]{:S(2)}) collective-permute-start(bf16[256,768]{1,0:T(8,128)(2,1)S(1)} %copy-done.12), channel_id=1, source_target_pairs={{0,1},{1,0},{2,3},{3,2},{4,5},{5,4},{6,7},{7,6},{8,9},{9,8},{10,11... | collective-permute-start | bytes 1179656 | tf_op jit(solution)/shard_map/ppermute | solution.py:786
  305.2 5.0 %collective-permute-start.61 = (bf16[512,768]{1,0:T(8,128)(2,1)}, bf16[512,768]{1,0:T(8,128)(2,1)}, u32[]{:S(2)}, u32[]{:S(2)}) collective-permute-start(bf16[512,768]{1,0:T(8,128)(2,1)} %get-tuple-element.419.refs_0_), channel_id=1, source_target_pairs={{0,1},{1,0},{2,3},{3,2},{4,5},{5,4},{6,7},{7,6},{8,9},{9,8},{10,11... | collective-permute-start | bytes 2359304 | tf_op jit(solution)/shard_map/ppermute | solution.py:786
  306.5 3.6 %collective-permute-start.46 = (bf16[256,768]{1,0:T(8,128)(2,1)}, bf16[256,768]{1,0:T(8,128)(2,1)}, u32[]{:S(2)}, u32[]{:S(2)}) collective-permute-start(bf16[256,768]{1,0:T(8,128)(2,1)} %collective-permute-done.40.refs_5_), channel_id=1, source_target_pairs={{0,1},{1,0},{2,3},{3,2},{4,5},{5,4},{6,7},{7,6},{8,9},{9,8},{10,11... | collective-permute-start | bytes 1179656 | tf_op jit(solution)/shard_map/ppermute | solution.py:786
  308.4 13.2 %collective-permute-start.62 = (bf16[512,768]{1,0:T(8,128)(2,1)S(1)}, bf16[512,768]{1,0:T(8,128)(2,1)}, u32[]{:S(2)}, u32[]{:S(2)}) collective-permute-start(bf16[512,768]{1,0:T(8,128)(2,1)S(1)} %copy-done), channel_id=1, source_target_pairs={{0,1},{1,0},{2,3},{3,2},{4,5},{5,4},{6,7},{7,6},{8,9},{9,8},{10,11... | collective-permute-start | bytes 2359304 | tf_op jit(solution)/shard_map/ppermute | solution.py:786
  309.0 12.6 %collective-permute-start.63 = (bf16[512,768]{1,0:T(8,128)(2,1)S(1)}, bf16[512,768]{1,0:T(8,128)(2,1)}, u32[]{:S(2)}, u32[]{:S(2)}) collective-permute-start(bf16[512,768]{1,0:T(8,128)(2,1)S(1)} %copy-done.1), channel_id=1, source_target_pairs={{0,1},{1,0},{2,3},{3,2},{4,5},{5,4},{6,7},{7,6},{8,9},{9,8},{10,11... | collective-permute-start | bytes 2359304 | tf_op jit(solution)/shard_map/ppermute | solution.py:786
  309.5 12.1 %collective-permute-start.64 = (bf16[512,768]{1,0:T(8,128)(2,1)S(1)}, bf16[512,768]{1,0:T(8,128)(2,1)}, u32[]{:S(2)}, u32[]{:S(2)}) collective-permute-start(bf16[512,768]{1,0:T(8,128)(2,1)S(1)} %collective-permute-done.58.refs_3_), channel_id=1, source_target_pairs={{0,1},{1,0},{2,3},{3,2},{4,5},{5,4},{6,7},{7,6},{8,9},{9,8},{10,11... | collective-permute-start | bytes 2359304 | tf_op jit(solution)/shard_map/ppermute | solution.py:786
  310.1 11.5 %collective-permute-start.65 = (bf16[512,768]{1,0:T(8,128)(2,1)S(1)}, bf16[512,768]{1,0:T(8,128)(2,1)}, u32[]{:S(2)}, u32[]{:S(2)}) collective-permute-start(bf16[512,768]{1,0:T(8,128)(2,1)S(1)} %collective-permute-done.59.refs_4_), channel_id=1, source_target_pairs={{0,1},{1,0},{2,3},{3,2},{4,5},{5,4},{6,7},{7,6},{8,9},{9,8},{10,11... | collective-permute-start | bytes 2359304 | tf_op jit(solution)/shard_map/ppermute | solution.py:786
  310.2 11.4 %collective-permute-start.66 = (bf16[512,768]{1,0:T(8,128)(2,1)}, bf16[512,768]{1,0:T(8,128)(2,1)}, u32[]{:S(2)}, u32[]{:S(2)}) collective-permute-start(bf16[512,768]{1,0:T(8,128)(2,1)} %collective-permute-done.60.refs_5_), channel_id=1, source_target_pairs={{0,1},{1,0},{2,3},{3,2},{4,5},{5,4},{6,7},{7,6},{8,9},{9,8},{10,11... | collective-permute-start | bytes 2359304 | tf_op jit(solution)/shard_map/ppermute | solution.py:786
  (63 other events, 419.1 us)

commit v4 on v3

--- a/solution.py
+++ b/solution.py
@@ -311,11 +311,11 @@
     return high, (value - high.astype(F32)).astype(BF)
 
 
-def attn_bwd_body(sc, q_r, k_r, v_r, g_r, lse, wq, wk, wv, base, da_r, stat, lo, *refs, first, last):
+def attn_bwd_body(sc, q_r, k_r, v_r, g_r, lse, wq, wk, wv, base, da_r, stat, lo, *refs, first, last, deps):
     if first:
         dq_o, dk_o, dv_o, one_o, two_o, small_o, acc = refs
     else:
-        dq_o, dk_o, dv_o, one_o, two_o, small_o, terms_o, i0, i1, i2, i3, acc = refs[5:]
+        dq_o, dk_o, dv_o, one_o, two_o, small_o, terms_o, i0, i1, i2, i3, acc = refs[5 + deps:]
     step = pl.program_id(0)
     steps = pl.num_programs(0)
     rows, wide = q_r.shape
@@ -394,7 +394,7 @@
             terms_o[16:32, :] = rest
 
 
-def attn_bwd(sc, q, k, v, g, lse, qkv_w, base, dattn, stat, lo, into):
+def attn_bwd(sc, q, k, v, g, lse, qkv_w, base, dattn, stat, lo, into, deps=()):
     rows, width = q.shape
     pairs = HEADS // 2
     wide = width // pairs
@@ -411,7 +411,7 @@
                   pl.BlockSpec((width, wide), lambda i, s: (0, pairs + off + i)),
                   pl.BlockSpec((width, wide), lambda i, s: (0, 2 * pairs + off + i)),
                   full((rows, width)), col, full((16, width)), full((rows, width))]
-        + [pl.BlockSpec(memory_space=pl.ANY)] * len(into),
+        + [pl.BlockSpec(memory_space=pl.ANY)] * (len(into) + len(deps)),
         out_specs=[col] * 5 + [full((16, width))]
         + ([full((rows, width))] if first else [full((32, width))] + [block] * 4),
         scratch_shapes=[] if first else [pltpu.VMEM((rows, width), F32)],
@@ -423,7 +423,7 @@
     else:
         outs += [shape_of((32, width), BF)] + [shape_of((rows // 2, width), BF)] * 4
     return pl.pallas_call(
-        functools.partial(attn_bwd_body, first=first, last=not first),
+        functools.partial(attn_bwd_body, first=first, last=not first, deps=len(deps)),
         grid_spec=grid,
         out_shape=outs,
         input_output_aliases={13 + i: i for i in range(len(into))},
@@ -431,7 +431,7 @@
         cost_estimate=cost(3 * rows * width * width + 5 * rows * rows * width, 6 * rows * width + 3 * width * width,
                            HEADS * rows * rows // 2),
         name="attn_bwd",
-    )(sc, q, k, v, g, lse, qkv_w, qkv_w, qkv_w, base, dattn, stat, lo, *into)
+    )(sc, q, k, v, g, lse, qkv_w, qkv_w, qkv_w, base, dattn, stat, lo, *into, *deps)
 
 
 def cut_out(sc, buf, u, sends, keeps, sems):
@@ -447,7 +447,7 @@
     return copies
 
 
-def wgrad_body(sc, act_h, send_h, peer_h, hlc, hlcp, dup_h, dupp_h, s0, s1, s2, k0, k1, k2,
+def wgrad_body(sc, act_h, send_h, peer_h, hlc, hlcp, dup_h, dupp_h, _, s0, s1, s2, k0, k1, k2,
                act, actp, dffn, low, lowp, dup, dupp, buf, sem_in, sem_out):
     side = act.shape[1]
     width = dffn.shape[1]
@@ -478,7 +478,7 @@
     wait(copies)
 
 
-def wgrad(sc, act, send, peer, hlc, hlcp, dup, dupp):
+def wgrad(sc, act, send, peer, hlc, hlcp, dup, dupp, dep):
     rows, side = act.shape
     width = hlc.shape[1] // 3
     units = 4
@@ -487,7 +487,7 @@
     part = shape_of((units * half, width), BF)
     return pl.pallas_call(
         wgrad_body,
-        in_specs=[pl.BlockSpec(memory_space=pltpu.SMEM)] + [anywhere] * 7,
+        in_specs=[pl.BlockSpec(memory_space=pltpu.SMEM)] + [anywhere] * 8,
         out_specs=[anywhere] * 6,
         out_shape=[part] * 6,
         scratch_shapes=[pltpu.VMEM((rows, side), BF), pltpu.VMEM((rows, side + width), BF), pltpu.VMEM((rows, width), BF),
@@ -497,10 +497,10 @@
         compiler_params=params(),
         cost_estimate=cost(16 * rows * width * width, 26 * rows * width),
         name="wgrad",
-    )(sc, act, send, peer, hlc, hlcp, dup, dupp)
-
-
-def wgrad_mix_body(sc, hlc, hlcp, dq_h, dk_h, dv_h, da_h, p1_h, p2_h, terms, small, s0, s1, s2, k0, k1, k2, small_o,
+    )(sc, act, send, peer, hlc, hlcp, dup, dupp, dep)
+
+
+def wgrad_mix_body(sc, hlc, hlcp, dq_h, dk_h, dv_h, da_h, p1_h, p2_h, terms, small, _, s0, s1, s2, k0, k1, k2, small_o,
                    l1, l1p, l2, l2p, r1, r1p, r2, r2p, buf, sem_in, sem_out):
     width = l1.shape[1]
     core = sc[S_CORE]
@@ -535,7 +535,7 @@
     wait(copies)
 
 
-def wgrad_mix(sc, hlc, hlcp, dq, dk, dv, da, p1, p2, terms, small):
+def wgrad_mix(sc, hlc, hlcp, dq, dk, dv, da, p1, p2, terms, small, dep):
     rows, width = dq.shape
     units = 2
     half = width // COLORS // 2
@@ -544,7 +544,7 @@
     part = shape_of((units * half, width), BF)
     return pl.pallas_call(
         wgrad_mix_body,
-        in_specs=[pl.BlockSpec(memory_space=pltpu.SMEM)] + [anywhere] * 8 + [vmem] * 2,
+        in_specs=[pl.BlockSpec(memory_space=pltpu.SMEM)] + [anywhere] * 8 + [vmem] * 2 + [anywhere],
         out_specs=[anywhere] * 6 + [vmem],
         out_shape=[part] * 6 + [shape_of(small.shape, F32)],
         scratch_shapes=[pltpu.VMEM((rows, width), BF)] * 8 + [pltpu.VMEM((units, width, width), BF),
@@ -552,16 +552,16 @@
         compiler_params=params(),
         cost_estimate=cost(8 * rows * width * width, 20 * rows * width),
         name="wgrad_mix",
-    )(sc, hlc, hlcp, dq, dk, dv, da, p1, p2, terms, small)
+    )(sc, hlc, hlcp, dq, dk, dv, da, p1, p2, terms, small, dep)
 
 
 def add_rows(one, two):
     return (one.astype(F32) + two.astype(F32)).astype(BF)
 
 
-def fold_body(sc, *refs, units, stage, small):
+def fold_body(sc, *refs, units, stage, small, deps):
     keeps, gots = refs[:COLORS], refs[COLORS:2 * COLORS]
-    outs = refs[2 * COLORS + small:]
+    outs = refs[2 * COLORS + small + deps:]
     rows = keeps[0].shape[0] // units
     half = rows // 2
     merged = stage == 2
@@ -585,7 +585,7 @@
         send[at + 16:at + 32, :] = rest
 
 
-def fold(sc, keeps, gots, small, units, stage):
+def fold(sc, keeps, gots, small, units, stage, deps=()):
     rows, width = keeps[0].shape
     vmem = pl.BlockSpec(memory_space=pltpu.VMEM)
     has = small is not None
@@ -600,14 +600,14 @@
         args.append(small)
         outs.append(shape_of(small.shape, F32))
     got = pl.pallas_call(
-        functools.partial(fold_body, units=units, stage=stage, small=has),
+        functools.partial(fold_body, units=units, stage=stage, small=has, deps=len(deps)),
         out_shape=outs,
-        in_specs=[pl.BlockSpec(memory_space=pltpu.SMEM)] + [vmem] * len(args),
+        in_specs=[pl.BlockSpec(memory_space=pltpu.SMEM)] + [vmem] * len(args) + [pl.BlockSpec(memory_space=pl.ANY)] * len(deps),
         out_specs=[vmem] * len(outs),
         compiler_params=params(),
         cost_estimate=cost(6 * rows * width, 18 * rows * width),
         name="fold",
-    )(sc, *args)
+    )(sc, *args, *deps)
     if has:
         small = got[-1]
     if stage == 2:
@@ -615,15 +615,16 @@
     return got[:COLORS], got[COLORS:2 * COLORS], small
 
 
-def total_body(keep, got, *refs):
+def total_body(keep, got, *refs, small):
     rows = keep.shape[0]
-    refs[-1 if len(refs) == 1 else 1][...] = add_rows(keep[...], got[0:rows, :])
-    if len(refs) > 1:
-        refs[2][...] = refs[0][...] + (
+    out = refs[-2] if small else refs[-1]
+    out[...] = add_rows(keep[...], got[0:rows, :])
+    if small:
+        refs[-1][...] = refs[0][...] + (
             got[rows:rows + 16, :].astype(F32) + got[rows + 16:rows + 32, :].astype(F32))
 
 
-def total(keep, got, small):
+def total(keep, got, small, deps):
     vmem = pl.BlockSpec(memory_space=pltpu.VMEM)
     args = [keep, got]
     outs = [shape_of(keep.shape, BF)]
@@ -631,20 +632,20 @@
         args.append(small)
         outs.append(shape_of(small.shape, F32))
     res = pl.pallas_call(
-        total_body,
+        functools.partial(total_body, small=small is not None),
         out_shape=outs,
-        in_specs=[vmem] * len(args),
+        in_specs=[vmem] * len(args) + [pl.BlockSpec(memory_space=pl.ANY)] * len(deps),
         out_specs=[vmem] * len(outs),
         compiler_params=params(),
         cost_estimate=cost(keep.size, 6 * keep.size),
         name="total",
-    )(*args)
+    )(*args, *deps)
     return res[0], (res[1] if small is not None else None)
 
 
-def join_body(sc, *refs, units, stage):
+def join_body(sc, *refs, units, stage, deps):
     outs = refs[-COLORS:]
-    n = (len(refs) - COLORS) // 2
+    n = (len(refs) - COLORS - deps) // 2
     owns, gots = refs[:n], refs[n:2 * n]
     rows = outs[0].shape[0] // units
     half = rows // 2
@@ -657,20 +658,42 @@
             outs[c][pl.ds(pl.multiple_of(u * rows + (1 - bit) * half, LEAF), half), :] = got[at:at + half, :]
 
 
-def joined(sc, owns, gots, units, stage):
+def joined(sc, owns, gots, units, stage, deps=()):
     width = owns[0].shape[1]
     rows = 2 * owns[0].shape[0] // (COLORS if len(owns) == 1 else 1)
     vmem = pl.BlockSpec(memory_space=pltpu.VMEM)
     args = list(owns) + list(gots)
     return pl.pallas_call(
-        functools.partial(join_body, units=units, stage=stage),
+        functools.partial(join_body, units=units, stage=stage, deps=len(deps)),
         out_shape=[shape_of((rows, width), BF)] * COLORS,
-        in_specs=[pl.BlockSpec(memory_space=pltpu.SMEM)] + [vmem] * len(args),
+        in_specs=[pl.BlockSpec(memory_space=pltpu.SMEM)] + [vmem] * len(args)
+        + [pl.BlockSpec(memory_space=pl.ANY)] * len(deps),
         out_specs=[vmem] * COLORS,
         compiler_params=params(),
         cost_estimate=cost(rows * width, 12 * rows * width),
         name="join",
-    )(sc, *args)
+    )(sc, *args, *deps)
+
+
+def pack_body(*refs, deps):
+    out = refs[-1]
+    rows = refs[0].shape[0]
+    for c in range(COLORS):
+        out[c * rows:(c + 1) * rows, :] = refs[c][...]
+
+
+def pack(values, deps):
+    rows, width = values[0].shape
+    vmem = pl.BlockSpec(memory_space=pltpu.VMEM)
+    return pl.pallas_call(
+        functools.partial(pack_body, deps=len(deps)),
+        out_shape=shape_of((COLORS * rows, width), BF),
+        in_specs=[vmem] * COLORS + [pl.BlockSpec(memory_space=pl.ANY)] * len(deps),
+        out_specs=vmem,
+        compiler_params=params(),
+        cost_estimate=cost(rows * width, 12 * rows * width),
+        name="pack",
+    )(*values, *deps)
 
 
 def final_body(sc, *refs, mixed):
@@ -705,11 +728,16 @@
                 write(outs[1], owns, gots)
 
 
-def final(sc, mine, theirs, first, kind):
+def final(sc, mine, theirs, first, kind, packed):
     width = mine[0].shape[1]
     half = width // COLORS // 2
     own = pl.BlockSpec((half, width), lambda j, s: (first + jnp.minimum(j, 1), 0))
     far = pl.BlockSpec((half, width), lambda j, s: (first + jnp.maximum(j - 2, 0), 0))
+
+    units = packed.shape[0] // (COLORS * half)
+
+    def far_got(c):
+        return pl.BlockSpec((half, width), lambda j, s: (c * units + first + jnp.maximum(j - 2, 0), 0))
 
     def place(j, s):
         return jnp.where(j < 2, s[S_CORE], 1 - s[S_CORE]) * 2 + j % 2
@@ -726,7 +754,7 @@
     grid = pltpu.PrefetchScalarGridSpec(
         num_scalar_prefetch=1,
         grid=(4,),
-        in_specs=[own] * (2 * COLORS) + [far] * (2 * COLORS),
+        in_specs=[own] * (2 * COLORS) + [far] * COLORS + [far_got(c) for c in range(COLORS)],
         out_specs=specs,
     )
     return pl.pallas_call(
@@ -736,15 +764,7 @@
         compiler_params=params(),
         cost_estimate=cost(4 * width * width, 24 * width * width),
         name="final",
-    )(sc, *mine, *theirs)
-
-
-def after(token, *values):
-    return lax.optimization_barrier((token,) + values)[1:]
-
-
-def corner(value):
-    return value[:8, :128]
+    )(sc, *mine, *theirs, *([packed] * COLORS))
 
 
 def body(
@@ -822,39 +842,27 @@
     send_p = core_swap(send)
     dup_p = core_swap(dup_send)
     *part, base = attn_bwd(sc, q, k, v, dctx, lse, qkv_weight, dres, dattn, stat, lo, ())
-    send_p, dup_p = after(corner(base), send_p, dup_p)
-    got = wgrad(sc, act, send, send_p, hlc, hlc_p, dup, dup_p)
+    got = wgrad(sc, act, send, send_p, hlc, hlc_p, dup, dup_p, base)
     sends1, keeps1 = got[:COLORS], got[COLORS:]
     gots1 = over(sends1, 0)
-    (base,) = after(corner(keeps1[0]), base)
     dq, dk, dv, one, two, small, terms, i0, i1, i2, i3 = attn_bwd(
-        sc, q, k, v, dctx, lse, qkv_weight, base, dattn, part[5], lo, tuple(part[:5]))
+        sc, q, k, v, dctx, lse, qkv_weight, base, dattn, part[5], lo, tuple(part[:5]), (keeps1[0],))
     one_p, two_p, terms_p = core_swap(one), core_swap(two), core_swap(terms)
-    token = corner(terms)
-
-    keeps1 = after(token, *keeps1, *gots1)
-    keeps1, gots1 = keeps1[:COLORS], keeps1[COLORS:]
-    sends1, keeps1, _ = fold(sc, keeps1, gots1, None, 4, 0)
+    sends1, keeps1, _ = fold(sc, keeps1, gots1, None, 4, 0, (terms,))
     gots1 = over(sends1, 1)
-    one_p, two_p, terms_p = after(corner(keeps1[0]), one_p, two_p, terms_p)
-    *got, small = wgrad_mix(sc, hlc, hlc_p, dq, dk, dv, dattn, one_p, two_p, terms_p, small)
+    *got, small = wgrad_mix(sc, hlc, hlc_p, dq, dk, dv, dattn, one_p, two_p, terms_p, small, keeps1[0])
     sends2, keeps2 = list(got[:COLORS]), got[COLORS:]
     high, rest = split_terms(small)
     sends2[0] = jnp.concatenate([sends2[0], high, rest], 0)
     gots2 = over(sends2, 0)
-    token = corner(keeps2[0])
+    token = keeps2[0]
 
     def step(kind, token, keeps, gots, small, units, stage):
-        held = [] if small is None else [small]
-        vals = after(token, *keeps, *gots, *held)
-        n = len(keeps)
-        keeps, gots = vals[:n], vals[n:2 * n]
-        small = vals[2 * n] if held else None
         if kind == "fold":
             if stage < 3:
-                sends, keeps, small = fold(sc, keeps, gots, small, units, stage)
+                sends, keeps, small = fold(sc, keeps, gots, small, units, stage, (token,))
             else:
-                whole, small = total(keeps[0], gots[0], small)
+                whole, small = total(keeps[0], gots[0], small, (token,))
                 for mask in later:
                     if small is None:
                         whole = add_rows(whole, permute(whole, mask))
@@ -866,8 +874,9 @@
                         small = small + (more[size:size + 16].astype(F32) + more[size + 16:].astype(F32))
                 sends = keeps = [whole]
         else:
-            sends = keeps = joined(sc, keeps, gots, units, stage)
-        return sends, keeps, small, corner(keeps[0])
+            deps = (token,) + (tuple(back[1:]) if (units, stage) == (4, 3) else ())
+            sends = keeps = joined(sc, keeps, gots, units, stage, deps)
+        return sends, keeps, small, keeps[0]
 
     plan = [("fold", 1, 1), ("fold", 2, 0), ("fold", 1, 2), ("fold", 2, 1), ("fold", 1, 3), ("fold", 2, 2),
             ("join", 1, 3), ("fold", 2, 3), ("join", 1, 2), ("join", 2, 3), ("join", 1, 1), ("join", 2, 2),
@@ -886,17 +895,14 @@
         if kind == "join" and stage == 1:
             far[piece] = [core_swap(value) for value in keeps]
         if at == 0:
-            blocks = after(token, i0, i1, i2, i3)
-            back = [blocks[0]]
+            blocks = [i0, i1, i2, i3]
+            back = [i0]
             for k_at in range(1, nseq):
                 pairs = [(i, i ^ k_at) for i in range(nseq) if i < count]
                 back.append(lax.ppermute(blocks[k_at], "seq", pairs))
 
     keeps1, gots1 = state[1][:2]
-    vals = after(token, *keeps1, *gots1)
-    keeps1, gots1 = vals[:COLORS], vals[COLORS:]
-    far1 = far[1] + [core_swap(value) for value in gots1]
-    back = after(corner(gots1[0]), *back)
+    packed1 = core_swap(pack(gots1, (token,)))
     shown = []
     for p in range(count):
         value = back[0]
@@ -906,13 +912,11 @@
     layer_out = jnp.stack([value[:local] for value in shown])
     input_grad = jnp.stack([value[local:] for value in shown])
     mine1 = list(keeps1) + list(gots1)
-    (down_grad,) = final(sc, mine1, far1, 0, "rows")
-    (up_grad,) = final(sc, mine1, far1, 2, "cols")
+    (down_grad,) = final(sc, mine1, far[1], 0, "rows", packed1)
+    (up_grad,) = final(sc, mine1, far[1], 2, "cols", packed1)
     keeps2, gots2, small, _ = state[2]
-    vals = after(corner(up_grad), corner(down_grad), *keeps2, *gots2)[1:]
-    keeps2, gots2 = vals[:COLORS], vals[COLORS:]
-    far2 = far[2] + [core_swap(value) for value in gots2]
-    qkv_grad, out_grad = final(sc, list(keeps2) + list(gots2), far2, 0, "mixed")
+    packed2 = core_swap(pack(gots2, (down_grad, up_grad)))
+    qkv_grad, out_grad = final(sc, list(keeps2) + list(gots2), far[2], 0, "mixed", packed2)
     return (
         layer_out,
         input_grad,

time: 339 us -> 330 us (0.973)
  waiting for transfers between devices: 75.7 us -> 55.5 us
  local copies, waits for them, and re-layouts: 28.3 us -> 39.1 us
  starting transfers between devices: 82.5 us -> 75.5 us
  Pallas kernels: 144 us -> 149 us
    ppermute x58 -> x54, waiting for transfers between devices: 75.7 us -> 55.5 us  [permute(): lax.ppermute(value, ('seq', 'dp'), [(i, i ^ mask) for i in range(members)])]
    unnamed x120 -> x148, local copies, waits for them, and re-layouts: 13 us -> 21.9 us
    pallas_call x8 -> x10, Pallas kernels: 17.2 us -> 22.8 us  [the longest x6 13.7 us: joined(): pl.pallas_call(functools.partial(join_body, units=units, stage=stage, dep...]
    ppermute x58 -> x54, starting transfers between devices: 54 us -> 48.5 us  [permute(): lax.ppermute(value, ('seq', 'dp'), [(i, i ^ mask) for i in range(members)])]
  transfers between devices with their start and end apart: 67 -> 63, of which waited for: 21 -> 17; matrix products, arithmetic and copies ran while one was open for 5% -> 6% of each run, Pallas kernels for 29% -> 37%
where the time goes in v4:
time: 330 us; the launch traced here: 329 us
  Pallas kernels  149 us (45%)
  starting transfers between devices  75.5 us (23%)
  waiting for transfers between devices  55.5 us (17%)
  local copies, waits for them, and re-layouts  39.1 us (12%)
  other arithmetic  7 us (2%)
    ppermute x54, waiting for transfers between devices, permute(): lax.ppermute(value, ('seq', 'dp'), [(i, i ^ mask) for i in range(members)])  55.5 us
    ppermute x54, starting transfers between devices, permute(): lax.ppermute(value, ('seq', 'dp'), [(i, i ^ mask) for i in range(members)])  48.5 us
    pallas_call x2, Pallas kernels, attn_bwd(): pl.pallas_call(functools.partial(attn_bwd_body, first=first, last=not fir...  27 us
    pallas_call x1, Pallas kernels, ffn(): pl.pallas_call(ffn_body, in_specs=[smem] + [anywhere] * 5 + [vmem] * 11,...  24 us
    pallas_call x3, Pallas kernels, final(): pl.pallas_call(functools.partial(final_body, mixed=len(outs) == 2), grid_...  23.8 us
    unnamed x148, local copies, waits for them, and re-layouts  21.9 us
    ppermute x6, starting transfers between devices, to_holder(): blocks.append(lax.ppermute(parts[k - 1], 'seq', pairs))  18.8 us
    pallas_call x1, Pallas kernels, attn_fwd(): pl.pallas_call(attn_fwd_body, grid_spec=grid, out_shape=[shape_of((rows,...  16.7 us
  transfers between devices with their start and end apart: 63, of which 17 were waited for; matrix products, arithmetic and copies ran while one was open for 6% of the time, Pallas kernels for 37%

profile of v4, /device:TPU:0, one launch (start us, length us, event | category | flops | bytes accessed | tf_op | source)
XLA Modules:
  0.0 328.8 jit_solution(11860352995477111772)
XLA Ops:
  0.7 2.0 dynamic-slice_bitcast_fusion.3
  3.9 7.0 %collective-permute-start = (bf16[128,768]{1,0:T(8,128)(2,1)S(1)}, bf16[128,768]{1,0:T(8,128)(2,1)S(1)}, u32[]{:S(2)}, u32[]{:S(2)}) collective-permute-start(bf16[128,768]{1,0:T(8,128)(2,1)S(1)} %get-tuple-element.243), channel_id=1, source_target_pairs={{0,8},{8,0},{24,16},{1,9},{9,1},{25,17},{2,10},{10,2},{26,18},{3,1... | collective-permute-start | bytes 589832 | tf_op jit(solution)/shard_map/ppermute | solution.py:827
  10.9 1.9 collective-permute-start.1
  25.6 2.1 dynamic-slice_bitcast_fusion
  29.0 4.6 %collective-permute-start.4 = (bf16[128,768]{1,0:T(8,128)(2,1)S(1)}, bf16[128,768]{1,0:T(8,128)(2,1)S(1)}, u32[]{:S(2)}, u32[]{:S(2)}) collective-permute-start(bf16[128,768]{1,0:T(8,128)(2,1)S(1)} %get-tuple-element.239), channel_id=1, source_target_pairs={{0,16},{16,0},{24,8},{1,17},{17,1},{25,9},{2,18},{18,2},{26,10},{3... | collective-permute-start | bytes 589832 | tf_op jit(solution)/shard_map/ppermute | solution.py:827
  33.5 2.7 collective-permute-start.3
  36.3 16.7 %attn_fwd.1 = (bf16[512,2304]{1,0:T(8,128)(2,1)}, bf16[512,768]{1,0:T(8,128)(2,1)}, bf16[512,768]{1,0:T(8,128)(2,1)}, bf16[512,768]{1,0:T(8,128)(2,1)}, f32[16,5...) custom-call(s32[8]{0:T(128)} %stack.56.sc, bf16[128,768]{1,0:T(8,128)(2,1)} %get-tuple-element.120.h0, ...), custom_call_target="tpu_custom_call" | custom-call | flops 3221225472 | bytes 9437184 | tf_op jit(solution)/shard_map/attn_fwd/pallas_call | solution.py:151
  53.9 24.0 %ffn.1 = (bf16[512,1536]{1,0:T(8,128)(2,1)}, bf16[512,2304]{1,0:T(8,128)(2,1)}, bf16[512,1536]{1,0:T(8,128)(2,1)}, bf16[512,1536]{1,0:T(8,128)(2,1)}, bf16[512,7...) custom-call(s32[8]{0:T(128)} %stack.56.sc, ...), custom_call_target="tpu_custom_call" | custom-call | flops 9663676416 | bytes 18874368 | tf_op jit(solution)/shard_map/ffn/pallas_call | solution.py:292
  78.5 13.4 %attn_bwd.2 = (bf16[512,768]{1,0:T(8,128)(2,1)}, bf16[512,768]{1,0:T(8,128)(2,1)}, bf16[512,768]{1,0:T(8,128)(2,1)}, bf16[512,768]{1,0:T(8,128)(2,1)}, bf16[512,...) custom-call(s32[8]{0:T(128)} %stack.56.sc, bf16[512,768]{1,0:T(8,128)(2,1)} %get-tuple-element.124.q_r, ...), custom_call_target="tpu_custom_call" | custom-call | flops 1912602624 | bytes 4128768 | tf_op jit(solution)/shard_map/attn_bwd/pallas_call | solution.py:425
  93.9 9.7 %wgrad.1 = (bf16[512,768]{1,0:T(8,128)(2,1)}, bf16[512,768]{1,0:T(8,128)(2,1)}, bf16[512,768]{1,0:T(8,128)(2,1)}, bf16[512,768]{1,0:T(8,128)(2,1)}, bf16[512,768]{1,0:T(8,128)(2,1)}, /*index=5*/bf16[512,768]{1,0:T(8,128)(2,1)}) custom-call(s32[8]{0:T(128)} %stack.56.sc, bf16[512,1536]{1,0:T(8,128)(2,1)} %get-tuple-element.144.act_h, ...), custom_call_target="tpu_custom_call" | custom-call | flops 4831838208 | bytes 10223616 | tf_op jit(solution)/shard_map/wgrad/pallas_call | solution.py:488
  105.7 1.6 collective-permute-start.17
  107.3 13.6 %attn_bwd.3 = (bf16[512,768]{1,0:T(8,128)(2,1)}, bf16[512,768]{1,0:T(8,128)(2,1)}, bf16[512,768]{1,0:T(8,128)(2,1)}, bf16[512,768]{1,0:T(8,128)(2,1)}, bf16[512,...) custom-call(s32[8]{0:T(128)} %stack.56.sc, ...), custom_call_target="tpu_custom_call", output_to_operand_aliasing={{0}: (13, {}), {1}: (14, {}), {2}: (15, {}), {3}: (16, {}),... | custom-call | flops 1912602624 | bytes 4128768 | tf_op jit(solution)/shard_map/attn_bwd/pallas_call | solution.py:425
  121.5 2.3 collective-permute-done.15.refs_3_
  126.1 4.2 %fold.6 = (bf16[256,768]{1,0:T(8,128)(2,1)}, bf16[256,768]{1,0:T(8,128)(2,1)}, bf16[256,768]{1,0:T(8,128)(2,1)}, bf16[256,768]{1,0:T(8,128)(2,1)}, bf16[256,768]{1,0:T(8,128)(2,1)}, /*index=5*/bf16[256,768]{1,0:T(8,128)(2,1)}) custom-call(s32[8]{0:T(128)} %stack.56.sc, bf16[512,768]{1,0:T(8,128)(2,1)} %get-tuple-element.148.refs_5_.refs_0_, ...), custom_call_target="tpu_custom_call" | custom-call | flops 2359296 | bytes 7077888 | tf_op jit(solution)/shard_map/fold/pallas_call | solution.py:602
  131.5 1.6 collective-permute-start.22
  135.1 8.9 %wgrad_mix.1 = (bf16[256,768]{1,0:T(8,128)(2,1)}, bf16[256,768]{1,0:T(8,128)(2,1)}, bf16[256,768]{1,0:T(8,128)(2,1)}, bf16[256,768]{1,0:T(8,128)(2,1)}, bf16[256...) custom-call(s32[8]{0:T(128)} %stack.56.sc, bf16[512,2304]{1,0:T(8,128)(2,1)} %get-tuple-element.127.hlc, ...), custom_call_target="tpu_custom_call" | custom-call | flops 2415919104 | bytes 7864320 | tf_op jit(solution)/shard_map/wgrad_mix/pallas_call | solution.py:545
  146.5 1.6 collective-permute-start.18
  149.4 2.8 fold.7
  152.2 1.7 collective-permute-start.27
  154.4 1.5 collective-permute-start.29
  155.9 3.4 %collective-permute-done.20.refs_5_ = bf16[256,768]{1,0:T(8,128)(2,1)S(1)} collective-permute-done((bf16[256,768]{1,0:T(8,128)(2,1)}, bf16[256,768]{1,0:T(8,128)(2,1)S(1)}, u32[]{:S(2)}, u32[]{:S(2)}) %collective-permute-start.20) | collective-permute-done | bytes 393248 | tf_op jit(solution)/shard_map/ppermute | solution.py:806
  160.4 2.9 fold.8
  166.3 2.3 fold.9
  168.6 2.6 collective-permute-start.33
  171.2 3.5 %collective-permute-start.9 = (bf16[256,768]{1,0:T(8,128)(2,1)}, bf16[256,768]{1,0:T(8,128)(2,1)S(1)}, u32[]{:S(2)}, u32[]{:S(2)}) collective-permute-start(bf16[256,768]{1,0:T(8,128)(2,1)} %get-tuple-element.149), channel_id=1, source_target_pairs={{0,24},{8,16},{16,8},{1,25},{9,17},{17,9},{2,26},{10,18},{18,10},{... | collective-permute-start | bytes 1179656 | tf_op jit(solution)/shard_map/ppermute | solution.py:902
  174.8 2.7 collective-permute-start.10
  177.6 1.9 collective-permute-start.11
  180.2 2.3 fold.10
  182.5 2.0 collective-permute-start.31
  185.2 1.8 total.2.refs_7_.refs_0_
  187.4 3.1 collective-permute-done.31.refs_4_
  190.5 4.8 %collective-permute-done.32.refs_5_ = bf16[64,768]{1,0:T(8,128)(2,1)S(1)} collective-permute-done((bf16[64,768]{1,0:T(8,128)(2,1)}, bf16[64,768]{1,0:T(8,128)(2,1)S(1)}, u32[]{:S(2)}, u32[]{:S(2)}) %collective-permute-start.32) | collective-permute-done | bytes 98336 | tf_op jit(solution)/shard_map/ppermute | solution.py:806
  195.3 1.6 collective-permute-start.30
  196.9 3.8 %collective-permute-done.30.refs_3_ = bf16[96,768]{1,0:T(8,128)(2,1)S(1)} collective-permute-done((bf16[96,768]{1,0:T(8,128)(2,1)}, bf16[96,768]{1,0:T(8,128)(2,1)S(1)}, u32[]{:S(2)}, u32[]{:S(2)}) %collective-permute-start.30) | collective-permute-done | bytes 147488 | tf_op jit(solution)/shard_map/ppermute | solution.py:806
  201.3 2.0 fold.11
  203.3 1.5 collective-permute-start.34
  205.9 1.9 join.6
  209.9 1.6 collective-permute-start.37
  212.9 1.7 total.3
  216.4 2.4 join.7
  218.9 1.6 collective-permute-start.44
  220.5 2.0 collective-permute-start.43
  222.5 1.9 collective-permute-start.36
  224.4 5.8 %collective-permute-done.36.refs_1_ = bf16[96,768]{1,0:T(8,128)(2,1)S(1)} collective-permute-done((bf16[96,768]{1,0:T(8,128)(2,1)}, bf16[96,768]{1,0:T(8,128)(2,1)S(1)}, u32[]{:S(2)}, u32[]{:S(2)}) %collective-permute-start.36) | collective-permute-done | bytes 147488 | tf_op jit(solution)/shard_map/ppermute | solution.py:806
  230.9 1.7 join.8
  233.7 3.2 join.9
  237.7 1.3 collective-permute-start.55
  240.9 12.0 %collective-permute-done.41.refs_4_ = bf16[64,768]{1,0:T(8,128)(2,1)S(1)} collective-permute-done((bf16[64,768]{1,0:T(8,128)(2,1)S(1)}, bf16[64,768]{1,0:T(8,128)(2,1)S(1)}, u32[]{:S(2)}, u32[]{:S(2)}) %collective-permute-start.41) | collective-permute-done | bytes 98336 | tf_op jit(solution)/shard_map/ppermute | solution.py:806
  252.9 1.7 collective-permute-start.40
  254.6 3.9 %collective-permute-done.40.refs_3_ = bf16[64,768]{1,0:T(8,128)(2,1)S(1)} collective-permute-done((bf16[64,768]{1,0:T(8,128)(2,1)S(1)}, bf16[64,768]{1,0:T(8,128)(2,1)S(1)}, u32[]{:S(2)}, u32[]{:S(2)}) %collective-permute-start.40) | collective-permute-done | bytes 98336 | tf_op jit(solution)/shard_map/ppermute | solution.py:806
  259.2 2.0 join.10
  261.6 2.0 collective-permute-start.47
  263.6 3.4 %collective-permute-done.46.refs_3_ = bf16[128,768]{1,0:T(8,128)(2,1)S(1)} collective-permute-done((bf16[128,768]{1,0:T(8,128)(2,1)}, bf16[128,768]{1,0:T(8,128)(2,1)S(1)}, u32[]{:S(2)}, u32[]{:S(2)}) %collective-permute-start.46) | collective-permute-done | bytes 196640 | tf_op jit(solution)/shard_map/ppermute | solution.py:806
  268.0 4.9 %collective-permute-done.48.refs_5_ = bf16[128,768]{1,0:T(8,128)(2,1)S(1)} collective-permute-done((bf16[128,768]{1,0:T(8,128)(2,1)}, bf16[128,768]{1,0:T(8,128)(2,1)S(1)}, u32[]{:S(2)}, u32[]{:S(2)}) %collective-permute-start.48) | collective-permute-done | bytes 196640 | tf_op jit(solution)/shard_map/ppermute | solution.py:806
  273.6 2.4 join.11
  277.4 3.3 pack.2
  282.2 4.4 %collective-permute-done.59.refs_7_ = bf16[512,768]{1,0:T(8,128)(2,1)S(1)} collective-permute-done((bf16[512,768]{1,0:T(8,128)(2,1)S(1)}, bf16[512,768]{1,0:T(8,128)(2,1)S(1)}, u32[]{:S(2)}, u32[]{:S(2)}) %collective-permute-start.59) | collective-permute-done | bytes 786464 | tf_op jit(solution)/shard_map/ppermute | solution.py:806
  286.6 1.7 collective-permute-start.51
  290.1 1.4 copy-done
  291.5 8.1 %final.4.refs_4_ = f32[768,3072]{1,0:T(8,128)} custom-call(s32[8]{0:T(128)} %stack.56.sc, bf16[512,768]{1,0:T(8,128)(2,1)} %get-tuple-element.213.refs_6_.refs_0_, bf16[512,768]{1,0:T(8,128)(2,1)} %get-tuple-element.220.refs_1_, bf16[512,768]{1,0:T(8,128)(2,1)} %get-tuple-element.221.refs_2_, bf16[512,768]{1,0:T(8,128)(2,1)} %copy-done.4, ...), custom_call_target="tpu_custom_call" | custom-call | flops 2359296 | bytes 14155776 | tf_op jit(solution)/shard_map/final/pallas_call | solution.py:760
  299.6 7.8 %final.3.refs_3_ = f32[3072,768]{1,0:T(8,128)} custom-call(s32[8]{0:T(128)} %stack.56.sc, bf16[512,768]{1,0:T(8,128)(2,1)} %get-tuple-element.213.refs_6_.refs_0_, bf16[512,768]{1,0:T(8,128)(2,1)} %get-tuple-element.220.refs_1_, bf16[512,768]{1,0:T(8,128)(2,1)} %get-tuple-element.221.refs_2_, bf16[512,768]{1,0:T(8,128)(2,1)} %copy-done.4, ...), custom_call_target="tpu_custom_call" | custom-call | flops 2359296 | bytes 14155776 | tf_op jit(solution)/shard_map/final/pallas_call | solution.py:760
  309.0 2.3 pack.3
  316.8 1.9 slice_reduce_fusion
  320.7 7.8 %final.5 = (f32[768,2304]{1,0:T(8,128)}, f32[768,768]{1,0:T(8,128)}) custom-call(s32[8]{0:T(128)} %stack.56.sc, bf16[256,768]{1,0:T(8,128)(2,1)} %get-tuple-element.217.refs_3_.refs_0_, bf16[256,768]{1,0:T(8,128)(2,1)} %get-tuple-element.218.refs_1_, bf16[256,768]{1,0:T(8,128)(2,1)} %get-tuple-element.219.refs_2_, bf16[256,768]{1,0:T(8,128)(2,1)} %copy-done.19, ...), custom_call_target="tpu_custom_call" | custom-call | flops 2359296 | bytes 14155776 | tf_op jit(solution)/shard_map/final/pallas_call | solution.py:760
  (257 shorter events, 64.2 us)
Async XLA Ops:
  2.6 22.9 %collective-permute-start.2 = (bf16[128,768]{1,0:T(8,128)(2,1)S(1)}, bf16[128,768]{1,0:T(8,128)(2,1)S(1)}, u32[]{:S(2)}, u32[]{:S(2)}) collective-permute-start(bf16[128,768]{1,0:T(8,128)(2,1)S(1)} %get-tuple-element.242), channel_id=1, source_target_pairs={{8,16},{16,8},{24,0},{9,17},{17,9},{25,1},{10,18},{18,10},{26,2},{... | collective-permute-start | bytes 589832 | tf_op jit(solution)/shard_map/ppermute | solution.py:827
  3.9 21.6 %collective-permute-start = (bf16[128,768]{1,0:T(8,128)(2,1)S(1)}, bf16[128,768]{1,0:T(8,128)(2,1)S(1)}, u32[]{:S(2)}, u32[]{:S(2)}) collective-permute-start(bf16[128,768]{1,0:T(8,128)(2,1)S(1)} %get-tuple-element.243), channel_id=1, source_target_pairs={{0,8},{8,0},{24,16},{1,9},{9,1},{25,17},{2,10},{10,2},{26,18},{3,1... | collective-permute-start | bytes 589832 | tf_op jit(solution)/shard_map/ppermute | solution.py:827
  10.9 14.6 %collective-permute-start.1 = (bf16[128,768]{1,0:T(8,128)(2,1)S(1)}, bf16[128,768]{1,0:T(8,128)(2,1)S(1)}, u32[]{:S(2)}, u32[]{:S(2)}) collective-permute-start(bf16[128,768]{1,0:T(8,128)(2,1)S(1)} %get-tuple-element.245), channel_id=1, source_target_pairs={{0,16},{16,0},{24,8},{1,17},{17,1},{25,9},{2,18},{18,2},{26,10},{3... | collective-permute-start | bytes 589832 | tf_op jit(solution)/shard_map/ppermute | solution.py:827
  27.7 25.4 %collective-permute-start.5 = (bf16[128,768]{1,0:T(8,128)(2,1)S(1)}, bf16[128,768]{1,0:T(8,128)(2,1)S(1)}, u32[]{:S(2)}, u32[]{:S(2)}) collective-permute-start(bf16[128,768]{1,0:T(8,128)(2,1)S(1)} %get-tuple-element.238), channel_id=1, source_target_pairs={{8,16},{16,8},{24,0},{9,17},{17,9},{25,1},{10,18},{18,10},{26,2},{... | collective-permute-start | bytes 589832 | tf_op jit(solution)/shard_map/ppermute | solution.py:827
  29.0 24.1 %collective-permute-start.4 = (bf16[128,768]{1,0:T(8,128)(2,1)S(1)}, bf16[128,768]{1,0:T(8,128)(2,1)S(1)}, u32[]{:S(2)}, u32[]{:S(2)}) collective-permute-start(bf16[128,768]{1,0:T(8,128)(2,1)S(1)} %get-tuple-element.239), channel_id=1, source_target_pairs={{0,16},{16,0},{24,8},{1,17},{17,1},{25,9},{2,18},{18,2},{26,10},{3... | collective-permute-start | bytes 589832 | tf_op jit(solution)/shard_map/ppermute | solution.py:827
  33.5 19.6 %collective-permute-start.3 = (bf16[128,768]{1,0:T(8,128)(2,1)S(1)}, bf16[128,768]{1,0:T(8,128)(2,1)S(1)}, u32[]{:S(2)}, u32[]{:S(2)}) collective-permute-start(bf16[128,768]{1,0:T(8,128)(2,1)S(1)} %get-tuple-element.240), channel_id=1, source_target_pairs={{0,8},{8,0},{24,16},{1,9},{9,1},{25,17},{2,10},{10,2},{26,18},{3,1... | collective-permute-start | bytes 589832 | tf_op jit(solution)/shard_map/ppermute | solution.py:827
  53.0 39.0 %collective-permute-start.7 = (bf16[512,2304]{1,0:T(8,128)(2,1)}, bf16[512,2304]{1,0:T(8,128)(2,1)S(1)}, u32[]{:S(2)}, u32[]{:S(2)}) collective-permute-start(bf16[512,2304]{1,0:T(8,128)(2,1)} %get-tuple-element.127.hlc), channel_id=1, source_target_pairs={{0,1},{1,0},{2,3},{3,2},{4,5},{5,4},{6,7},{7,6},{8,9},{9,8},{10,11... | collective-permute-start | bytes 7077896 | tf_op jit(solution)/shard_map/ppermute | solution.py:806
  77.9 14.1 %collective-permute-start.6 = (bf16[512,2304]{1,0:T(8,128)(2,1)}, bf16[512,2304]{1,0:T(8,128)(2,1)}, u32[]{:S(2)}, u32[]{:S(2)}) collective-permute-start(bf16[512,2304]{1,0:T(8,128)(2,1)} %get-tuple-element.145.send_h), channel_id=1, source_target_pairs={{0,1},{1,0},{2,3},{3,2},{4,5},{5,4},{6,7},{7,6},{8,9},{9,8},{10,11... | collective-permute-start | bytes 7077896 | tf_op jit(solution)/shard_map/ppermute | solution.py:806
  78.5 13.5 %collective-permute-start.8 = (bf16[512,1536]{1,0:T(8,128)(2,1)}, bf16[512,1536]{1,0:T(8,128)(2,1)S(1)}, u32[]{:S(2)}, u32[]{:S(2)}) collective-permute-start(bf16[512,1536]{1,0:T(8,128)(2,1)} %get-tuple-element.147), channel_id=1, source_target_pairs={{0,1},{1,0},{2,3},{3,2},{4,5},{5,4},{6,7},{7,6},{8,9},{9,8},{10,11... | collective-permute-start | bytes 4718600 | tf_op jit(solution)/shard_map/ppermute | solution.py:806
  103.6 20.2 %collective-permute-start.15 = (bf16[512,768]{1,0:T(8,128)(2,1)}, bf16[512,768]{1,0:T(8,128)(2,1)S(1)}, u32[]{:S(2)}, u32[]{:S(2)}) collective-permute-start(bf16[512,768]{1,0:T(8,128)(2,1)} %get-tuple-element.162), channel_id=1, source_target_pairs={{0,8},{1,9},{2,10},{3,11},{4,12},{5,13},{6,14},{7,15},{8,0},{9,1},... | collective-permute-start | bytes 2359304 | tf_op jit(solution)/shard_map/ppermute | solution.py:806
  104.9 19.8 %collective-permute-start.16 = (bf16[512,768]{1,0:T(8,128)(2,1)}, bf16[512,768]{1,0:T(8,128)(2,1)S(1)}, u32[]{:S(2)}, u32[]{:S(2)}) collective-permute-start(bf16[512,768]{1,0:T(8,128)(2,1)} %get-tuple-element.163), channel_id=1, source_target_pairs={{0,16},{1,17},{2,18},{3,19},{4,20},{5,21},{6,22},{7,23},{8,24},{9,... | collective-permute-start | bytes 2359304 | tf_op jit(solution)/shard_map/ppermute | solution.py:806
  105.7 19.6 %collective-permute-start.17 = (bf16[512,768]{1,0:T(8,128)(2,1)}, bf16[512,768]{1,0:T(8,128)(2,1)S(1)}, u32[]{:S(2)}, u32[]{:S(2)}) collective-permute-start(bf16[512,768]{1,0:T(8,128)(2,1)} %get-tuple-element.164), channel_id=1, source_target_pairs={{0,2},{1,3},{2,0},{3,1},{4,6},{5,7},{6,4},{7,5},{8,10},{9,11},{10,... | collective-permute-start | bytes 2359304 | tf_op jit(solution)/shard_map/ppermute | solution.py:806
  120.9 13.1 %collective-permute-start.12 = (bf16[512,768]{1,0:T(8,128)(2,1)}, bf16[512,768]{1,0:T(8,128)(2,1)S(1)}, u32[]{:S(2)}, u32[]{:S(2)}) collective-permute-start(bf16[512,768]{1,0:T(8,128)(2,1)} %get-tuple-element.156), channel_id=1, source_target_pairs={{0,1},{1,0},{2,3},{3,2},{4,5},{5,4},{6,7},{7,6},{8,9},{9,8},{10,11... | collective-permute-start | bytes 2359304 | tf_op jit(solution)/shard_map/ppermute | solution.py:806
  121.0 13.0 %collective-permute-start.13 = (bf16[512,768]{1,0:T(8,128)(2,1)}, bf16[512,768]{1,0:T(8,128)(2,1)S(1)}, u32[]{:S(2)}, u32[]{:S(2)}) collective-permute-start(bf16[512,768]{1,0:T(8,128)(2,1)} %get-tuple-element.157), channel_id=1, source_target_pairs={{0,1},{1,0},{2,3},{3,2},{4,5},{5,4},{6,7},{7,6},{8,9},{9,8},{10,11... | collective-permute-start | bytes 2359304 | tf_op jit(solution)/shard_map/ppermute | solution.py:806
  123.8 9.3 %collective-permute-start.14 = (bf16[32,768]{1,0:T(8,128)(2,1)}, bf16[32,768]{1,0:T(8,128)(2,1)S(1)}, u32[]{:S(2)}, u32[]{:S(2)}) collective-permute-start(bf16[32,768]{1,0:T(8,128)(2,1)} %get-tuple-element.158.refs_6_), channel_id=1, source_target_pairs={{0,1},{1,0},{2,3},{3,2},{4,5},{5,4},{6,7},{7,6},{8,9},{9,8},{10,11... | collective-permute-start | bytes 147464 | tf_op jit(solution)/shard_map/ppermute | solution.py:806
  130.4 17.7 %collective-permute-start.21 = (bf16[256,768]{1,0:T(8,128)(2,1)}, bf16[256,768]{1,0:T(8,128)(2,1)S(1)}, u32[]{:S(2)}, u32[]{:S(2)}) collective-permute-start(bf16[256,768]{1,0:T(8,128)(2,1)} %get-tuple-element.175), channel_id=1, source_target_pairs={{0,16},{1,17},{2,18},{3,19},{4,20},{5,21},{6,22},{7,23},{8,24},{9,... | collective-permute-start | bytes 1179656 | tf_op jit(solution)/shard_map/ppermute | solution.py:806
  131.5 17.0 %collective-permute-start.22 = (bf16[256,768]{1,0:T(8,128)(2,1)}, bf16[256,768]{1,0:T(8,128)(2,1)S(1)}, u32[]{:S(2)}, u32[]{:S(2)}) collective-permute-start(bf16[256,768]{1,0:T(8,128)(2,1)} %get-tuple-element.176), channel_id=1, source_target_pairs={{0,2},{1,3},{2,0},{3,1},{4,6},{5,7},{6,4},{7,5},{8,10},{9,11},{10,... | collective-permute-start | bytes 1179656 | tf_op jit(solution)/shard_map/ppermute | solution.py:806
  133.1 15.4 %collective-permute-start.23 = (bf16[256,768]{1,0:T(8,128)(2,1)}, bf16[256,768]{1,0:T(8,128)(2,1)S(1)}, u32[]{:S(2)}, u32[]{:S(2)}) collective-permute-start(bf16[256,768]{1,0:T(8,128)(2,1)} %get-tuple-element.177), channel_id=1, source_target_pairs={{0,8},{1,9},{2,10},{3,11},{4,12},{5,13},{6,14},{7,15},{8,0},{9,1},... | collective-permute-start | bytes 1179656 | tf_op jit(solution)/shard_map/ppermute | solution.py:806
  144.0 10.4 %collective-permute-start.19 = (bf16[256,768]{1,0:T(8,128)(2,1)}, bf16[256,768]{1,0:T(8,128)(2,1)S(1)}, u32[]{:S(2)}, u32[]{:S(2)}) collective-permute-start(bf16[256,768]{1,0:T(8,128)(2,1)} %get-tuple-element.171), channel_id=1, source_target_pairs={{0,16},{1,17},{2,18},{3,19},{4,20},{5,21},{6,22},{7,23},{8,24},{9,... | collective-permute-start | bytes 1179656 | tf_op jit(solution)/shard_map/ppermute | solution.py:806
  146.5 13.1 %collective-permute-start.18 = (bf16[288,768]{1,0:T(8,128)(2,1)S(1)}, bf16[288,768]{1,0:T(8,128)(2,1)S(1)}, u32[]{:S(2)}, u32[]{:S(2)}) collective-permute-start(bf16[288,768]{1,0:T(8,128)(2,1)S(1)} %pad_maximum_fusion.2), channel_id=1, source_target_pairs={{0,8},{1,9},{2,10},{3,11},{4,12},{5,13},{6,14},{7,15},{8,0},{9,1},... | collective-permute-start | bytes 1327112 | tf_op jit(solution)/shard_map/ppermute | solution.py:806
  148.1 11.2 %collective-permute-start.20 = (bf16[256,768]{1,0:T(8,128)(2,1)}, bf16[256,768]{1,0:T(8,128)(2,1)S(1)}, u32[]{:S(2)}, u32[]{:S(2)}) collective-permute-start(bf16[256,768]{1,0:T(8,128)(2,1)} %get-tuple-element.172), channel_id=1, source_target_pairs={{0,2},{1,3},{2,0},{3,1},{4,6},{5,7},{6,4},{7,5},{8,10},{9,11},{10,... | collective-permute-start | bytes 1179656 | tf_op jit(solution)/shard_map/ppermute | solution.py:806
  152.2 25.3 %copy-start.69 = (bf16[256,768]{1,0:T(8,128)(2,1)S(1)}, bf16[256,768]{1,0:T(8,128)(2,1)}, u32[]{:S(2)}) copy-start(bf16[256,768]{1,0:T(8,128)(2,1)} %get-tuple-element.151) | copy-start | bytes 1179652
  152.2 12.3 %collective-permute-start.27 = (bf16[128,768]{1,0:T(8,128)(2,1)}, bf16[128,768]{1,0:T(8,128)(2,1)S(1)}, u32[]{:S(2)}, u32[]{:S(2)}) collective-permute-start(bf16[128,768]{1,0:T(8,128)(2,1)} %get-tuple-element.188), channel_id=1, source_target_pairs={{0,2},{1,3},{2,0},{3,1},{4,6},{5,7},{6,4},{7,5},{8,10},{9,11},{10,... | collective-permute-start | bytes 589832 | tf_op jit(solution)/shard_map/ppermute | solution.py:806
  153.9 11.7 %collective-permute-start.28 = (bf16[128,768]{1,0:T(8,128)(2,1)}, bf16[128,768]{1,0:T(8,128)(2,1)S(1)}, u32[]{:S(2)}, u32[]{:S(2)}) collective-permute-start(bf16[128,768]{1,0:T(8,128)(2,1)} %get-tuple-element.189), channel_id=1, source_target_pairs={{0,8},{1,9},{2,10},{3,11},{4,12},{5,13},{6,14},{7,15},{8,0},{9,1},... | collective-permute-start | bytes 589832 | tf_op jit(solution)/shard_map/ppermute | solution.py:806
  154.4 11.2 %collective-permute-start.29 = (bf16[128,768]{1,0:T(8,128)(2,1)}, bf16[128,768]{1,0:T(8,128)(2,1)S(1)}, u32[]{:S(2)}, u32[]{:S(2)}) collective-permute-start(bf16[128,768]{1,0:T(8,128)(2,1)} %get-tuple-element.190), channel_id=1, source_target_pairs={{0,16},{1,17},{2,18},{3,19},{4,20},{5,21},{6,22},{7,23},{8,24},{9,... | collective-permute-start | bytes 589832 | tf_op jit(solution)/shard_map/ppermute | solution.py:806
  163.2 16.2 %collective-permute-start.24 = (bf16[160,768]{1,0:T(8,128)(2,1)}, bf16[160,768]{1,0:T(8,128)(2,1)S(1)}, u32[]{:S(2)}, u32[]{:S(2)}) collective-permute-start(bf16[160,768]{1,0:T(8,128)(2,1)} %get-tuple-element.182), channel_id=1, source_target_pairs={{0,16},{1,17},{2,18},{3,19},{4,20},{5,21},{6,22},{7,23},{8,24},{9,... | collective-permute-start | bytes 737288 | tf_op jit(solution)/shard_map/ppermute | solution.py:806
  164.1 10.7 %collective-permute-start.25 = (bf16[128,768]{1,0:T(8,128)(2,1)}, bf16[128,768]{1,0:T(8,128)(2,1)S(1)}, u32[]{:S(2)}, u32[]{:S(2)}) collective-permute-start(bf16[128,768]{1,0:T(8,128)(2,1)} %get-tuple-element.183), channel_id=1, source_target_pairs={{0,2},{1,3},{2,0},{3,1},{4,6},{5,7},{6,4},{7,5},{8,10},{9,11},{10,... | collective-permute-start | bytes 589832 | tf_op jit(solution)/shard_map/ppermute | solution.py:806
  164.5 13.0 %collective-permute-start.26 = (bf16[128,768]{1,0:T(8,128)(2,1)}, bf16[128,768]{1,0:T(8,128)(2,1)S(1)}, u32[]{:S(2)}, u32[]{:S(2)}) collective-permute-start(bf16[128,768]{1,0:T(8,128)(2,1)} %get-tuple-element.184), channel_id=1, source_target_pairs={{0,8},{1,9},{2,10},{3,11},{4,12},{5,13},{6,14},{7,15},{8,0},{9,1},... | collective-permute-start | bytes 589832 | tf_op jit(solution)/shard_map/ppermute | solution.py:806
  168.6 15.9 %collective-permute-start.33 = (bf16[192,768]{1,0:T(8,128)(2,1)}, bf16[192,768]{1,0:T(8,128)(2,1)S(1)}, u32[]{:S(2)}, u32[]{:S(2)}) collective-permute-start(bf16[192,768]{1,0:T(8,128)(2,1)} %get-tuple-element.199), channel_id=1, source_target_pairs={{0,4},{1,5},{2,6},{3,7},{4,0},{5,1},{6,2},{7,3},{8,12},{9,13},{10,... | collective-permute-start | bytes 884744 | tf_op jit(solution)/shard_map/ppermute | solution.py:806
  171.2 33.6 %collective-permute-start.9 = (bf16[256,768]{1,0:T(8,128)(2,1)}, bf16[256,768]{1,0:T(8,128)(2,1)S(1)}, u32[]{:S(2)}, u32[]{:S(2)}) collective-permute-start(bf16[256,768]{1,0:T(8,128)(2,1)} %get-tuple-element.149), channel_id=1, source_target_pairs={{0,24},{8,16},{16,8},{1,25},{9,17},{17,9},{2,26},{10,18},{18,10},{... | collective-permute-start | bytes 1179656 | tf_op jit(solution)/shard_map/ppermute | solution.py:902
  174.8 30.0 %collective-permute-start.10 = (bf16[256,768]{1,0:T(8,128)(2,1)S(1)}, bf16[256,768]{1,0:T(8,128)(2,1)S(1)}, u32[]{:S(2)}, u32[]{:S(2)}) collective-permute-start(bf16[256,768]{1,0:T(8,128)(2,1)S(1)} %copy-done.70), channel_id=1, source_target_pairs={{0,16},{8,24},{16,0},{1,17},{9,25},{17,1},{2,18},{10,26},{18,2},{3... | collective-permute-start | bytes 1179656 | tf_op jit(solution)/shard_map/ppermute | solution.py:902
  177.6 27.3 %collective-permute-start.11 = (bf16[256,768]{1,0:T(8,128)(2,1)S(1)}, bf16[256,768]{1,0:T(8,128)(2,1)S(1)}, u32[]{:S(2)}, u32[]{:S(2)}) collective-permute-start(bf16[256,768]{1,0:T(8,128)(2,1)S(1)} %copy-done.69), channel_id=1, source_target_pairs={{0,8},{8,0},{16,24},{1,9},{9,1},{17,25},{2,10},{10,2},{18,26},{3,1... | collective-permute-start | bytes 1179656 | tf_op jit(solution)/shard_map/ppermute | solution.py:902
  182.5 8.0 %collective-permute-start.31 = (bf16[64,768]{1,0:T(8,128)(2,1)}, bf16[64,768]{1,0:T(8,128)(2,1)S(1)}, u32[]{:S(2)}, u32[]{:S(2)}) collective-permute-start(bf16[64,768]{1,0:T(8,128)(2,1)} %get-tuple-element.196), channel_id=1, source_target_pairs={{0,8},{1,9},{2,10},{3,11},{4,12},{5,13},{6,14},{7,15},{8,0},{9,1},... | collective-permute-start | bytes 294920 | tf_op jit(solution)/shard_map/ppermute | solution.py:806
  187.1 17.8 %collective-permute-start.35 = (bf16[192,768]{1,0:T(8,128)(2,1)}, bf16[192,768]{1,0:T(8,128)(2,1)S(1)}, u32[]{:S(2)}, u32[]{:S(2)}) collective-permute-start(bf16[192,768]{1,0:T(8,128)(2,1)} %total.2.refs_7_.refs_0_), channel_id=1, source_target_pairs={{0,4},{1,5},{2,6},{3,7},{4,0},{5,1},{6,2},{7,3},{8,12},{9,13},{10,... | collective-permute-start | bytes 884744 | tf_op jit(solution)/shard_map/ppermute | solution.py:806
  190.5 4.8 %collective-permute-start.32 = (bf16[64,768]{1,0:T(8,128)(2,1)}, bf16[64,768]{1,0:T(8,128)(2,1)S(1)}, u32[]{:S(2)}, u32[]{:S(2)}) collective-permute-start(bf16[64,768]{1,0:T(8,128)(2,1)} %get-tuple-element.197), channel_id=1, source_target_pairs={{0,16},{1,17},{2,18},{3,19},{4,20},{5,21},{6,22},{7,23},{8,24},{9,... | collective-permute-start | bytes 294920 | tf_op jit(solution)/shard_map/ppermute | solution.py:806
  195.3 5.4 %collective-permute-start.30 = (bf16[96,768]{1,0:T(8,128)(2,1)}, bf16[96,768]{1,0:T(8,128)(2,1)S(1)}, u32[]{:S(2)}, u32[]{:S(2)}) collective-permute-start(bf16[96,768]{1,0:T(8,128)(2,1)} %get-tuple-element.195), channel_id=1, source_target_pairs={{0,2},{1,3},{2,0},{3,1},{4,6},{5,7},{6,4},{7,5},{8,10},{9,11},{10,... | collective-permute-start | bytes 442376 | tf_op jit(solution)/shard_map/ppermute | solution.py:806
  203.3 8.9 %collective-permute-start.34 = (bf16[128,768]{1,0:T(8,128)(2,1)}, bf16[128,768]{1,0:T(8,128)(2,1)S(1)}, u32[]{:S(2)}, u32[]{:S(2)}) collective-permute-start(bf16[128,768]{1,0:T(8,128)(2,1)} %get-tuple-element.201), channel_id=1, source_target_pairs={{0,4},{1,5},{2,6},{3,7},{4,0},{5,1},{6,2},{7,3},{8,12},{9,13},{10,... | collective-permute-start | bytes 589832 | tf_op jit(solution)/shard_map/ppermute | solution.py:806
  207.9 6.7 %collective-permute-start.38 = (bf16[128,768]{1,0:T(8,128)(2,1)}, bf16[128,768]{1,0:T(8,128)(2,1)S(1)}, u32[]{:S(2)}, u32[]{:S(2)}) collective-permute-start(bf16[128,768]{1,0:T(8,128)(2,1)} %get-tuple-element.205.refs_1_), channel_id=1, source_target_pairs={{0,8},{1,9},{2,10},{3,11},{4,12},{5,13},{6,14},{7,15},{8,0},{9,1},... | collective-permute-start | bytes 589832 | tf_op jit(solution)/shard_map/ppermute | solution.py:806
  208.9 5.9 %collective-permute-start.39 = (bf16[128,768]{1,0:T(8,128)(2,1)}, bf16[128,768]{1,0:T(8,128)(2,1)S(1)}, u32[]{:S(2)}, u32[]{:S(2)}) collective-permute-start(bf16[128,768]{1,0:T(8,128)(2,1)} %get-tuple-element.206.refs_2_), channel_id=1, source_target_pairs={{0,16},{1,17},{2,18},{3,19},{4,20},{5,21},{6,22},{7,23},{8,24},{9,... | collective-permute-start | bytes 589832 | tf_op jit(solution)/shard_map/ppermute | solution.py:806
  209.9 5.9 %collective-permute-start.37 = (bf16[128,768]{1,0:T(8,128)(2,1)}, bf16[128,768]{1,0:T(8,128)(2,1)S(1)}, u32[]{:S(2)}, u32[]{:S(2)}) collective-permute-start(bf16[128,768]{1,0:T(8,128)(2,1)} %get-tuple-element.203.refs_1_.refs_0_), channel_id=1, source_target_pairs={{0,2},{1,3},{2,0},{3,1},{4,6},{5,7},{6,4},{7,5},{8,10},{9,11},{10,... | collective-permute-start | bytes 589832 | tf_op jit(solution)/shard_map/ppermute | solution.py:806
  218.9 13.8 %collective-permute-start.44 = (bf16[256,768]{1,0:T(8,128)(2,1)}, bf16[256,768]{1,0:T(8,128)(2,1)S(1)}, u32[]{:S(2)}, u32[]{:S(2)}) collective-permute-start(bf16[256,768]{1,0:T(8,128)(2,1)} %get-tuple-element.211.refs_1_), channel_id=1, source_target_pairs={{0,2},{1,3},{2,0},{3,1},{4,6},{5,7},{6,4},{7,5},{8,10},{9,11},{10,... | collective-permute-start | bytes 1179656 | tf_op jit(solution)/shard_map/ppermute | solution.py:806
  220.4 12.2 %collective-permute-start.45 = (bf16[256,768]{1,0:T(8,128)(2,1)}, bf16[256,768]{1,0:T(8,128)(2,1)S(1)}, u32[]{:S(2)}, u32[]{:S(2)}) collective-permute-start(bf16[256,768]{1,0:T(8,128)(2,1)} %get-tuple-element.212.refs_2_), channel_id=1, source_target_pairs={{0,8},{1,9},{2,10},{3,11},{4,12},{5,13},{6,14},{7,15},{8,0},{9,1},... | collective-permute-start | bytes 1179656 | tf_op jit(solution)/shard_map/ppermute | solution.py:806
  220.5 12.1 %collective-permute-start.43 = (bf16[256,768]{1,0:T(8,128)(2,1)}, bf16[256,768]{1,0:T(8,128)(2,1)S(1)}, u32[]{:S(2)}, u32[]{:S(2)}) collective-permute-start(bf16[256,768]{1,0:T(8,128)(2,1)} %get-tuple-element.207.refs_2_.refs_0_), channel_id=1, source_target_pairs={{0,16},{1,17},{2,18},{3,19},{4,20},{5,21},{6,22},{7,23},{8,24},{9,... | collective-permute-start | bytes 1179656 | tf_op jit(solution)/shard_map/ppermute | solution.py:806
  222.5 7.7 %collective-permute-start.36 = (bf16[96,768]{1,0:T(8,128)(2,1)}, bf16[96,768]{1,0:T(8,128)(2,1)S(1)}, u32[]{:S(2)}, u32[]{:S(2)}) collective-permute-start(bf16[96,768]{1,0:T(8,128)(2,1)} %get-tuple-element.204.refs_6_.refs_0_), channel_id=1, source_target_pairs={{0,4},{1,5},{2,6},{3,7},{4,0},{5,1},{6,2},{7,3},{8,12},{9,13},{10,... | collective-permute-start | bytes 442376 | tf_op jit(solution)/shard_map/ppermute | solution.py:806
  236.8 39.2 %collective-permute-start.56 = (bf16[512,768]{1,0:T(8,128)(2,1)}, bf16[512,768]{1,0:T(8,128)(2,1)S(1)}, u32[]{:S(2)}, u32[]{:S(2)}) collective-permute-start(bf16[512,768]{1,0:T(8,128)(2,1)} %get-tuple-element.220.refs_1_), channel_id=1, source_target_pairs={{0,16},{1,17},{2,18},{3,19},{4,20},{5,21},{6,22},{7,23},{8,24},{9,... | collective-permute-start | bytes 2359304 | tf_op jit(solution)/shard_map/ppermute | solution.py:806
  236.8 39.2 %collective-permute-start.57 = (bf16[512,768]{1,0:T(8,128)(2,1)}, bf16[512,768]{1,0:T(8,128)(2,1)S(1)}, u32[]{:S(2)}, u32[]{:S(2)}) collective-permute-start(bf16[512,768]{1,0:T(8,128)(2,1)} %get-tuple-element.221.refs_2_), channel_id=1, source_target_pairs={{0,2},{1,3},{2,0},{3,1},{4,6},{5,7},{6,4},{7,5},{8,10},{9,11},{10,... | collective-permute-start | bytes 2359304 | tf_op jit(solution)/shard_map/ppermute | solution.py:806
  237.7 38.4 %collective-permute-start.55 = (bf16[512,768]{1,0:T(8,128)(2,1)}, bf16[512,768]{1,0:T(8,128)(2,1)S(1)}, u32[]{:S(2)}, u32[]{:S(2)}) collective-permute-start(bf16[512,768]{1,0:T(8,128)(2,1)} %get-tuple-element.213.refs_6_.refs_0_), channel_id=1, source_target_pairs={{0,8},{1,9},{2,10},{3,11},{4,12},{5,13},{6,14},{7,15},{8,0},{9,1},... | collective-permute-start | bytes 2359304 | tf_op jit(solution)/shard_map/ppermute | solution.py:806
  239.0 13.9 %collective-permute-start.41 = (bf16[64,768]{1,0:T(8,128)(2,1)S(1)}, bf16[64,768]{1,0:T(8,128)(2,1)S(1)}, u32[]{:S(2)}, u32[]{:S(2)}) collective-permute-start(bf16[64,768]{1,0:T(8,128)(2,1)S(1)} %copy-done.60), channel_id=1, source_target_pairs={{0,8},{1,9},{2,10},{3,11},{4,12},{5,13},{6,14},{7,15},{8,0},{9,1},... | collective-permute-start | bytes 294920 | tf_op jit(solution)/shard_map/ppermute | solution.py:806
  239.7 14.9 %collective-permute-start.42 = (bf16[64,768]{1,0:T(8,128)(2,1)S(1)}, bf16[64,768]{1,0:T(8,128)(2,1)S(1)}, u32[]{:S(2)}, u32[]{:S(2)}) collective-permute-start(bf16[64,768]{1,0:T(8,128)(2,1)S(1)} %copy-done.61), channel_id=1, source_target_pairs={{0,16},{1,17},{2,18},{3,19},{4,20},{5,21},{6,22},{7,23},{8,24},{9,... | collective-permute-start | bytes 294920 | tf_op jit(solution)/shard_map/ppermute | solution.py:806
  252.9 5.7 %collective-permute-start.40 = (bf16[64,768]{1,0:T(8,128)(2,1)S(1)}, bf16[64,768]{1,0:T(8,128)(2,1)S(1)}, u32[]{:S(2)}, u32[]{:S(2)}) collective-permute-start(bf16[64,768]{1,0:T(8,128)(2,1)S(1)} %copy-done.39), channel_id=1, source_target_pairs={{0,2},{1,3},{2,0},{3,1},{4,6},{5,7},{6,4},{7,5},{8,10},{9,11},{10,... | collective-permute-start | bytes 294920 | tf_op jit(solution)/shard_map/ppermute | solution.py:806
  261.1 5.9 %collective-permute-start.46 = (bf16[128,768]{1,0:T(8,128)(2,1)}, bf16[128,768]{1,0:T(8,128)(2,1)S(1)}, u32[]{:S(2)}, u32[]{:S(2)}) collective-permute-start(bf16[128,768]{1,0:T(8,128)(2,1)} %get-tuple-element.214.refs_0_.refs_6_), channel_id=1, source_target_pairs={{0,16},{1,17},{2,18},{3,19},{4,20},{5,21},{6,22},{7,23},{8,24},{9,... | collective-permute-start | bytes 589832 | tf_op jit(solution)/shard_map/ppermute | solution.py:806
  261.6 6.4 %collective-permute-start.47 = (bf16[128,768]{1,0:T(8,128)(2,1)}, bf16[128,768]{1,0:T(8,128)(2,1)S(1)}, u32[]{:S(2)}, u32[]{:S(2)}) collective-permute-start(bf16[128,768]{1,0:T(8,128)(2,1)} %get-tuple-element.215.refs_1_), channel_id=1, source_target_pairs={{0,2},{1,3},{2,0},{3,1},{4,6},{5,7},{6,4},{7,5},{8,10},{9,11},{10,... | collective-permute-start | bytes 589832 | tf_op jit(solution)/shard_map/ppermute | solution.py:806
  267.0 5.9 %collective-permute-start.48 = (bf16[128,768]{1,0:T(8,128)(2,1)}, bf16[128,768]{1,0:T(8,128)(2,1)S(1)}, u32[]{:S(2)}, u32[]{:S(2)}) collective-permute-start(bf16[128,768]{1,0:T(8,128)(2,1)} %get-tuple-element.216.refs_2_), channel_id=1, source_target_pairs={{0,8},{1,9},{2,10},{3,11},{4,12},{5,13},{6,14},{7,15},{8,0},{9,1},... | collective-permute-start | bytes 589832 | tf_op jit(solution)/shard_map/ppermute | solution.py:806
  280.7 9.4 %collective-permute-start.61 = (bf16[1536,768]{1,0:T(8,128)(2,1)}, bf16[1536,768]{1,0:T(8,128)(2,1)S(1)}, u32[]{:S(2)}, u32[]{:S(2)}) collective-permute-start(bf16[1536,768]{1,0:T(8,128)(2,1)} %pack.2), channel_id=1, source_target_pairs={{0,1},{1,0},{2,3},{3,2},{4,5},{5,4},{6,7},{7,6},{8,9},{9,8},{10,11... | collective-permute-start | bytes 7077896 | tf_op jit(solution)/shard_map/ppermute | solution.py:806
  280.7 5.9 %collective-permute-start.59 = (bf16[512,768]{1,0:T(8,128)(2,1)S(1)}, bf16[512,768]{1,0:T(8,128)(2,1)S(1)}, u32[]{:S(2)}, u32[]{:S(2)}) collective-permute-start(bf16[512,768]{1,0:T(8,128)(2,1)S(1)} %copy-done.6), channel_id=1, source_target_pairs={{0,1},{1,0},{2,3},{3,2},{4,5},{5,4},{6,7},{7,6},{8,9},{9,8},{10,11... | collective-permute-start | bytes 2359304 | tf_op jit(solution)/shard_map/ppermute | solution.py:806
  281.2 7.1 %collective-permute-start.60 = (bf16[512,768]{1,0:T(8,128)(2,1)}, bf16[512,768]{1,0:T(8,128)(2,1)S(1)}, u32[]{:S(2)}, u32[]{:S(2)}) collective-permute-start(bf16[512,768]{1,0:T(8,128)(2,1)} %get-tuple-element.221.refs_2_), channel_id=1, source_target_pairs={{0,1},{1,0},{2,3},{3,2},{4,5},{5,4},{6,7},{7,6},{8,9},{9,8},{10,11... | collective-permute-start | bytes 2359304 | tf_op jit(solution)/shard_map/ppermute | solution.py:806
  281.2 7.8 %collective-permute-start.58 = (bf16[512,768]{1,0:T(8,128)(2,1)S(1)}, bf16[512,768]{1,0:T(8,128)(2,1)S(1)}, u32[]{:S(2)}, u32[]{:S(2)}) collective-permute-start(bf16[512,768]{1,0:T(8,128)(2,1)S(1)} %copy-done.5), channel_id=1, source_target_pairs={{0,1},{1,0},{2,3},{3,2},{4,5},{5,4},{6,7},{7,6},{8,9},{9,8},{10,11... | collective-permute-start | bytes 2359304 | tf_op jit(solution)/shard_map/ppermute | solution.py:806
  281.7 25.8 %collective-permute-start.50 = (bf16[256,768]{1,0:T(8,128)(2,1)}, bf16[256,768]{1,0:T(8,128)(2,1)}, u32[]{:S(2)}, u32[]{:S(2)}) collective-permute-start(bf16[256,768]{1,0:T(8,128)(2,1)} %get-tuple-element.218.refs_1_), channel_id=1, source_target_pairs={{0,16},{1,17},{2,18},{3,19},{4,20},{5,21},{6,22},{7,23},{8,24},{9,... | collective-permute-start | bytes 1179656 | tf_op jit(solution)/shard_map/ppermute | solution.py:806
  286.6 21.0 %collective-permute-start.51 = (bf16[256,768]{1,0:T(8,128)(2,1)}, bf16[256,768]{1,0:T(8,128)(2,1)S(1)}, u32[]{:S(2)}, u32[]{:S(2)}) collective-permute-start(bf16[256,768]{1,0:T(8,128)(2,1)} %get-tuple-element.219.refs_2_), channel_id=1, source_target_pairs={{0,2},{1,3},{2,0},{3,1},{4,6},{5,7},{6,4},{7,5},{8,10},{9,11},{10,... | collective-permute-start | bytes 1179656 | tf_op jit(solution)/shard_map/ppermute | solution.py:806
  288.3 19.2 %collective-permute-start.49 = (bf16[256,768]{1,0:T(8,128)(2,1)}, bf16[256,768]{1,0:T(8,128)(2,1)S(1)}, u32[]{:S(2)}, u32[]{:S(2)}) collective-permute-start(bf16[256,768]{1,0:T(8,128)(2,1)} %get-tuple-element.217.refs_3_.refs_0_), channel_id=1, source_target_pairs={{0,8},{1,9},{2,10},{3,11},{4,12},{5,13},{6,14},{7,15},{8,0},{9,1},... | collective-permute-start | bytes 1179656 | tf_op jit(solution)/shard_map/ppermute | solution.py:806
  311.4 7.4 %collective-permute-start.62 = (bf16[768,768]{1,0:T(8,128)(2,1)}, bf16[768,768]{1,0:T(8,128)(2,1)S(1)}, u32[]{:S(2)}, u32[]{:S(2)}) collective-permute-start(bf16[768,768]{1,0:T(8,128)(2,1)} %pack.3), channel_id=1, source_target_pairs={{0,1},{1,0},{2,3},{3,2},{4,5},{5,4},{6,7},{7,6},{8,9},{9,8},{10,11... | collective-permute-start | bytes 3538952 | tf_op jit(solution)/shard_map/ppermute | solution.py:806
  312.7 6.0 %collective-permute-start.53 = (bf16[256,768]{1,0:T(8,128)(2,1)S(1)}, bf16[256,768]{1,0:T(8,128)(2,1)S(1)}, u32[]{:S(2)}, u32[]{:S(2)}) collective-permute-start(bf16[256,768]{1,0:T(8,128)(2,1)S(1)} %copy-done.26), channel_id=1, source_target_pairs={{0,1},{1,0},{2,3},{3,2},{4,5},{5,4},{6,7},{7,6},{8,9},{9,8},{10,11... | collective-permute-start | bytes 1179656 | tf_op jit(solution)/shard_map/ppermute | solution.py:806
  313.2 5.6 %collective-permute-start.54 = (bf16[256,768]{1,0:T(8,128)(2,1)S(1)}, bf16[256,768]{1,0:T(8,128)(2,1)S(1)}, u32[]{:S(2)}, u32[]{:S(2)}) collective-permute-start(bf16[256,768]{1,0:T(8,128)(2,1)S(1)} %copy-done.27), channel_id=1, source_target_pairs={{0,1},{1,0},{2,3},{3,2},{4,5},{5,4},{6,7},{7,6},{8,9},{9,8},{10,11... | collective-permute-start | bytes 1179656 | tf_op jit(solution)/shard_map/ppermute | solution.py:806
  313.3 5.4 %collective-permute-start.52 = (bf16[256,768]{1,0:T(8,128)(2,1)S(1)}, bf16[256,768]{1,0:T(8,128)(2,1)S(1)}, u32[]{:S(2)}, u32[]{:S(2)}) collective-permute-start(bf16[256,768]{1,0:T(8,128)(2,1)S(1)} %copy-done.11), channel_id=1, source_target_pairs={{0,1},{1,0},{2,3},{3,2},{4,5},{5,4},{6,7},{7,6},{8,9},{9,8},{10,11... | collective-permute-start | bytes 1179656 | tf_op jit(solution)/shard_map/ppermute | solution.py:806
  (73 other events, 206.2 us)
